TPU v7x, 128 devices: a whole 4x4x4 slice. The times are simulated.
128 devices in a mesh: blk: 32 (over z, y, core), col: 4 (over x).
Axes of the slice: x: 4, y: 4, z: 4, core: 2. Of those that a mesh axis runs over, the one named last changes fastest.
Arguments:
- rank_in: float32 [4096, 512], P(('blk', 'col')), may hold values from 0.5 to 1.5
- delta_in: float32 [4096, 512], P(('blk', 'col'))
- out_degree: int32 [4096, 512], P(('blk', 'col')), may hold values from 98 to 194
- tile_weight: bfloat16 [4096, 512, 512], P(('blk', 'col'))
- tile_source: int32 [4096], P(('blk', 'col')), may hold values from 0 to 1023, as said below
- tile_row: int32 [4096], P(('blk', 'col')), may hold values from 0 to 127
- tile_valid: int32 [4096], P(('blk', 'col')), may hold values 0 or 1
Outputs:
- rank_out: float32 [4096, 512], P(('blk', 'col'))
- delta_out: float32 [4096, 512], P(('blk', 'col'))
- masses: float32 [6], replicated
Inputs may be any that keep to these rules, and one draw needn't show every extreme that they name: `tile_source`: slot j of the 32 slots of each device (tiles i with i % 32 = j) names a source block from 32 * j to 32 * j + 31.
All inputs are finite; a program needn't handle non-finite values. No bound on the sum of `tile_valid` on one device may be relied on, other than what follows from the above.
Results may differ from a plain program's by a relative error of at most 0.00039.
Values may be sent and summed in bfloat16 or wider, within the bound.
No kernel may reach another device: no remote copies, remote signals or barrier semaphores. Data moves between devices by JAX's collectives and lax.ppermute only.
A program may use at most 64 MiB of HBM per device.

v0:
```python
import functools

import jax
import jax.numpy as jnp
from jax import lax
from jax.sharding import Mesh
from jax.sharding import PartitionSpec as P

ITERS = 6
BLK = ("blk_0", "blk_1", "blk_2")
BLK_COL = ("blk_0", "blk_1", "blk_2", "col")


damping = 0.85


def in_blocks(shard, dim, peers):
    lengths = shard.shape
    blocks = shard.reshape(*lengths[:dim], peers, lengths[dim] // peers, *lengths[dim + 1 :])
    return jnp.moveaxis(blocks, dim, 0)


def summed_on_arrival(shard, axis, dim):
    peers = lax.axis_size(axis)
    blocks = lax.all_to_all(in_blocks(shard, dim, peers), axis, 0, 0, tiled=True)
    return jnp.sum(blocks, axis=0)


def by_axis(shard, axes):
    return functools.reduce(lax.psum, axes, shard)


def on_device(rank_in, delta_in, out_degree, tile_weight, tile_source, tile_row, tile_valid):
    owned = delta_in.shape[0]
    width = delta_in.shape[1]
    n_group = lax.axis_size(BLK)
    n_column = lax.axis_size("col")
    group_rows = owned * n_column
    cells = owned * n_group * n_column * width
    scale = damping / out_degree.astype(jnp.float32)
    valid = tile_valid.astype(jnp.float32)[:, None]
    onehot = (tile_row[None, :] == jnp.arange(group_rows, dtype=jnp.int32)[:, None]).astype(
        jnp.float32
    )
    wanted = (tile_source - jnp.arange(n_group, dtype=jnp.int32) * owned).reshape(n_group, 1)
    asked = lax.all_to_all(wanted, BLK, split_axis=0, concat_axis=0, tiled=True).reshape(n_group)
    delta = delta_in
    total = rank_in
    local_masses = []
    for step in range(ITERS):
        local_mass = jnp.sum(jnp.abs(delta)) / cells
        local_masses.append(local_mass)
        total = total + delta
        contrib = (delta * scale).astype(jnp.bfloat16)
        picked = lax.all_to_all(contrib[asked], BLK, split_axis=0, concat_axis=0, tiled=True)
        product = (
            jnp.einsum("tuv,tv->tu", tile_weight, picked, preferred_element_type=jnp.float32)
            * valid
        )
        partial_value = jnp.dot(onehot, product, precision=lax.Precision.HIGHEST)
        delta = summed_on_arrival(partial_value, "col", 0)
    stacked = jnp.stack(local_masses)
    stacked = by_axis(stacked, BLK_COL)
    return (total, delta, stacked)


def solution(mesh):
    finer = Mesh(
        mesh.devices.reshape(4, 4, 2, mesh.shape["col"]), ("blk_0", "blk_1", "blk_2", "col")
    )
    placed = (
        P(BLK_COL, None),
        P(BLK_COL, None),
        P(BLK_COL, None),
        P(BLK_COL, None, None),
        P(BLK_COL),
        P(BLK_COL),
        P(BLK_COL),
    )
    return jax.shard_map(
        on_device,
        mesh=finer,
        in_specs=placed,
        out_specs=(P(BLK_COL, None), P(BLK_COL, None), P()),
        check_vma=False,
    )
```

profile of v0, /device:TPU:0, one launch (start us, length us, event | category | flops | bytes accessed | tf_op | source)
XLA Modules:
  0.0 247.0 jit_solution(9369890108432884228)
XLA Ops:
  0.6 0.0 copy-start
  0.6 0.0 copy-start.3
  0.7 0.7 subtract_bitcast_fusion
  1.3 0.7 copy.17
  2.0 8.4 %all-to-all-start = ((s32[32,1,1]{2,1,0:T(1,128)}), s32[32,1,1]{2,1,0:T(1,128)S(1)}, u32[]{:S(2)}, u32[]{:S(2)}) async-start(s32[32,1,1]{2,1,0:T(1,128)} %copy.17), calls=%async_computation | async-start | bytes 32768 | tf_op jit(solution)/shard_map/all_to_all | solution.py:46
  10.5 0.9 multiply_convert_fusion.5
  11.4 6.4 %all-to-all-done = s32[32,1,1]{2,1,0:T(1,128)S(1)} async-done(((s32[32,1,1]{2,1,0:T(1,128)}), s32[32,1,1]{2,1,0:T(1,128)S(1)}, u32[]{:S(2)}, u32[]{:S(2)}) %all-to-all-start) | async-done | bytes 160 | tf_op jit(solution)/shard_map/all_to_all | solution.py:46
  17.7 0.7 reduce
  18.4 0.6 gather_fusion
  19.1 0.5 broadcast.45
  19.6 0.7 reduce.1
  20.2 0.6 reshape.143
  20.9 3.9 %all-to-all-start.1 = ((bf16[32,2,256]{2,1,0:T(2,128)(2,1)}), bf16[32,2,256]{2,1,0:T(2,128)(2,1)S(1)}, u32[]{:S(2)}, u32[]{:S(2)}) async-start(bf16[32,2,256]{2,1,0:T(2,128)(2,1)} %reshape.143), calls=%async_computation.1 | async-start | bytes 65536 | tf_op jit(solution)/shard_map/all_to_all | solution.py:55
  24.7 0.7 convert_element_type.27
  25.4 6.7 %all-to-all-done.1 = bf16[32,2,256]{2,1,0:T(2,128)(2,1)S(1)} async-done(((bf16[32,2,256]{2,1,0:T(2,128)(2,1)}), bf16[32,2,256]{2,1,0:T(2,128)(2,1)S(1)}, u32[]{:S(2)}, u32[]{:S(2)}) %all-to-all-start.1) | async-done | bytes 32800 | tf_op jit(solution)/shard_map/all_to_all | solution.py:55
  32.2 10.2 %fusion.16 = f32[32,1,512]{2,1,0:T(1,128)S(1)} fusion(bf16[32,512,512]{2,1,0:T(8,128)(2,1)} %param.10, bf16[32,1,512]{2,1,0:T(2,128)(2,1)S(1)} %reshape.144), kind=kOutput, calls=%fused_computation.28 | convolution fusion | flops 16777216 | bytes 16875520 | tf_op jit(solution)/shard_map/tuv,tv->tu/dot_general | solution.py:57
  42.3 0.0 copy-done.3
  42.3 0.3 fusion.15
  42.7 11.0 %all_to_all.114 = f32[4,32,512]{2,1,0:T(8,128)S(1)} all-to-all(f32[4,32,512]{2,1,0:T(8,128)S(1)} %bitcast.66), channel_id=1, replica_groups=mesh['blk_0'=4,'blk_1'=4,'blk_2'=2,'col'=4] {'col'}, dimensions={0} | all-to-all | bytes 524288 | tf_op jit(solution)/shard_map/all_to_all | solution.py:25
  53.8 0.0 copy-done
  53.8 0.6 gather_fusion.1
  54.4 0.7 reduce.2
  55.1 10.7 %all_to_all.115 = bf16[32,2,256]{2,1,0:T(2,128)(2,1)S(1)} all-to-all(bf16[32,2,256]{2,1,0:T(2,128)(2,1)S(1)} %reshape.145), channel_id=1, replica_groups=mesh['blk_0'=4,'blk_1'=4,'blk_2'=2,'col'=4] {'blk_0','blk_1','blk_2'}, dimensions={0} | all-to-all | bytes 65536 | tf_op jit(solution)/shard_map/all_to_all | solution.py:55
  65.8 10.2 %fusion.13 = f32[32,1,512]{2,1,0:T(1,128)S(1)} fusion(bf16[32,512,512]{2,1,0:T(8,128)(2,1)} %param.10, bf16[32,1,512]{2,1,0:T(2,128)(2,1)S(1)} %reshape.146), kind=kOutput, calls=%fused_computation.24 | convolution fusion | flops 16777216 | bytes 16875520 | tf_op jit(solution)/shard_map/tuv,tv->tu/dot_general | solution.py:57
  76.0 0.3 fusion.12
  76.4 9.6 %all_to_all.116 = f32[4,32,512]{2,1,0:T(8,128)S(1)} all-to-all(f32[4,32,512]{2,1,0:T(8,128)S(1)} %bitcast.67), channel_id=1, replica_groups=mesh['blk_0'=4,'blk_1'=4,'blk_2'=2,'col'=4] {'col'}, dimensions={0} | all-to-all | bytes 524288 | tf_op jit(solution)/shard_map/all_to_all | solution.py:25
  86.0 0.6 gather_fusion.2
  86.7 0.7 reduce.3
  87.3 10.7 %all_to_all.117 = bf16[32,2,256]{2,1,0:T(2,128)(2,1)S(1)} all-to-all(bf16[32,2,256]{2,1,0:T(2,128)(2,1)S(1)} %reshape.147), channel_id=1, replica_groups=mesh['blk_0'=4,'blk_1'=4,'blk_2'=2,'col'=4] {'blk_0','blk_1','blk_2'}, dimensions={0} | all-to-all | bytes 65536 | tf_op jit(solution)/shard_map/all_to_all | solution.py:55
  98.1 10.2 %fusion.10 = f32[32,1,512]{2,1,0:T(1,128)S(1)} fusion(bf16[32,512,512]{2,1,0:T(8,128)(2,1)} %param.10, bf16[32,1,512]{2,1,0:T(2,128)(2,1)S(1)} %reshape.148), kind=kOutput, calls=%fused_computation.20 | convolution fusion | flops 16777216 | bytes 16875520 | tf_op jit(solution)/shard_map/tuv,tv->tu/dot_general | solution.py:57
  108.2 0.3 fusion.9
  108.6 9.6 %all_to_all.118 = f32[4,32,512]{2,1,0:T(8,128)S(1)} all-to-all(f32[4,32,512]{2,1,0:T(8,128)S(1)} %bitcast.68), channel_id=1, replica_groups=mesh['blk_0'=4,'blk_1'=4,'blk_2'=2,'col'=4] {'col'}, dimensions={0} | all-to-all | bytes 524288 | tf_op jit(solution)/shard_map/all_to_all | solution.py:25
  118.3 0.6 gather_fusion.3
  118.9 0.7 reduce.4
  119.6 10.7 %all_to_all.119 = bf16[32,2,256]{2,1,0:T(2,128)(2,1)S(1)} all-to-all(bf16[32,2,256]{2,1,0:T(2,128)(2,1)S(1)} %reshape.149), channel_id=1, replica_groups=mesh['blk_0'=4,'blk_1'=4,'blk_2'=2,'col'=4] {'blk_0','blk_1','blk_2'}, dimensions={0} | all-to-all | bytes 65536 | tf_op jit(solution)/shard_map/all_to_all | solution.py:55
  130.3 0.0 copy-start.1
  130.3 0.0 copy-start.2
  130.3 10.2 %fusion.7 = f32[32,1,512]{2,1,0:T(1,128)S(1)} fusion(bf16[32,512,512]{2,1,0:T(8,128)(2,1)} %param.10, bf16[32,1,512]{2,1,0:T(2,128)(2,1)S(1)} %reshape.150), kind=kOutput, calls=%fused_computation.16 | convolution fusion | flops 16777216 | bytes 16875520 | tf_op jit(solution)/shard_map/tuv,tv->tu/dot_general | solution.py:57
  140.5 0.3 fusion.6
  140.9 9.6 %all_to_all.120 = f32[4,32,512]{2,1,0:T(8,128)S(1)} all-to-all(f32[4,32,512]{2,1,0:T(8,128)S(1)} %bitcast.69), channel_id=1, replica_groups=mesh['blk_0'=4,'blk_1'=4,'blk_2'=2,'col'=4] {'col'}, dimensions={0} | all-to-all | bytes 524288 | tf_op jit(solution)/shard_map/all_to_all | solution.py:25
  150.5 0.6 gather_fusion.4
  151.2 0.7 reduce.5
  151.9 10.7 %all_to_all.121 = bf16[32,2,256]{2,1,0:T(2,128)(2,1)S(1)} all-to-all(bf16[32,2,256]{2,1,0:T(2,128)(2,1)S(1)} %reshape.151), channel_id=1, replica_groups=mesh['blk_0'=4,'blk_1'=4,'blk_2'=2,'col'=4] {'blk_0','blk_1','blk_2'}, dimensions={0} | all-to-all | bytes 65536 | tf_op jit(solution)/shard_map/all_to_all | solution.py:55
  162.6 10.2 %fusion.4 = f32[32,1,512]{2,1,0:T(1,128)S(1)} fusion(bf16[32,512,512]{2,1,0:T(8,128)(2,1)} %param.10, bf16[32,1,512]{2,1,0:T(2,128)(2,1)S(1)} %reshape.152), kind=kOutput, calls=%fused_computation.12 | convolution fusion | flops 16777216 | bytes 16875520 | tf_op jit(solution)/shard_map/tuv,tv->tu/dot_general | solution.py:57
  172.8 0.3 fusion.3
  173.1 9.6 %all_to_all.122 = f32[4,32,512]{2,1,0:T(8,128)S(1)} all-to-all(f32[4,32,512]{2,1,0:T(8,128)S(1)} %bitcast.70), channel_id=1, replica_groups=mesh['blk_0'=4,'blk_1'=4,'blk_2'=2,'col'=4] {'col'}, dimensions={0} | all-to-all | bytes 524288 | tf_op jit(solution)/shard_map/all_to_all | solution.py:25
  182.7 0.0 copy-done.1
  182.7 0.0 copy-done.2
  182.8 1.4 abs_reduce_fusion
  184.1 0.6 gather_fusion.5
  184.8 0.7 reduce.6
  185.5 10.7 %all_to_all.123 = bf16[32,2,256]{2,1,0:T(2,128)(2,1)S(1)} all-to-all(bf16[32,2,256]{2,1,0:T(2,128)(2,1)S(1)} %reshape.153), channel_id=1, replica_groups=mesh['blk_0'=4,'blk_1'=4,'blk_2'=2,'col'=4] {'blk_0','blk_1','blk_2'}, dimensions={0} | all-to-all | bytes 65536 | tf_op jit(solution)/shard_map/all_to_all | solution.py:55
  196.2 10.2 %fusion.1 = f32[32,1,512]{2,1,0:T(1,128)S(1)} fusion(bf16[32,512,512]{2,1,0:T(8,128)(2,1)} %param.10, bf16[32,1,512]{2,1,0:T(2,128)(2,1)S(1)} %reshape.154), kind=kOutput, calls=%fused_computation.8 | convolution fusion | flops 16777216 | bytes 16875520 | tf_op jit(solution)/shard_map/tuv,tv->tu/dot_general | solution.py:57
  206.4 1.0 fusion
  207.4 3.4 %all-to-all-start.12 = ((f32[4,32,512]{2,1,0:T(8,128)}), f32[4,32,512]{2,1,0:T(8,128)S(1)}, u32[]{:S(2)}, u32[]{:S(2)}) async-start(f32[4,32,512]{2,1,0:T(8,128)} %bitcast.25), calls=%async_computation.12 | async-start | bytes 524288 | tf_op jit(solution)/shard_map/all_to_all | solution.py:25
  214.6 0.1 stack.27
  214.7 8.9 %psum.28 = f32[6]{0:T(128)S(1)} all-reduce(f32[6]{0:T(128)S(1)} %stack.27), channel_id=1, replica_groups=mesh['blk_0'=4,'blk_1'=4,'blk_2'=2,'col'=4] {'blk_0'}, use_global_device_ids=true, to_apply=%region_12.0 | all-reduce | flops 6 | bytes 48 | tf_op jit(solution)/shard_map/psum | solution.py:30
  223.6 8.9 %psum.29 = f32[6]{0:T(128)S(1)} all-reduce(f32[6]{0:T(128)S(1)} %psum.28), channel_id=1, replica_groups=mesh['blk_0'=4,'blk_1'=4,'blk_2'=2,'col'=4] {'blk_1'}, use_global_device_ids=true, to_apply=%region_13.0 | all-reduce | flops 6 | bytes 48 | tf_op jit(solution)/shard_map/psum | solution.py:30
  232.5 2.4 psum.30
  234.9 11.4 %psum.31 = f32[6]{0:T(128)} all-reduce(f32[6]{0:T(128)S(1)} %psum.30), channel_id=1, replica_groups=mesh['blk_0'=4,'blk_1'=4,'blk_2'=2,'col'=4] {'col'}, use_global_device_ids=true, to_apply=%region_15.0 | all-reduce | flops 6 | bytes 48 | tf_op jit(solution)/shard_map/psum | solution.py:30
  246.3 0.0 all-to-all-done.12
  246.3 0.6 reduce_sum.113
  (22 shorter events, 0.4 us)
Async XLA Ops:
  0.6 53.1 %copy-start = (s32[32,512]{1,0:T(8,128)S(1)}, s32[32,512]{1,0:T(8,128)}, u32[]{:S(2)}) copy-start(s32[32,512]{1,0:T(8,128)} %param.9) | copy-start | bytes 196612
  0.6 41.7 %copy-start.3 = (s32[32]{0:T(128)S(1)}, s32[32]{0:T(128)}, u32[]{:S(2)}) copy-start(s32[32]{0:T(128)} %param.12) | copy-start | bytes 388
  2.0 15.7 %all-to-all-start = ((s32[32,1,1]{2,1,0:T(1,128)}), s32[32,1,1]{2,1,0:T(1,128)S(1)}, u32[]{:S(2)}, u32[]{:S(2)}) async-start(s32[32,1,1]{2,1,0:T(1,128)} %copy.17), calls=%async_computation | async-start | bytes 32768 | tf_op jit(solution)/shard_map/all_to_all | solution.py:46
  20.9 11.3 %all-to-all-start.1 = ((bf16[32,2,256]{2,1,0:T(2,128)(2,1)}), bf16[32,2,256]{2,1,0:T(2,128)(2,1)S(1)}, u32[]{:S(2)}, u32[]{:S(2)}) async-start(bf16[32,2,256]{2,1,0:T(2,128)(2,1)} %reshape.143), calls=%async_computation.1 | async-start | bytes 65536 | tf_op jit(solution)/shard_map/all_to_all | solution.py:55
  130.3 52.4 %copy-start.1 = (f32[32,512]{1,0:T(8,128)S(1)}, f32[32,512]{1,0:T(8,128)}, u32[]{:S(2)}) copy-start(f32[32,512]{1,0:T(8,128)} %param.8) | copy-start | bytes 196612
  130.3 52.4 %copy-start.2 = (f32[32,512]{1,0:T(8,128)S(1)}, f32[32,512]{1,0:T(8,128)}, u32[]{:S(2)}) copy-start(f32[32,512]{1,0:T(8,128)} %param.7) | copy-start | bytes 196612
  207.4 39.0 %all-to-all-start.12 = ((f32[4,32,512]{2,1,0:T(8,128)}), f32[4,32,512]{2,1,0:T(8,128)S(1)}, u32[]{:S(2)}, u32[]{:S(2)}) async-start(f32[4,32,512]{2,1,0:T(8,128)} %bitcast.25), calls=%async_computation.12 | async-start | bytes 524288 | tf_op jit(solution)/shard_map/all_to_all | solution.py:25
where the time goes:
time: 248 us; the launch traced here: 247 us
  blocking collectives  135 us (54%)
  matrix products  63.8 us (26%)
  starting transfers between devices  15.7 us (6%)
  waiting for transfers between devices  13.1 us (5%)
  other arithmetic  9.07 us (4%)
  local copies, waits for them, and re-layouts  5.96 us (2%)
  between operations  4.75 us (2%)
    dot_general x6, matrix products, on_device(): jnp.einsum('tuv,tv->tu', tile_weight, picked, preferred_element_type=jnp....  61.1 us
    all_to_all x5, blocking collectives, on_device(): lax.all_to_all(contrib[asked], BLK, split_axis=0, concat_axis=0, tiled=True)  53.5 us
    all_to_all x5, blocking collectives, summed_on_arrival(): lax.all_to_all(in_blocks(shard, dim, peers), axis, 0, 0, tiled=True)  49.5 us
    psum x4, blocking collectives, by_axis(): return functools.reduce(lax.psum, axes, shard)  31.6 us
    all_to_all x1, starting transfers between devices, on_device(): lax.all_to_all(wanted, BLK, split_axis=0, concat_axis=0, tiled=True)  8.42 us
    all_to_all x1, waiting for transfers between devices, on_device(): lax.all_to_all(contrib[asked], BLK, split_axis=0, concat_axis=0, tiled=True)  6.75 us
    all_to_all x1, waiting for transfers between devices, on_device(): lax.all_to_all(wanted, BLK, split_axis=0, concat_axis=0, tiled=True)  6.38 us
  transfers between devices with their start and end apart: 3, of which 2 were waited for; matrix products, arithmetic and copies ran while one was open for 1% of the time, Pallas kernels for 0%

commit v1 on v0

v1 whole, which is shorter than its diff:
```python
import functools

import jax
import jax.numpy as jnp
from jax import lax
from jax.experimental import pallas as pl
from jax.experimental.pallas import tpu as pltpu
from jax.sharding import Mesh
from jax.sharding import PartitionSpec as P

ITERS = 6
BLK = ("blk_0", "blk_1", "blk_2")
BLK_COL = ("blk_0", "blk_1", "blk_2", "col")
LANES = 128
GROUP = 8

damping = 0.85

VMEM = pl.BlockSpec(memory_space=pltpu.VMEM)
SMEM = pl.BlockSpec(memory_space=pltpu.SMEM)


def lane_row(column):
    rows = lax.broadcasted_iota(jnp.int32, column.shape, 0)
    lanes = lax.broadcasted_iota(jnp.int32, column.shape, 1)
    return jnp.sum(jnp.where(rows == lanes, column, 0.0), axis=0, keepdims=True)


def pieces(value):
    high = value.astype(jnp.bfloat16).astype(jnp.float32)
    rest = value - high
    middle = rest.astype(jnp.bfloat16).astype(jnp.float32)
    low = (rest - middle).astype(jnp.bfloat16).astype(jnp.float32)
    return high, middle, low


def plan_kernel(cols, me, row, valid, order, place, count):
    tiles = row.shape[0]
    owned = tiles
    c = me[0]

    def live(i, n):
        target = lax.rem(row[i] // owned + cols - c, cols) * owned + lax.rem(row[i], owned)
        place[i] = target

        @pl.when(valid[i] != 0)
        def _():
            order[n] = i

        return n + (valid[i] != 0).astype(jnp.int32)

    n = lax.fori_loop(0, tiles, live, jnp.int32(0))
    count[0] = n

    def rest(i, m):
        @pl.when(valid[i] == 0)
        def _():
            order[m] = i

        return m + (valid[i] == 0).astype(jnp.int32)

    lax.fori_loop(0, tiles, rest, n)


def send(asked, owned, contrib, message, extra):
    for b in range(asked.shape[0]):
        block = contrib[lax.rem(asked[b], owned)]
        if extra is None:
            message[b, 0:4, :] = block.astype(jnp.bfloat16)
        else:
            message[b] = jnp.concatenate([block, extra], axis=0).astype(jnp.bfloat16)


def first_kernel(asked, delta_in, rank_in, degree, message, scale, total, masses, contrib):
    owned = delta_in.shape[0]
    mass = jnp.zeros((1, LANES), jnp.float32)
    for r in range(4):
        part = slice(LANES * r, LANES * (r + 1))
        delta = delta_in[:, part]
        factor = damping / degree[:, part].astype(jnp.float32)
        scale[:, r, :] = factor
        total[:, r, :] = rank_in[:, part] + delta
        contrib[:, r, :] = (delta * factor)
        mass = mass + jnp.sum(jnp.abs(delta), axis=0, keepdims=True)
    masses[...] = jnp.concatenate([mass, jnp.zeros((7, LANES), jnp.float32)], axis=0)
    send(asked, owned, contrib, message, None)


def join_kernel(step, cells, asked, own, one, two, three, scale, total, masses, *rest):
    message, total_out, masses_out, contrib = rest
    owned = own.shape[0]
    delta = own[...] + one[...] + two[...] + three[...]
    total_out[...] = total[...] + delta
    contrib[...] = delta * scale[...]
    mass = jnp.sum(jnp.sum(jnp.abs(delta), axis=0), axis=0, keepdims=True)
    rows = lax.broadcasted_iota(jnp.int32, (8, LANES), 0)
    merged = jnp.where(rows == step, mass, masses[...])
    masses_out[...] = merged
    extra = None
    if step == ITERS - 1:
        sums = jnp.broadcast_to(jnp.sum(merged, axis=1, keepdims=True) / cells, (8, LANES))
        extra = jnp.concatenate([*pieces(lane_row(sums)), jnp.zeros((1, LANES), jnp.float32)], axis=0)
    send(asked, owned, contrib, message, extra)


def tile_kernel(last, order, place, count, picked, weight, own, one, two, three, vectors, sums):
    owned = weight.shape[0]
    sums[...] = jnp.zeros_like(sums)
    vectors[...] = picked[...].astype(jnp.float32)
    rows = lax.broadcasted_iota(jnp.int32, (8, LANES), 0)

    def group(g, carry):
        products = []
        for u in range(GROUP):
            i = g * GROUP + u
            j = order[i]
            live = jnp.where(i < count[0], 1.0, 0.0)
            wide = jnp.concatenate(
                [jnp.broadcast_to(vectors[j, r : r + 1, :], (8, LANES)) for r in range(4)], axis=1
            )
            product = lax.dot_general(
                (wide * live).astype(jnp.bfloat16),
                weight[j],
                (((1,), (1,)), ((), ())),
                preferred_element_type=jnp.float32,
            )
            block = product[:, 3 * LANES :]
            for r in (2, 1, 0):
                block = jnp.where(rows == r, product[:, LANES * r : LANES * (r + 1)], block)
            products.append((j, block))
        for j, block in products:
            q = place[j]
            sums[q] = sums[q] + block[:4]
        return carry

    lax.fori_loop(0, (count[0] + GROUP - 1) // GROUP, group, 0)
    for s, out in enumerate((own, one, two, three)):
        out[0:owned] = sums[s * owned : (s + 1) * owned]
    if last:
        mass = jnp.zeros((1, LANES), jnp.float32)
        for r in (4, 5, 6):
            mass = mass + jnp.sum(vectors[:, r, :], axis=0, keepdims=True)
        for out in (own, one, two, three):
            out[owned] = jnp.broadcast_to(mass, (4, LANES))


def last_kernel(me, own, one, two, three, total, rank_out, delta_out, masses, ordered):
    owned = total.shape[0]
    for r in range(4):
        part = slice(LANES * r, LANES * (r + 1))
        rank_out[:, part] = total[:, r, :]
        delta_out[:, part] = (
            own[0:owned, r, :] + one[0:owned, r, :] + two[0:owned, r, :] + three[0:owned, r, :]
        )
    for s, part in enumerate((own, one, two, three)):
        ordered[lax.rem(me[0] + 4 - s, 4)] = part[owned]
    masses[...] = (ordered[0] + ordered[1] + ordered[2] + ordered[3])[0:1]


def f32(*shape):
    return jax.ShapeDtypeStruct(shape, jnp.float32)


def s32(*shape):
    return jax.ShapeDtypeStruct(shape, jnp.int32)


def call(kernel, outs, specs_in, specs_out, scratch, vmem=8):
    return pl.pallas_call(
        kernel,
        out_shape=outs,
        in_specs=specs_in,
        out_specs=specs_out,
        scratch_shapes=scratch,
        compiler_params=pltpu.CompilerParams(vmem_limit_bytes=vmem << 20),
    )


def on_device(rank_in, delta_in, out_degree, tile_weight, tile_source, tile_row, tile_valid):
    owned, width = delta_in.shape
    tiles = tile_row.shape[0]
    n_group = lax.axis_size(BLK)
    n_column = lax.axis_size("col")
    cells = owned * n_group * n_column * width
    me = lax.axis_index("col").astype(jnp.int32).reshape(1)
    asked = lax.all_to_all(
        tile_source.reshape(n_group, 1), BLK, split_axis=0, concat_axis=0, tiled=True
    ).reshape(n_group)
    order, place, count = call(
        functools.partial(plan_kernel, n_column),
        (s32(tiles), s32(tiles), s32(1)),
        [SMEM] * 3,
        (SMEM,) * 3,
        [],
    )(me, tile_row, tile_valid)
    held = f32(owned, 4, LANES)
    message = jax.ShapeDtypeStruct((n_group, 8, LANES), jnp.bfloat16)
    block_scratch = pltpu.VMEM((owned, 4, LANES), jnp.float32)
    out, scale, total, masses = call(
        first_kernel,
        (message, held, held, f32(8, LANES)),
        [SMEM] + [VMEM] * 3,
        (VMEM,) * 4,
        [block_scratch],
    )(asked, delta_in, rank_in, out_degree)
    for step in range(ITERS):
        picked = lax.all_to_all(out, BLK, split_axis=0, concat_axis=0, tiled=True)
        last = step == ITERS - 1
        sent = f32(owned + last, 4, LANES)
        parts = call(
            functools.partial(tile_kernel, last),
            (sent,) * 4,
            [SMEM] * 3 + [VMEM] * 2,
            (VMEM,) * 4,
            [
                pltpu.VMEM((tiles, 8, LANES), jnp.float32),
                pltpu.VMEM((n_column * owned, 4, LANES), jnp.float32),
            ],
            vmem=24,
        )(order, place, count, picked, tile_weight)
        own, others = parts[0], parts[1:]
        others = [
            lax.ppermute(part, "col", [(i, (i + s + 1) % n_column) for i in range(n_column)])
            for s, part in enumerate(others)
        ]
        if not last:
            out, total, masses = call(
                functools.partial(join_kernel, step + 1, cells),
                (message, held, f32(8, LANES)),
                [SMEM] + [VMEM] * 7,
                (VMEM,) * 3,
                [block_scratch],
            )(asked, own, *others, scale, total, masses)
    rank_out, delta_out, stacked = call(
        last_kernel,
        (f32(owned, width), f32(owned, width), f32(1, LANES)),
        [SMEM] + [VMEM] * 5,
        (VMEM,) * 3,
        [pltpu.VMEM((4, 4, LANES), jnp.float32)],
    )(me, own, *others, total)
    return rank_out, delta_out, stacked[0, :ITERS]


def solution(mesh):
    finer = Mesh(
        mesh.devices.reshape(4, 4, 2, mesh.shape["col"]), ("blk_0", "blk_1", "blk_2", "col")
    )
    placed = (
        P(BLK_COL, None),
        P(BLK_COL, None),
        P(BLK_COL, None),
        P(BLK_COL, None, None),
        P(BLK_COL),
        P(BLK_COL),
        P(BLK_COL),
    )
    return jax.shard_map(
        on_device,
        mesh=finer,
        in_specs=placed,
        out_specs=(P(BLK_COL, None), P(BLK_COL, None), P()),
        check_vma=False,
    )
```

time: 248 us -> 183 us (0.74)
  blocking collectives: 135 us -> 68.1 us
  matrix products: 63.8 us -> 0 us
  Pallas kernels: 0 us -> 37.5 us
  starting transfers between devices: 15.7 us -> 34.9 us
  waiting for transfers between devices: 13.1 us -> 29.6 us
  other arithmetic: 9.07 us -> 0.66 us
  local copies, waits for them, and re-layouts: 5.96 us -> 10.8 us
  between operations: 4.75 us -> 0.77 us
    dot_general x12 -> x0, matrix products: 63.8 us -> none  [the longest x6 61.1 us: on_device(): jnp.einsum('tuv,tv->tu', tile_weight, picked, preferred_element_type=jnp....]
    pallas_call x0 -> x14, Pallas kernels: none -> 37.5 us  [the longest x6 29.4 us: on_device(): call(functools.partial(tile_kernel, last), (sent,) * 4, [SMEM] * 3 + [VME...]
    all_to_all x10 -> x6, blocking collectives: 103 us -> 68.1 us  [the longest x5 52.6 us: on_device(): picked = lax.all_to_all(out, BLK, split_axis=0, concat_axis=0, tiled=True)]
    psum x4 -> x0, blocking collectives: 31.6 us -> none  [by_axis(): return functools.reduce(lax.psum, axes, shard)]
    ppermute x0 -> x18, starting transfers between devices: none -> 31.1 us  [on_device(): lax.ppermute(part, 'col', [(i, (i + s + 1) % n_column) for i in range(n_c...]
    ppermute x0 -> x18, waiting for transfers between devices: none -> 25.4 us  [on_device(): lax.ppermute(part, 'col', [(i, (i + s + 1) % n_column) for i in range(n_c...]
    all_to_all x3 -> x1, starting transfers between devices: 15.7 us -> 3.86 us  [on_device(): picked = lax.all_to_all(out, BLK, split_axis=0, concat_axis=0, tiled=True)]
    all_to_all x3 -> x1, waiting for transfers between devices: 13.1 us -> 4.2 us  [on_device(): picked = lax.all_to_all(out, BLK, split_axis=0, concat_axis=0, tiled=True)]
  transfers between devices with their start and end apart: 3 -> 19, of which waited for: 2 -> 19; matrix products, arithmetic and copies ran while one was open for 1% -> 0% of each run, Pallas kernels for 0% -> 1%
where the time goes in v1:
time: 183 us; the launch traced here: 182 us
  blocking collectives  68.1 us (37%)
  Pallas kernels  37.5 us (20%)
  starting transfers between devices  34.9 us (19%)
  waiting for transfers between devices  29.6 us (16%)
  local copies, waits for them, and re-layouts  10.8 us (6%)
    all_to_all x5, blocking collectives, on_device(): picked = lax.all_to_all(out, BLK, split_axis=0, concat_axis=0, tiled=True)  52.6 us
    ppermute x18, starting transfers between devices, on_device(): lax.ppermute(part, 'col', [(i, (i + s + 1) % n_column) for i in range(n_c...  31.1 us
    pallas_call x6, Pallas kernels, on_device(): call(functools.partial(tile_kernel, last), (sent,) * 4, [SMEM] * 3 + [VME...  29.4 us
    ppermute x18, waiting for transfers between devices, on_device(): lax.ppermute(part, 'col', [(i, (i + s + 1) % n_column) for i in range(n_c...  25.4 us
    all_to_all x1, blocking collectives, on_device(): lax.all_to_all(tile_source.reshape(n_group, 1), BLK, split_axis=0, concat...  15.6 us
    unnamed x14, local copies, waits for them, and re-layouts  9.6 us
    all_to_all x1, waiting for transfers between devices, on_device(): picked = lax.all_to_all(out, BLK, split_axis=0, concat_axis=0, tiled=True)  4.2 us
    pallas_call x5, Pallas kernels, on_device(): call(functools.partial(join_kernel, step + 1, cells), (message, held, f32...  3.97 us
  transfers between devices with their start and end apart: 19, of which 19 were waited for; matrix products, arithmetic and copies ran while one was open for 0% of the time, Pallas kernels for 1%

profile of v1, /device:TPU:0, one launch (start us, length us, event | category | flops | bytes accessed | tf_op | source)
XLA Modules:
  0.0 182.4 jit_solution(16071366674357799684)
XLA Ops:
  0.6 0.7 copy.11
  1.4 15.6 %all_to_all.39 = s32[32,1,1]{2,1,0:T(1,128)S(1)} all-to-all(s32[32,1,1]{2,1,0:T(1,128)S(1)} %copy.11), channel_id=1, replica_groups=mesh['blk_0'=4,'blk_1'=4,'blk_2'=2,'col'=4] {'blk_0','blk_1','blk_2'}, dimensions={0} | all-to-all | bytes 256 | tf_op jit(solution)/shard_map/all_to_all | solution.py:186
  16.9 0.7 reduce.asked
  17.6 0.8 copy-done.2
  18.4 0.8 copy-done.3
  19.3 0.8 copy-done.4
  20.1 1.3 shard_map.95
  21.4 3.9 %all-to-all-start.1 = ((bf16[32,8,128]{2,1,0:T(8,128)(2,1)}), bf16[32,8,128]{2,1,0:T(8,128)(2,1)S(1)}, u32[]{:S(2)}, u32[]{:S(2)}) async-start(bf16[32,8,128]{2,1,0:T(8,128)(2,1)} %get-tuple-element.54), calls=%async_computation.1 | async-start | bytes 131072 | tf_op jit(solution)/shard_map/all_to_all | solution.py:207
  25.3 0.0 copy-start.5
  25.3 0.6 copy-done.5
  26.0 0.7 copy-done.6
  26.6 2.0 %shard_map.94 = (s32[32]{0:T(128)S(1)}, s32[32]{0:T(128)S(1)}, s32[1]{0:T(128)}) custom-call(s32[1]{0:T(128)} %bitcast.me, s32[32]{0:T(128)S(1)} %copy-done.5, s32[32]{0:T(128)S(1)} %copy-done.6), custom_call_target="tpu_custom_call" | custom-call | tf_op jit(solution)/shard_map/pallas_call | solution.py:189
  28.6 4.2 %all-to-all-done.1.picked = bf16[32,8,128]{2,1,0:T(8,128)(2,1)S(1)} async-done(((bf16[32,8,128]{2,1,0:T(8,128)(2,1)}), bf16[32,8,128]{2,1,0:T(8,128)(2,1)S(1)}, u32[]{:S(2)}, u32[]{:S(2)}) %all-to-all-start.1) | async-done | bytes 65568 | tf_op jit(solution)/shard_map/all_to_all | solution.py:207
  32.8 5.8 %copy-done = bf16[32,512,512]{2,1,0:T(8,128)(2,1)S(1)} copy-done((bf16[32,512,512]{2,1,0:T(8,128)(2,1)S(1)}, bf16[32,512,512]{2,1,0:T(8,128)(2,1)}, u32[]{:S(2)}) %copy-start) | copy-done | bytes 16777240
  38.6 5.0 %shard_map.96 = (f32[32,4,128]{2,1,0:T(4,128)S(1)}, f32[32,4,128]{2,1,0:T(4,128)S(1)}, f32[32,4,128]{2,1,0:T(4,128)S(1)}, f32[32,4,128]{2,1,0:T(4,128)S(1)}) custom-call(s32[32]{0:T(128)S(1)} %get-tuple-element.51.order, s32[32]{0:T(128)S(1)} %get-tuple-element.52.place, s32[1]{0:T(128)} %get-tuple-element.53.count, ...), custom_call_target="tpu_custom_call" | custom-call | tf_op jit(solution)/shard_map/pallas_call | solution.py:210
  43.6 1.6 collective-permute-start
  45.2 3.9 %collective-permute-start.1 = (f32[32,4,128]{2,1,0:T(4,128)S(1)}, f32[32,4,128]{2,1,0:T(4,128)S(1)}, u32[]{:S(2)}, u32[]{:S(2)}) collective-permute-start(f32[32,4,128]{2,1,0:T(4,128)S(1)} %get-tuple-element.57), channel_id=1, source_target_pairs={{0,2},{1,3},{2,0},{3,1},{4,6},{5,7},{6,4},{7,5},{8,10},{9,11},{10,... | collective-permute-start | bytes 196616 | tf_op jit(solution)/shard_map/ppermute | solution.py:223
  49.1 0.2 collective-permute-start.2
  49.3 0.6 collective-permute-done.one
  49.9 2.5 %collective-permute-done.1.two = f32[32,4,128]{2,1,0:T(4,128)S(1)} collective-permute-done((f32[32,4,128]{2,1,0:T(4,128)S(1)}, f32[32,4,128]{2,1,0:T(4,128)S(1)}, u32[]{:S(2)}, u32[]{:S(2)}) %collective-permute-start.1) | collective-permute-done | bytes 65568 | tf_op jit(solution)/shard_map/ppermute | solution.py:223
  52.4 1.0 collective-permute-done.2.three
  53.4 0.7 shard_map.97
  54.0 10.4 %all_to_all.40.picked = bf16[32,8,128]{2,1,0:T(8,128)(2,1)S(1)} all-to-all(bf16[32,8,128]{2,1,0:T(8,128)(2,1)S(1)} %get-tuple-element.62), channel_id=1, replica_groups=mesh['blk_0'=4,'blk_1'=4,'blk_2'=2,'col'=4] {'blk_0','blk_1','blk_2'}, dimensions={0} | all-to-all | bytes 131072 | tf_op jit(solution)/shard_map/all_to_all | solution.py:207
  64.5 4.9 %shard_map.98 = (f32[32,4,128]{2,1,0:T(4,128)S(1)}, f32[32,4,128]{2,1,0:T(4,128)S(1)}, f32[32,4,128]{2,1,0:T(4,128)S(1)}, f32[32,4,128]{2,1,0:T(4,128)S(1)}) custom-call(s32[32]{0:T(128)S(1)} %get-tuple-element.51.order, s32[32]{0:T(128)S(1)} %get-tuple-element.52.place, s32[1]{0:T(128)} %get-tuple-element.53.count, ...), custom_call_target="tpu_custom_call" | custom-call | tf_op jit(solution)/shard_map/pallas_call | solution.py:210
  69.4 0.9 collective-permute-start.3
  70.3 4.9 %collective-permute-start.4 = (f32[32,4,128]{2,1,0:T(4,128)S(1)}, f32[32,4,128]{2,1,0:T(4,128)S(1)}, u32[]{:S(2)}, u32[]{:S(2)}) collective-permute-start(f32[32,4,128]{2,1,0:T(4,128)S(1)} %get-tuple-element.65), channel_id=1, source_target_pairs={{0,2},{1,3},{2,0},{3,1},{4,6},{5,7},{6,4},{7,5},{8,10},{9,11},{10,... | collective-permute-start | bytes 196616 | tf_op jit(solution)/shard_map/ppermute | solution.py:223
  75.2 1.5 collective-permute-done.3.one
  76.7 1.5 collective-permute-done.4.two
  78.1 1.3 collective-permute-done.5.three
  79.4 0.7 shard_map.99
  80.1 10.4 %all_to_all.41.picked = bf16[32,8,128]{2,1,0:T(8,128)(2,1)S(1)} all-to-all(bf16[32,8,128]{2,1,0:T(8,128)(2,1)S(1)} %get-tuple-element.69), channel_id=1, replica_groups=mesh['blk_0'=4,'blk_1'=4,'blk_2'=2,'col'=4] {'blk_0','blk_1','blk_2'}, dimensions={0} | all-to-all | bytes 131072 | tf_op jit(solution)/shard_map/all_to_all | solution.py:207
  90.6 4.9 %shard_map.100 = (f32[32,4,128]{2,1,0:T(4,128)S(1)}, f32[32,4,128]{2,1,0:T(4,128)S(1)}, f32[32,4,128]{2,1,0:T(4,128)S(1)}, f32[32,4,128]{2,1,0:T(4,128)S(1)}) custom-call(s32[32]{0:T(128)S(1)} %get-tuple-element.51.order, s32[32]{0:T(128)S(1)} %get-tuple-element.52.place, s32[1]{0:T(128)} %get-tuple-element.53.count, ...), custom_call_target="tpu_custom_call" | custom-call | tf_op jit(solution)/shard_map/pallas_call | solution.py:210
  95.4 0.3 collective-permute-start.6
  95.7 4.2 %collective-permute-start.7 = (f32[32,4,128]{2,1,0:T(4,128)S(1)}, f32[32,4,128]{2,1,0:T(4,128)S(1)}, u32[]{:S(2)}, u32[]{:S(2)}) collective-permute-start(f32[32,4,128]{2,1,0:T(4,128)S(1)} %get-tuple-element.72), channel_id=1, source_target_pairs={{0,2},{1,3},{2,0},{3,1},{4,6},{5,7},{6,4},{7,5},{8,10},{9,11},{10,... | collective-permute-start | bytes 196616 | tf_op jit(solution)/shard_map/ppermute | solution.py:223
  100.0 1.0 collective-permute-done.6.one
  101.0 2.0 %collective-permute-done.7.two = f32[32,4,128]{2,1,0:T(4,128)S(1)} collective-permute-done((f32[32,4,128]{2,1,0:T(4,128)S(1)}, f32[32,4,128]{2,1,0:T(4,128)S(1)}, u32[]{:S(2)}, u32[]{:S(2)}) %collective-permute-start.7) | collective-permute-done | bytes 65568 | tf_op jit(solution)/shard_map/ppermute | solution.py:223
  103.0 1.2 collective-permute-done.8.three
  104.2 0.7 shard_map.101
  104.9 10.6 %all_to_all.42.picked = bf16[32,8,128]{2,1,0:T(8,128)(2,1)S(1)} all-to-all(bf16[32,8,128]{2,1,0:T(8,128)(2,1)S(1)} %get-tuple-element.76), channel_id=1, replica_groups=mesh['blk_0'=4,'blk_1'=4,'blk_2'=2,'col'=4] {'blk_0','blk_1','blk_2'}, dimensions={0} | all-to-all | bytes 131072 | tf_op jit(solution)/shard_map/all_to_all | solution.py:207
  115.5 4.9 %shard_map.102 = (f32[32,4,128]{2,1,0:T(4,128)S(1)}, f32[32,4,128]{2,1,0:T(4,128)S(1)}, f32[32,4,128]{2,1,0:T(4,128)S(1)}, f32[32,4,128]{2,1,0:T(4,128)S(1)}) custom-call(s32[32]{0:T(128)S(1)} %get-tuple-element.51.order, s32[32]{0:T(128)S(1)} %get-tuple-element.52.place, s32[1]{0:T(128)} %get-tuple-element.53.count, ...), custom_call_target="tpu_custom_call" | custom-call | tf_op jit(solution)/shard_map/pallas_call | solution.py:210
  120.4 1.0 collective-permute-start.9
  121.4 4.2 %collective-permute-start.10 = (f32[32,4,128]{2,1,0:T(4,128)S(1)}, f32[32,4,128]{2,1,0:T(4,128)S(1)}, u32[]{:S(2)}, u32[]{:S(2)}) collective-permute-start(f32[32,4,128]{2,1,0:T(4,128)S(1)} %get-tuple-element.79), channel_id=1, source_target_pairs={{0,2},{1,3},{2,0},{3,1},{4,6},{5,7},{6,4},{7,5},{8,10},{9,11},{10,... | collective-permute-start | bytes 196616 | tf_op jit(solution)/shard_map/ppermute | solution.py:223
  125.7 0.8 collective-permute-done.9.one
  126.4 2.2 %collective-permute-done.10.two = f32[32,4,128]{2,1,0:T(4,128)S(1)} collective-permute-done((f32[32,4,128]{2,1,0:T(4,128)S(1)}, f32[32,4,128]{2,1,0:T(4,128)S(1)}, u32[]{:S(2)}, u32[]{:S(2)}) %collective-permute-start.10) | collective-permute-done | bytes 65568 | tf_op jit(solution)/shard_map/ppermute | solution.py:223
  128.7 1.3 collective-permute-done.11.three
  129.9 0.7 shard_map.103
  130.6 10.4 %all_to_all.43.picked = bf16[32,8,128]{2,1,0:T(8,128)(2,1)S(1)} all-to-all(bf16[32,8,128]{2,1,0:T(8,128)(2,1)S(1)} %get-tuple-element.83), channel_id=1, replica_groups=mesh['blk_0'=4,'blk_1'=4,'blk_2'=2,'col'=4] {'blk_0','blk_1','blk_2'}, dimensions={0} | all-to-all | bytes 131072 | tf_op jit(solution)/shard_map/all_to_all | solution.py:207
  141.0 4.9 %shard_map.104 = (f32[32,4,128]{2,1,0:T(4,128)S(1)}, f32[32,4,128]{2,1,0:T(4,128)S(1)}, f32[32,4,128]{2,1,0:T(4,128)S(1)}, f32[32,4,128]{2,1,0:T(4,128)S(1)}) custom-call(s32[32]{0:T(128)S(1)} %get-tuple-element.51.order, s32[32]{0:T(128)S(1)} %get-tuple-element.52.place, s32[1]{0:T(128)} %get-tuple-element.53.count, ...), custom_call_target="tpu_custom_call" | custom-call | tf_op jit(solution)/shard_map/pallas_call | solution.py:210
  145.9 0.5 collective-permute-start.12
  146.4 4.2 %collective-permute-start.13 = (f32[32,4,128]{2,1,0:T(4,128)S(1)}, f32[32,4,128]{2,1,0:T(4,128)S(1)}, u32[]{:S(2)}, u32[]{:S(2)}) collective-permute-start(f32[32,4,128]{2,1,0:T(4,128)S(1)} %get-tuple-element.86), channel_id=1, source_target_pairs={{0,2},{1,3},{2,0},{3,1},{4,6},{5,7},{6,4},{7,5},{8,10},{9,11},{10,... | collective-permute-start | bytes 196616 | tf_op jit(solution)/shard_map/ppermute | solution.py:223
  150.6 0.0 collective-permute-start.14
  150.6 0.8 collective-permute-done.12.one
  151.5 2.2 %collective-permute-done.13.two = f32[32,4,128]{2,1,0:T(4,128)S(1)} collective-permute-done((f32[32,4,128]{2,1,0:T(4,128)S(1)}, f32[32,4,128]{2,1,0:T(4,128)S(1)}, u32[]{:S(2)}, u32[]{:S(2)}) %collective-permute-start.13) | collective-permute-done | bytes 65568 | tf_op jit(solution)/shard_map/ppermute | solution.py:223
  153.7 1.2 collective-permute-done.14.three
  154.9 1.3 shard_map.105
  156.2 10.6 %all_to_all.44.picked = bf16[32,8,128]{2,1,0:T(8,128)(2,1)S(1)} all-to-all(bf16[32,8,128]{2,1,0:T(8,128)(2,1)S(1)} %get-tuple-element.90), channel_id=1, replica_groups=mesh['blk_0'=4,'blk_1'=4,'blk_2'=2,'col'=4] {'blk_0','blk_1','blk_2'}, dimensions={0} | all-to-all | bytes 131072 | tf_op jit(solution)/shard_map/all_to_all | solution.py:207
  166.8 4.9 %shard_map.106 = (f32[33,4,128]{2,1,0:T(4,128)S(1)}, f32[33,4,128]{2,1,0:T(4,128)S(1)}, f32[33,4,128]{2,1,0:T(4,128)S(1)}, f32[33,4,128]{2,1,0:T(4,128)S(1)}) custom-call(s32[32]{0:T(128)S(1)} %get-tuple-element.51.order, s32[32]{0:T(128)S(1)} %get-tuple-element.52.place, s32[1]{0:T(128)} %get-tuple-element.53.count, ...), custom_call_target="tpu_custom_call" | custom-call | tf_op jit(solution)/shard_map/pallas_call | solution.py:210
  171.7 0.8 collective-permute-start.15
  172.6 4.2 %collective-permute-start.16 = (f32[33,4,128]{2,1,0:T(4,128)S(1)}, f32[33,4,128]{2,1,0:T(4,128)S(1)}, u32[]{:S(2)}, u32[]{:S(2)}) collective-permute-start(f32[33,4,128]{2,1,0:T(4,128)S(1)} %get-tuple-element.93), channel_id=1, source_target_pairs={{0,2},{1,3},{2,0},{3,1},{4,6},{5,7},{6,4},{7,5},{8,10},{9,11},{10,... | collective-permute-start | bytes 202760 | tf_op jit(solution)/shard_map/ppermute | solution.py:223
  176.8 0.8 collective-permute-done.15.one
  177.6 2.3 %collective-permute-done.16.two = f32[33,4,128]{2,1,0:T(4,128)S(1)} collective-permute-done((f32[33,4,128]{2,1,0:T(4,128)S(1)}, f32[33,4,128]{2,1,0:T(4,128)S(1)}, u32[]{:S(2)}, u32[]{:S(2)}) %collective-permute-start.16) | collective-permute-done | bytes 67616 | tf_op jit(solution)/shard_map/ppermute | solution.py:223
  179.9 1.2 collective-permute-done.17.three
  181.1 0.8 shard_map.107
  181.9 0.5 slice_bitcast_fusion
  (11 shorter events, 0.0 us)
Async XLA Ops:
  17.6 0.8 copy-start.2
  18.4 0.8 copy-start.3
  19.3 0.8 copy-start.4
  21.4 11.3 %all-to-all-start.1 = ((bf16[32,8,128]{2,1,0:T(8,128)(2,1)}), bf16[32,8,128]{2,1,0:T(8,128)(2,1)S(1)}, u32[]{:S(2)}, u32[]{:S(2)}) async-start(bf16[32,8,128]{2,1,0:T(8,128)(2,1)} %get-tuple-element.54), calls=%async_computation.1 | async-start | bytes 131072 | tf_op jit(solution)/shard_map/all_to_all | solution.py:207
  25.3 0.7 copy-start.5
  26.0 0.7 copy-start.6
  32.8 5.8 %copy-start = (bf16[32,512,512]{2,1,0:T(8,128)(2,1)S(1)}, bf16[32,512,512]{2,1,0:T(8,128)(2,1)}, u32[]{:S(2)}) copy-start(bf16[32,512,512]{2,1,0:T(8,128)(2,1)} %weight.11) | copy-start | bytes 50331652
  38.6 25.9 %copy-start.1 = (bf16[32,512,512]{2,1,0:T(8,128)(2,1)S(1)}, bf16[32,512,512]{2,1,0:T(8,128)(2,1)}, u32[]{:S(2)}) copy-start(bf16[32,512,512]{2,1,0:T(8,128)(2,1)} %weight.11) | copy-start | bytes 50331652
  43.6 6.3 %collective-permute-start = (f32[32,4,128]{2,1,0:T(4,128)S(1)}, f32[32,4,128]{2,1,0:T(4,128)S(1)}, u32[]{:S(2)}, u32[]{:S(2)}) collective-permute-start(f32[32,4,128]{2,1,0:T(4,128)S(1)} %get-tuple-element.56), channel_id=1, source_target_pairs={{0,1},{1,2},{2,3},{3,0},{4,5},{5,6},{6,7},{7,4},{8,9},{9,10},{10,1... | collective-permute-start | bytes 196616 | tf_op jit(solution)/shard_map/ppermute | solution.py:223
  45.2 7.2 %collective-permute-start.1 = (f32[32,4,128]{2,1,0:T(4,128)S(1)}, f32[32,4,128]{2,1,0:T(4,128)S(1)}, u32[]{:S(2)}, u32[]{:S(2)}) collective-permute-start(f32[32,4,128]{2,1,0:T(4,128)S(1)} %get-tuple-element.57), channel_id=1, source_target_pairs={{0,2},{1,3},{2,0},{3,1},{4,6},{5,7},{6,4},{7,5},{8,10},{9,11},{10,... | collective-permute-start | bytes 196616 | tf_op jit(solution)/shard_map/ppermute | solution.py:223
  49.1 4.3 %collective-permute-start.2 = (f32[32,4,128]{2,1,0:T(4,128)S(1)}, f32[32,4,128]{2,1,0:T(4,128)S(1)}, u32[]{:S(2)}, u32[]{:S(2)}) collective-permute-start(f32[32,4,128]{2,1,0:T(4,128)S(1)} %get-tuple-element.58), channel_id=1, source_target_pairs={{0,3},{1,0},{2,1},{3,2},{4,7},{5,4},{6,5},{7,6},{8,11},{9,8},{10,9... | collective-permute-start | bytes 196616 | tf_op jit(solution)/shard_map/ppermute | solution.py:223
  69.4 7.3 %collective-permute-start.3 = (f32[32,4,128]{2,1,0:T(4,128)S(1)}, f32[32,4,128]{2,1,0:T(4,128)S(1)}, u32[]{:S(2)}, u32[]{:S(2)}) collective-permute-start(f32[32,4,128]{2,1,0:T(4,128)S(1)} %get-tuple-element.64), channel_id=1, source_target_pairs={{0,1},{1,2},{2,3},{3,0},{4,5},{5,6},{6,7},{7,4},{8,9},{9,10},{10,1... | collective-permute-start | bytes 196616 | tf_op jit(solution)/shard_map/ppermute | solution.py:223
  70.3 7.8 %collective-permute-start.4 = (f32[32,4,128]{2,1,0:T(4,128)S(1)}, f32[32,4,128]{2,1,0:T(4,128)S(1)}, u32[]{:S(2)}, u32[]{:S(2)}) collective-permute-start(f32[32,4,128]{2,1,0:T(4,128)S(1)} %get-tuple-element.65), channel_id=1, source_target_pairs={{0,2},{1,3},{2,0},{3,1},{4,6},{5,7},{6,4},{7,5},{8,10},{9,11},{10,... | collective-permute-start | bytes 196616 | tf_op jit(solution)/shard_map/ppermute | solution.py:223
  75.2 4.3 %collective-permute-start.5 = (f32[32,4,128]{2,1,0:T(4,128)S(1)}, f32[32,4,128]{2,1,0:T(4,128)S(1)}, u32[]{:S(2)}, u32[]{:S(2)}) collective-permute-start(f32[32,4,128]{2,1,0:T(4,128)S(1)} %get-tuple-element.66), channel_id=1, source_target_pairs={{0,3},{1,0},{2,1},{3,2},{4,7},{5,4},{6,5},{7,6},{8,11},{9,8},{10,9... | collective-permute-start | bytes 196616 | tf_op jit(solution)/shard_map/ppermute | solution.py:223
  95.4 5.6 %collective-permute-start.6 = (f32[32,4,128]{2,1,0:T(4,128)S(1)}, f32[32,4,128]{2,1,0:T(4,128)S(1)}, u32[]{:S(2)}, u32[]{:S(2)}) collective-permute-start(f32[32,4,128]{2,1,0:T(4,128)S(1)} %get-tuple-element.71), channel_id=1, source_target_pairs={{0,1},{1,2},{2,3},{3,0},{4,5},{5,6},{6,7},{7,4},{8,9},{9,10},{10,1... | collective-permute-start | bytes 196616 | tf_op jit(solution)/shard_map/ppermute | solution.py:223
  95.7 7.2 %collective-permute-start.7 = (f32[32,4,128]{2,1,0:T(4,128)S(1)}, f32[32,4,128]{2,1,0:T(4,128)S(1)}, u32[]{:S(2)}, u32[]{:S(2)}) collective-permute-start(f32[32,4,128]{2,1,0:T(4,128)S(1)} %get-tuple-element.72), channel_id=1, source_target_pairs={{0,2},{1,3},{2,0},{3,1},{4,6},{5,7},{6,4},{7,5},{8,10},{9,11},{10,... | collective-permute-start | bytes 196616 | tf_op jit(solution)/shard_map/ppermute | solution.py:223
  100.0 4.3 %collective-permute-start.8 = (f32[32,4,128]{2,1,0:T(4,128)S(1)}, f32[32,4,128]{2,1,0:T(4,128)S(1)}, u32[]{:S(2)}, u32[]{:S(2)}) collective-permute-start(f32[32,4,128]{2,1,0:T(4,128)S(1)} %get-tuple-element.73), channel_id=1, source_target_pairs={{0,3},{1,0},{2,1},{3,2},{4,7},{5,4},{6,5},{7,6},{8,11},{9,8},{10,9... | collective-permute-start | bytes 196616 | tf_op jit(solution)/shard_map/ppermute | solution.py:223
  120.4 6.0 %collective-permute-start.9 = (f32[32,4,128]{2,1,0:T(4,128)S(1)}, f32[32,4,128]{2,1,0:T(4,128)S(1)}, u32[]{:S(2)}, u32[]{:S(2)}) collective-permute-start(f32[32,4,128]{2,1,0:T(4,128)S(1)} %get-tuple-element.78), channel_id=1, source_target_pairs={{0,1},{1,2},{2,3},{3,0},{4,5},{5,6},{6,7},{7,4},{8,9},{9,10},{10,1... | collective-permute-start | bytes 196616 | tf_op jit(solution)/shard_map/ppermute | solution.py:223
  121.4 7.2 %collective-permute-start.10 = (f32[32,4,128]{2,1,0:T(4,128)S(1)}, f32[32,4,128]{2,1,0:T(4,128)S(1)}, u32[]{:S(2)}, u32[]{:S(2)}) collective-permute-start(f32[32,4,128]{2,1,0:T(4,128)S(1)} %get-tuple-element.79), channel_id=1, source_target_pairs={{0,2},{1,3},{2,0},{3,1},{4,6},{5,7},{6,4},{7,5},{8,10},{9,11},{10,... | collective-permute-start | bytes 196616 | tf_op jit(solution)/shard_map/ppermute | solution.py:223
  125.7 4.3 %collective-permute-start.11 = (f32[32,4,128]{2,1,0:T(4,128)S(1)}, f32[32,4,128]{2,1,0:T(4,128)S(1)}, u32[]{:S(2)}, u32[]{:S(2)}) collective-permute-start(f32[32,4,128]{2,1,0:T(4,128)S(1)} %get-tuple-element.80), channel_id=1, source_target_pairs={{0,3},{1,0},{2,1},{3,2},{4,7},{5,4},{6,5},{7,6},{8,11},{9,8},{10,9... | collective-permute-start | bytes 196616 | tf_op jit(solution)/shard_map/ppermute | solution.py:223
  145.9 5.5 %collective-permute-start.12 = (f32[32,4,128]{2,1,0:T(4,128)S(1)}, f32[32,4,128]{2,1,0:T(4,128)S(1)}, u32[]{:S(2)}, u32[]{:S(2)}) collective-permute-start(f32[32,4,128]{2,1,0:T(4,128)S(1)} %get-tuple-element.85), channel_id=1, source_target_pairs={{0,1},{1,2},{2,3},{3,0},{4,5},{5,6},{6,7},{7,4},{8,9},{9,10},{10,1... | collective-permute-start | bytes 196616 | tf_op jit(solution)/shard_map/ppermute | solution.py:223
  146.4 7.2 %collective-permute-start.13 = (f32[32,4,128]{2,1,0:T(4,128)S(1)}, f32[32,4,128]{2,1,0:T(4,128)S(1)}, u32[]{:S(2)}, u32[]{:S(2)}) collective-permute-start(f32[32,4,128]{2,1,0:T(4,128)S(1)} %get-tuple-element.86), channel_id=1, source_target_pairs={{0,2},{1,3},{2,0},{3,1},{4,6},{5,7},{6,4},{7,5},{8,10},{9,11},{10,... | collective-permute-start | bytes 196616 | tf_op jit(solution)/shard_map/ppermute | solution.py:223
  150.6 4.3 %collective-permute-start.14 = (f32[32,4,128]{2,1,0:T(4,128)S(1)}, f32[32,4,128]{2,1,0:T(4,128)S(1)}, u32[]{:S(2)}, u32[]{:S(2)}) collective-permute-start(f32[32,4,128]{2,1,0:T(4,128)S(1)} %get-tuple-element.87), channel_id=1, source_target_pairs={{0,3},{1,0},{2,1},{3,2},{4,7},{5,4},{6,5},{7,6},{8,11},{9,8},{10,9... | collective-permute-start | bytes 196616 | tf_op jit(solution)/shard_map/ppermute | solution.py:223
  171.7 5.9 %collective-permute-start.15 = (f32[33,4,128]{2,1,0:T(4,128)S(1)}, f32[33,4,128]{2,1,0:T(4,128)S(1)}, u32[]{:S(2)}, u32[]{:S(2)}) collective-permute-start(f32[33,4,128]{2,1,0:T(4,128)S(1)} %get-tuple-element.92), channel_id=1, source_target_pairs={{0,1},{1,2},{2,3},{3,0},{4,5},{5,6},{6,7},{7,4},{8,9},{9,10},{10,1... | collective-permute-start | bytes 202760 | tf_op jit(solution)/shard_map/ppermute | solution.py:223
  172.6 7.3 %collective-permute-start.16 = (f32[33,4,128]{2,1,0:T(4,128)S(1)}, f32[33,4,128]{2,1,0:T(4,128)S(1)}, u32[]{:S(2)}, u32[]{:S(2)}) collective-permute-start(f32[33,4,128]{2,1,0:T(4,128)S(1)} %get-tuple-element.93), channel_id=1, source_target_pairs={{0,2},{1,3},{2,0},{3,1},{4,6},{5,7},{6,4},{7,5},{8,10},{9,11},{10,... | collective-permute-start | bytes 202760 | tf_op jit(solution)/shard_map/ppermute | solution.py:223
  176.8 4.3 %collective-permute-start.17 = (f32[33,4,128]{2,1,0:T(4,128)S(1)}, f32[33,4,128]{2,1,0:T(4,128)S(1)}, u32[]{:S(2)}, u32[]{:S(2)}) collective-permute-start(f32[33,4,128]{2,1,0:T(4,128)S(1)} %get-tuple-element.94), channel_id=1, source_target_pairs={{0,3},{1,0},{2,1},{3,2},{4,7},{5,4},{6,5},{7,6},{8,11},{9,8},{10,9... | collective-permute-start | bytes 202760 | tf_op jit(solution)/shard_map/ppermute | solution.py:223

commit v2 on v1

v2 whole, which is shorter than its diff:
```python
import functools

import jax
import jax.numpy as jnp
from jax import lax
from jax.experimental import pallas as pl
from jax.experimental.pallas import tpu as pltpu
from jax.sharding import Mesh
from jax.sharding import PartitionSpec as P

ITERS = 6
BLK = ("blk_0", "blk_1", "blk_2")
BLK_COL = ("blk_0", "blk_1", "blk_2", "col")
LANES = 128
GROUP = 16
FIRST_GROUP = 4
EARLY = 20

damping = 0.85

VMEM = pl.BlockSpec(memory_space=pltpu.VMEM)
SMEM = pl.BlockSpec(memory_space=pltpu.SMEM)
HBM = pl.BlockSpec(memory_space=pltpu.HBM)


def lane_row(column):
    rows = lax.broadcasted_iota(jnp.int32, column.shape, 0)
    lanes = lax.broadcasted_iota(jnp.int32, column.shape, 1)
    return jnp.sum(jnp.where(rows == lanes, column, 0.0), axis=0, keepdims=True)


def pieces(value):
    high = value.astype(jnp.bfloat16).astype(jnp.float32)
    rest = value - high
    middle = rest.astype(jnp.bfloat16).astype(jnp.float32)
    low = (rest - middle).astype(jnp.bfloat16).astype(jnp.float32)
    return high, middle, low


def plan(cols, c, row, valid, table):
    tiles = row.shape[0]
    owned = tiles

    def live(i, n):
        table[tiles + i] = lax.rem(row[i] // owned + cols - c, cols) * owned + lax.rem(row[i], owned)
        table[3 * tiles + i] = valid[i]

        @pl.when(valid[i] != 0)
        def _():
            table[n] = i

        return n + (valid[i] != 0).astype(jnp.int32)

    n = lax.fori_loop(0, tiles, live, jnp.int32(0))
    table[2 * tiles] = n

    def rest(i, m):
        @pl.when(valid[i] == 0)
        def _():
            table[m] = i

        return m + (valid[i] == 0).astype(jnp.int32)

    lax.fori_loop(0, tiles, rest, n)


def send(asked, owned, contrib, message, extra):
    for b in range(asked.shape[0]):
        block = contrib[lax.rem(asked[b, 0, 0], owned)]
        if extra is None:
            message[b, 0:4, :] = block.astype(jnp.bfloat16)
        else:
            message[b] = jnp.concatenate([block, extra], axis=0).astype(jnp.bfloat16)


def stage_kernel(cols, *refs):
    me, delta_hbm, rank_hbm, degree_hbm, row_hbm, valid_hbm = refs[:6]
    table, scale, total, masses, contrib = refs[6:11]
    delta_in, rank_in, degree, row, valid, sems = refs[11:]
    copies = [
        pltpu.make_async_copy(source, target, sems.at[i])
        for i, (source, target) in enumerate(
            (
                (row_hbm, row),
                (valid_hbm, valid),
                (delta_hbm, delta_in),
                (rank_hbm, rank_in),
                (degree_hbm, degree),
            )
        )
    ]
    for copy in copies:
        copy.start()
    for copy in copies:
        copy.wait()
    plan(cols, me[0], row, valid, table)
    mass = jnp.zeros((1, LANES), jnp.float32)
    for r in range(4):
        part = slice(LANES * r, LANES * (r + 1))
        delta = delta_in[:, part]
        factor = damping / degree[:, part].astype(jnp.float32)
        scale[:, r, :] = factor
        total[:, r, :] = rank_in[:, part] + delta
        contrib[:, r, :] = delta * factor
        mass = mass + jnp.sum(jnp.abs(delta), axis=0, keepdims=True)
    masses[...] = jnp.concatenate([mass, jnp.zeros((7, LANES), jnp.float32)], axis=0)


def turn_kernel(low, high, *refs):
    weight, turned, mark = refs[0], refs[-2], refs[-1]
    mark[...] = jnp.zeros_like(mark)

    def turn(i, carry):
        turned[low + 2 * i] = weight[low + 2 * i].T
        turned[low + 2 * i + 1] = weight[low + 2 * i + 1].T
        return carry

    lax.fori_loop(0, (high - low) // 2, turn, 0)


def first_kernel(asked, contrib, message):
    send(asked, contrib.shape[0], contrib, message, None)


def join_kernel(step, cells, asked, own, one, two, three, scale, total, masses, *rest):
    message, total_out, masses_out, contrib = rest[-4:]
    owned = own.shape[0]
    delta = own[...] + one[...] + two[...] + three[...]
    total_out[...] = total[...] + delta
    contrib[...] = delta * scale[...]
    mass = jnp.sum(jnp.sum(jnp.abs(delta), axis=0), axis=0, keepdims=True)
    rows = lax.broadcasted_iota(jnp.int32, (8, LANES), 0)
    merged = jnp.where(rows == step, mass, masses[...])
    masses_out[...] = merged
    extra = None
    if step == ITERS - 1:
        sums = jnp.broadcast_to(jnp.sum(merged, axis=1, keepdims=True) / cells, (8, LANES))
        extra = jnp.concatenate([*pieces(lane_row(sums)), jnp.zeros((1, LANES), jnp.float32)], axis=0)
    send(asked, owned, contrib, message, extra)


def product(vectors, rows, j, live, weight, contracted):
    wide = jnp.concatenate(
        [jnp.broadcast_to(vectors[j, r : r + 1, :], (8, LANES)) for r in range(4)], axis=1
    )
    found = lax.dot_general(
        (wide * live).astype(jnp.bfloat16),
        weight,
        (((1,), (contracted,)), ((), ())),
        preferred_element_type=jnp.float32,
    )
    block = found[:, 3 * LANES :]
    for r in (2, 1, 0):
        block = jnp.where(rows == r, found[:, LANES * r : LANES * (r + 1)], block)
    return block[:4]


def start_tile_kernel(turn, table, picked, weight_hbm, own, one, two, three, weight, turned, vectors, sums, sems):
    owned = tiles = picked.shape[0]

    def fetch(j):
        return pltpu.make_async_copy(weight_hbm.at[j], weight.at[j], sems.at[j])

    for j in range(tiles):
        fetch(j).start()
    sums[...] = jnp.zeros_like(sums)
    vectors[...] = picked[...].astype(jnp.float32)
    rows = lax.broadcasted_iota(jnp.int32, (8, LANES), 0)

    def group(turning, g, carry):
        found = []
        for u in range(FIRST_GROUP):
            j = g * FIRST_GROUP + u
            fetch(j).wait()
            tile = weight[j]
            if turning:
                turned[j] = tile.T
            live = table[3 * tiles + j].astype(jnp.float32)
            found.append((j, product(vectors, rows, j, live, tile, 1)))
        for j, block in found:
            q = table[tiles + j]
            sums[q] = sums[q] + block
        return carry

    lax.fori_loop(0, turn // FIRST_GROUP, functools.partial(group, True), 0)
    lax.fori_loop(turn // FIRST_GROUP, tiles // FIRST_GROUP, functools.partial(group, False), 0)
    for s, out in enumerate((own, one, two, three)):
        out[...] = sums[s * owned : (s + 1) * owned]


def tile_kernel(last, table, picked, turned, own, one, two, three, vectors, sums):
    owned = tiles = picked.shape[0]
    count = table[2 * tiles]
    sums[...] = jnp.zeros_like(sums)
    vectors[...] = picked[...].astype(jnp.float32)
    rows = lax.broadcasted_iota(jnp.int32, (8, LANES), 0)

    def group(g, carry):
        found = []
        for u in range(GROUP):
            i = g * GROUP + u
            j = table[i]
            live = jnp.where(i < count, 1.0, 0.0)
            found.append((j, product(vectors, rows, j, live, turned[j], 0)))
        for j, block in found:
            q = table[tiles + j]
            sums[q] = sums[q] + block
        return carry

    lax.fori_loop(0, (count + GROUP - 1) // GROUP, group, 0)
    for s, out in enumerate((own, one, two, three)):
        out[0:owned] = sums[s * owned : (s + 1) * owned]
    if last:
        mass = jnp.zeros((1, LANES), jnp.float32)
        for r in (4, 5, 6):
            mass = mass + jnp.sum(vectors[:, r, :], axis=0, keepdims=True)
        for out in (own, one, two, three):
            out[owned] = jnp.broadcast_to(mass, (4, LANES))


def last_kernel(me, own, one, two, three, total, rank_out, delta_out, masses, ordered):
    owned = total.shape[0]
    for r in range(4):
        part = slice(LANES * r, LANES * (r + 1))
        rank_out[:, part] = total[:, r, :]
        delta_out[:, part] = (
            own[0:owned, r, :] + one[0:owned, r, :] + two[0:owned, r, :] + three[0:owned, r, :]
        )
    for s, part in enumerate((own, one, two, three)):
        ordered[lax.rem(me[0] + 4 - s, 4)] = part[owned]
    masses[...] = (ordered[0] + ordered[1] + ordered[2] + ordered[3])[0:1]


def f32(*shape):
    return jax.ShapeDtypeStruct(shape, jnp.float32)


def s32(*shape):
    return jax.ShapeDtypeStruct(shape, jnp.int32)


def call(kernel, outs, specs_in, specs_out, scratch, vmem=4, cost=None):
    return pl.pallas_call(
        kernel,
        out_shape=outs,
        in_specs=specs_in,
        out_specs=specs_out,
        scratch_shapes=scratch,
        cost_estimate=cost,
        compiler_params=pltpu.CompilerParams(vmem_limit_bytes=vmem << 20),
    )


def on_device(rank_in, delta_in, out_degree, tile_weight, tile_source, tile_row, tile_valid):
    owned, width = delta_in.shape
    tiles = tile_row.shape[0]
    n_group = lax.axis_size(BLK)
    n_column = lax.axis_size("col")
    cells = owned * n_group * n_column * width
    me = lax.axis_index("col").astype(jnp.int32).reshape(1)
    asked = lax.all_to_all(
        tile_source.reshape(n_group, 1, 1), BLK, split_axis=0, concat_axis=0, tiled=True
    )
    held = f32(owned, 4, LANES)
    message = jax.ShapeDtypeStruct((n_group, 8, LANES), jnp.bfloat16)
    block_scratch = pltpu.VMEM((owned, 4, LANES), jnp.float32)
    table, scale, total, masses, contrib = call(
        functools.partial(stage_kernel, n_column),
        (s32(4 * tiles), held, held, f32(8, LANES), held),
        [SMEM] + [HBM] * 5,
        (SMEM,) + (VMEM,) * 4,
        [
            pltpu.VMEM((owned, width), jnp.float32),
            pltpu.VMEM((owned, width), jnp.float32),
            pltpu.VMEM((owned, width), jnp.int32),
            pltpu.SMEM((tiles,), jnp.int32),
            pltpu.SMEM((tiles,), jnp.int32),
            pltpu.SemaphoreType.DMA((5,)),
        ],
    )(me, *(pltpu.with_memory_space_constraint(x, pltpu.HBM) for x in (delta_in, rank_in, out_degree, tile_row, tile_valid)))
    out = call(
        first_kernel,
        message,
        [SMEM, VMEM],
        VMEM,
        [],
    )(asked, contrib)
    keep = functools.partial(pltpu.with_memory_space_constraint, memory_space=pltpu.VMEM)
    resident = pltpu.VMEM(tile_weight.shape, tile_weight.dtype)
    tile_scratch = [
        pltpu.VMEM((tiles, 8, LANES), jnp.float32),
        pltpu.VMEM((n_column * owned, 4, LANES), jnp.float32),
    ]
    for step in range(ITERS):
        picked = lax.all_to_all(out, BLK, split_axis=0, concat_axis=0, tiled=True)
        last = step == ITERS - 1
        marks = []
        if step == 0:
            *parts, weight, turned = call(
                functools.partial(start_tile_kernel, EARLY),
                (held,) * 4 + (resident,) * 2,
                [SMEM, VMEM, HBM],
                (VMEM,) * 6,
                tile_scratch + [pltpu.SemaphoreType.DMA((tiles,))],
            )(table, picked, pltpu.with_memory_space_constraint(tile_weight, pltpu.HBM))
            turned, mark = pl.pallas_call(
                functools.partial(turn_kernel, EARLY, tiles),
                out_shape=(resident, f32(8, LANES)),
                in_specs=[VMEM] * 3,
                out_specs=(VMEM, VMEM),
                input_output_aliases={2: 0},
                cost_estimate=pl.CostEstimate(flops=0, transcendentals=0, bytes_accessed=12 << 20),
                compiler_params=pltpu.CompilerParams(vmem_limit_bytes=4 << 20),
            )(keep(weight), parts[0], keep(turned))
            marks = [mark]
        else:
            parts = call(
                functools.partial(tile_kernel, last),
                (f32(owned + last, 4, LANES),) * 4,
                [SMEM, VMEM, VMEM],
                (VMEM,) * 4,
                tile_scratch,
            )(table, picked, keep(turned))
        own, others = parts[0], parts[1:]
        others = [
            lax.ppermute(part, "col", [(i, (i + s + 1) % n_column) for i in range(n_column)])
            for s, part in enumerate(others)
        ]
        if not last:
            out, total, masses = call(
                functools.partial(join_kernel, step + 1, cells),
                (message, held, f32(8, LANES)),
                [SMEM] + [VMEM] * (7 + len(marks)),
                (VMEM,) * 3,
                [block_scratch],
            )(asked, own, *others, scale, total, masses, *marks)
    rank_out, delta_out, stacked = call(
        last_kernel,
        (f32(owned, width), f32(owned, width), f32(1, LANES)),
        [SMEM] + [VMEM] * 5,
        (VMEM,) * 3,
        [pltpu.VMEM((4, 4, LANES), jnp.float32)],
    )(me, own, *others, total)
    return rank_out, delta_out, stacked[0, :ITERS]


def solution(mesh):
    finer = Mesh(
        mesh.devices.reshape(4, 4, 2, mesh.shape["col"]), ("blk_0", "blk_1", "blk_2", "col")
    )
    placed = (
        P(BLK_COL, None),
        P(BLK_COL, None),
        P(BLK_COL, None),
        P(BLK_COL, None, None),
        P(BLK_COL),
        P(BLK_COL),
        P(BLK_COL),
    )
    return jax.shard_map(
        on_device,
        mesh=finer,
        in_specs=placed,
        out_specs=(P(BLK_COL, None), P(BLK_COL, None), P()),
        check_vma=False,
    )
```

time: 183 us -> 165 us (0.902)
  local copies, waits for them, and re-layouts: 10.8 us -> 1.85 us
  waiting for transfers between devices: 29.6 us -> 24.6 us
  blocking collectives: 68.1 us -> 65.1 us
    all_to_all x1 -> x0, blocking collectives: 15.6 us -> none  [on_device(): lax.all_to_all(tile_source.reshape(n_group, 1), BLK, split_axis=0, concat...]
    all_to_all x5 -> x6, blocking collectives: 52.6 us -> 65.1 us  [on_device(): picked = lax.all_to_all(out, BLK, split_axis=0, concat_axis=0, tiled=True)]
    unnamed x14 -> x0, local copies, waits for them, and re-layouts: 9.6 us -> none
    ppermute x18, waiting for transfers between devices: 25.4 us -> 19.6 us  [on_device(): lax.ppermute(part, 'col', [(i, (i + s + 1) % n_column) for i in range(n_c...]
    all_to_all x1, starting transfers between devices: 3.86 us -> 8.41 us  [on_device(): lax.all_to_all(tile_source.reshape(n_group, 1, 1), BLK, split_axis=0, con...]
    ppermute x18, starting transfers between devices: 31.1 us -> 27 us  [on_device(): lax.ppermute(part, 'col', [(i, (i + s + 1) % n_column) for i in range(n_c...]
    pallas_call x8 -> x9, Pallas kernels: 32.7 us -> 30.5 us  [the longest x5 15.3 us: on_device(): call(functools.partial(tile_kernel, last), (f32(owned + last, 4, LANES),)...]
  transfers between devices with their start and end apart: 19 -> 19, of which waited for: 19 -> 17; matrix products, arithmetic and copies ran while one was open for 0% -> 0% of each run, Pallas kernels for 1% -> 3%
where the time goes in v2:
time: 165 us; the launch traced here: 164 us
  blocking collectives  65.1 us (39%)
  Pallas kernels  36.6 us (22%)
  starting transfers between devices  35.4 us (21%)
  waiting for transfers between devices  24.6 us (15%)
  local copies, waits for them, and re-layouts  1.85 us (1%)
    all_to_all x6, blocking collectives, on_device(): picked = lax.all_to_all(out, BLK, split_axis=0, concat_axis=0, tiled=True)  65.1 us
    ppermute x18, starting transfers between devices, on_device(): lax.ppermute(part, 'col', [(i, (i + s + 1) % n_column) for i in range(n_c...  27 us
    ppermute x18, waiting for transfers between devices, on_device(): lax.ppermute(part, 'col', [(i, (i + s + 1) % n_column) for i in range(n_c...  19.6 us
    pallas_call x5, Pallas kernels, on_device(): call(functools.partial(tile_kernel, last), (f32(owned + last, 4, LANES),)...  15.3 us
    pallas_call x1, Pallas kernels, on_device(): call(functools.partial(start_tile_kernel, EARLY), (held,) * 4 + (resident...  10 us
    all_to_all x1, starting transfers between devices, on_device(): lax.all_to_all(tile_source.reshape(n_group, 1, 1), BLK, split_axis=0, con...  8.41 us
    pallas_call x5, Pallas kernels, on_device(): call(functools.partial(join_kernel, step + 1, cells), (message, held, f32...  5.27 us
    all_to_all x1, waiting for transfers between devices, on_device(): lax.all_to_all(tile_source.reshape(n_group, 1, 1), BLK, split_axis=0, con...  4.96 us
  transfers between devices with their start and end apart: 19, of which 17 were waited for; matrix products, arithmetic and copies ran while one was open for 0% of the time, Pallas kernels for 3%

profile of v2, /device:TPU:0, one launch (start us, length us, event | category | flops | bytes accessed | tf_op | source)
XLA Modules:
  0.0 164.3 jit_solution(4282348939508512571)
XLA Ops:
  0.6 1.3 copy.11
  2.0 8.4 %all-to-all-start = ((s32[32,1,1]{2,1,0:T(1,128)}), s32[32,1,1]{2,1,0:T(1,128)S(1)}, u32[]{:S(2)}, u32[]{:S(2)}) async-start(s32[32,1,1]{2,1,0:T(1,128)} %copy.11), calls=%async_computation | async-start | bytes 32768 | tf_op jit(solution)/shard_map/all_to_all | solution.py:261
  10.4 2.3 %shard_map.94 = (s32[128]{0:T(128)S(1)}, f32[32,4,128]{2,1,0:T(4,128)S(1)}, f32[32,4,128]{2,1,0:T(4,128)S(1)}, f32[8,128]{1,0:T(8,128)S(1)}, f32[32,4,128]{2,1,0:T(4,128)S(1)}) custom-call(s32[1]{0:T(128)} %bitcast.refs_0_.me, f32[32,512]{1,0:T(8,128)} %refs_1_.1, f32[32,512]{1,0:T(8,128)} %refs_2_.1, s32[32,512]{1,0:T(8,128)} %refs_3_.1, s32[32]{0:T(128)} %refs_4_.1, ...), custom_call_target="tpu_custom_call" | custom-call | tf_op jit(solution)/shard_map/pallas_call | solution.py:267
  12.7 5.0 %all-to-all-done.asked = s32[32,1,1]{2,1,0:T(1,128)S(1)} async-done(((s32[32,1,1]{2,1,0:T(1,128)}), s32[32,1,1]{2,1,0:T(1,128)S(1)}, u32[]{:S(2)}, u32[]{:S(2)}) %all-to-all-start) | async-done | bytes 160 | tf_op jit(solution)/shard_map/all_to_all | solution.py:261
  17.7 0.9 shard_map.95
  18.6 10.8 %all_to_all.35.picked = bf16[32,8,128]{2,1,0:T(8,128)(2,1)S(1)} all-to-all(bf16[32,8,128]{2,1,0:T(8,128)(2,1)S(1)} %shard_map.95), channel_id=1, replica_groups=mesh['blk_0'=4,'blk_1'=4,'blk_2'=2,'col'=4] {'blk_0','blk_1','blk_2'}, dimensions={0} | all-to-all | bytes 131072 | tf_op jit(solution)/shard_map/all_to_all | solution.py:295
  29.3 10.0 %shard_map.96 = (f32[32,4,128]{2,1,0:T(4,128)S(1)}, f32[32,4,128]{2,1,0:T(4,128)S(1)}, f32[32,4,128]{2,1,0:T(4,128)S(1)}, f32[32,4,128]{2,1,0:T(4,128)S(1)}, bf1...) custom-call(s32[128]{0:T(128)S(1)} %get-tuple-element.53.table, ...), custom_call_target="tpu_custom_call" | custom-call | tf_op jit(solution)/shard_map/pallas_call | solution.py:299
  39.4 1.6 collective-permute-start
  40.9 2.7 %collective-permute-start.1 = (f32[32,4,128]{2,1,0:T(4,128)S(1)}, f32[32,4,128]{2,1,0:T(4,128)S(1)}, u32[]{:S(2)}, u32[]{:S(2)}) collective-permute-start(f32[32,4,128]{2,1,0:T(4,128)S(1)} %get-tuple-element.57), channel_id=1, source_target_pairs={{0,2},{1,3},{2,0},{3,1},{4,6},{5,7},{6,4},{7,5},{8,10},{9,11},{10,... | collective-permute-start | bytes 196616 | tf_op jit(solution)/shard_map/ppermute | solution.py:326
  43.7 1.4 collective-permute-start.2
  45.1 1.9 %shard_map.97 = (bf16[32,512,512]{2,1,0:T(8,128)(2,1)S(1)}, f32[8,128]{1,0:T(8,128)S(1)}) custom-call(bf16[32,512,512]{2,1,0:T(8,128)(2,1)S(1)} %get-tuple-element.62.refs_0_, f32[32,4,128]{2,1,0:T(4,128)S(1)} %get-tuple-element.55.refs_1_.own, bf16[32,512,512]{2,1,0:T(8,128)(2,1)S(1)} %get-tuple-element.63.refs_2_), custom_call_target="tpu_custom_call", output_to_operand_aliasing={{0}: (2, {})} | custom-call | bytes 12582912 | tf_op jit(solution)/shard_map/pallas_call | solution.py:306
  47.1 0.0 collective-permute-done.one
  47.1 0.1 collective-permute-done.1.two
  47.2 0.8 collective-permute-done.2.three
  47.9 0.9 shard_map.98
  48.9 10.9 %all_to_all.36.picked = bf16[32,8,128]{2,1,0:T(8,128)(2,1)S(1)} all-to-all(bf16[32,8,128]{2,1,0:T(8,128)(2,1)S(1)} %get-tuple-element.65), channel_id=1, replica_groups=mesh['blk_0'=4,'blk_1'=4,'blk_2'=2,'col'=4] {'blk_0','blk_1','blk_2'}, dimensions={0} | all-to-all | bytes 131072 | tf_op jit(solution)/shard_map/all_to_all | solution.py:295
  59.7 3.0 %shard_map.99 = (f32[32,4,128]{2,1,0:T(4,128)S(1)}, f32[32,4,128]{2,1,0:T(4,128)S(1)}, f32[32,4,128]{2,1,0:T(4,128)S(1)}, f32[32,4,128]{2,1,0:T(4,128)S(1)}) custom-call(s32[128]{0:T(128)S(1)} %get-tuple-element.53.table, bf16[32,8,128]{2,1,0:T(8,128)(2,1)S(1)} %all_to_all.36.picked, bf16[32,512,512]{2,1,0:T(8,128)(2,1)S(1)} %get-tuple-element.66.turned), custom_call_target="tpu_custom_call" | custom-call | tf_op jit(solution)/shard_map/pallas_call | solution.py:317
  62.8 0.6 collective-permute-start.3
  63.4 3.5 %collective-permute-start.4 = (f32[32,4,128]{2,1,0:T(4,128)S(1)}, f32[32,4,128]{2,1,0:T(4,128)S(1)}, u32[]{:S(2)}, u32[]{:S(2)}) collective-permute-start(f32[32,4,128]{2,1,0:T(4,128)S(1)} %get-tuple-element.69), channel_id=1, source_target_pairs={{0,2},{1,3},{2,0},{3,1},{4,6},{5,7},{6,4},{7,5},{8,10},{9,11},{10,... | collective-permute-start | bytes 196616 | tf_op jit(solution)/shard_map/ppermute | solution.py:326
  66.9 0.3 collective-permute-start.5
  67.2 1.1 collective-permute-done.3.one
  68.3 2.1 %collective-permute-done.4.two = f32[32,4,128]{2,1,0:T(4,128)S(1)} collective-permute-done((f32[32,4,128]{2,1,0:T(4,128)S(1)}, f32[32,4,128]{2,1,0:T(4,128)S(1)}, u32[]{:S(2)}, u32[]{:S(2)}) %collective-permute-start.4) | collective-permute-done | bytes 65568 | tf_op jit(solution)/shard_map/ppermute | solution.py:326
  70.4 0.8 collective-permute-done.5.three
  71.2 0.9 shard_map.100
  72.1 10.9 %all_to_all.37.picked = bf16[32,8,128]{2,1,0:T(8,128)(2,1)S(1)} all-to-all(bf16[32,8,128]{2,1,0:T(8,128)(2,1)S(1)} %get-tuple-element.73), channel_id=1, replica_groups=mesh['blk_0'=4,'blk_1'=4,'blk_2'=2,'col'=4] {'blk_0','blk_1','blk_2'}, dimensions={0} | all-to-all | bytes 131072 | tf_op jit(solution)/shard_map/all_to_all | solution.py:295
  83.0 3.0 %shard_map.101 = (f32[32,4,128]{2,1,0:T(4,128)S(1)}, f32[32,4,128]{2,1,0:T(4,128)S(1)}, f32[32,4,128]{2,1,0:T(4,128)S(1)}, f32[32,4,128]{2,1,0:T(4,128)S(1)}) custom-call(s32[128]{0:T(128)S(1)} %get-tuple-element.53.table, bf16[32,8,128]{2,1,0:T(8,128)(2,1)S(1)} %all_to_all.37.picked, bf16[32,512,512]{2,1,0:T(8,128)(2,1)S(1)} %get-tuple-element.66.turned), custom_call_target="tpu_custom_call" | custom-call | tf_op jit(solution)/shard_map/pallas_call | solution.py:317
  86.0 0.1 collective-permute-start.6
  86.1 3.2 %collective-permute-start.7 = (f32[32,4,128]{2,1,0:T(4,128)S(1)}, f32[32,4,128]{2,1,0:T(4,128)S(1)}, u32[]{:S(2)}, u32[]{:S(2)}) collective-permute-start(f32[32,4,128]{2,1,0:T(4,128)S(1)} %get-tuple-element.76), channel_id=1, source_target_pairs={{0,2},{1,3},{2,0},{3,1},{4,6},{5,7},{6,4},{7,5},{8,10},{9,11},{10,... | collective-permute-start | bytes 196616 | tf_op jit(solution)/shard_map/ppermute | solution.py:326
  89.3 1.0 collective-permute-start.8
  90.2 2.6 %collective-permute-done.6.one = f32[32,4,128]{2,1,0:T(4,128)S(1)} collective-permute-done((f32[32,4,128]{2,1,0:T(4,128)S(1)}, f32[32,4,128]{2,1,0:T(4,128)S(1)}, u32[]{:S(2)}, u32[]{:S(2)}) %collective-permute-start.6) | collective-permute-done | bytes 65568 | tf_op jit(solution)/shard_map/ppermute | solution.py:326
  92.8 0.0 collective-permute-done.7.two
  92.8 0.7 collective-permute-done.8.three
  93.5 0.9 shard_map.102
  94.5 10.9 %all_to_all.38.picked = bf16[32,8,128]{2,1,0:T(8,128)(2,1)S(1)} all-to-all(bf16[32,8,128]{2,1,0:T(8,128)(2,1)S(1)} %get-tuple-element.80), channel_id=1, replica_groups=mesh['blk_0'=4,'blk_1'=4,'blk_2'=2,'col'=4] {'blk_0','blk_1','blk_2'}, dimensions={0} | all-to-all | bytes 131072 | tf_op jit(solution)/shard_map/all_to_all | solution.py:295
  105.4 3.0 %shard_map.103 = (f32[32,4,128]{2,1,0:T(4,128)S(1)}, f32[32,4,128]{2,1,0:T(4,128)S(1)}, f32[32,4,128]{2,1,0:T(4,128)S(1)}, f32[32,4,128]{2,1,0:T(4,128)S(1)}) custom-call(s32[128]{0:T(128)S(1)} %get-tuple-element.53.table, bf16[32,8,128]{2,1,0:T(8,128)(2,1)S(1)} %all_to_all.38.picked, bf16[32,512,512]{2,1,0:T(8,128)(2,1)S(1)} %get-tuple-element.66.turned), custom_call_target="tpu_custom_call" | custom-call | tf_op jit(solution)/shard_map/pallas_call | solution.py:317
  108.4 1.0 collective-permute-start.9
  109.4 3.0 %collective-permute-start.10 = (f32[32,4,128]{2,1,0:T(4,128)S(1)}, f32[32,4,128]{2,1,0:T(4,128)S(1)}, u32[]{:S(2)}, u32[]{:S(2)}) collective-permute-start(f32[32,4,128]{2,1,0:T(4,128)S(1)} %get-tuple-element.83), channel_id=1, source_target_pairs={{0,2},{1,3},{2,0},{3,1},{4,6},{5,7},{6,4},{7,5},{8,10},{9,11},{10,... | collective-permute-start | bytes 196616 | tf_op jit(solution)/shard_map/ppermute | solution.py:326
  112.4 0.2 collective-permute-start.11
  112.6 1.6 collective-permute-done.9.one
  114.2 1.7 %collective-permute-done.10.two = f32[32,4,128]{2,1,0:T(4,128)S(1)} collective-permute-done((f32[32,4,128]{2,1,0:T(4,128)S(1)}, f32[32,4,128]{2,1,0:T(4,128)S(1)}, u32[]{:S(2)}, u32[]{:S(2)}) %collective-permute-start.10) | collective-permute-done | bytes 65568 | tf_op jit(solution)/shard_map/ppermute | solution.py:326
  115.9 0.8 collective-permute-done.11.three
  116.7 0.9 shard_map.104
  117.6 10.9 %all_to_all.39.picked = bf16[32,8,128]{2,1,0:T(8,128)(2,1)S(1)} all-to-all(bf16[32,8,128]{2,1,0:T(8,128)(2,1)S(1)} %get-tuple-element.87), channel_id=1, replica_groups=mesh['blk_0'=4,'blk_1'=4,'blk_2'=2,'col'=4] {'blk_0','blk_1','blk_2'}, dimensions={0} | all-to-all | bytes 131072 | tf_op jit(solution)/shard_map/all_to_all | solution.py:295
  128.5 3.2 %shard_map.105 = (f32[32,4,128]{2,1,0:T(4,128)S(1)}, f32[32,4,128]{2,1,0:T(4,128)S(1)}, f32[32,4,128]{2,1,0:T(4,128)S(1)}, f32[32,4,128]{2,1,0:T(4,128)S(1)}) custom-call(s32[128]{0:T(128)S(1)} %get-tuple-element.53.table, bf16[32,8,128]{2,1,0:T(8,128)(2,1)S(1)} %all_to_all.39.picked, bf16[32,512,512]{2,1,0:T(8,128)(2,1)S(1)} %get-tuple-element.66.turned), custom_call_target="tpu_custom_call" | custom-call | tf_op jit(solution)/shard_map/pallas_call | solution.py:317
  131.7 0.2 collective-permute-start.12
  131.9 3.1 %collective-permute-start.13 = (f32[32,4,128]{2,1,0:T(4,128)S(1)}, f32[32,4,128]{2,1,0:T(4,128)S(1)}, u32[]{:S(2)}, u32[]{:S(2)}) collective-permute-start(f32[32,4,128]{2,1,0:T(4,128)S(1)} %get-tuple-element.90), channel_id=1, source_target_pairs={{0,2},{1,3},{2,0},{3,1},{4,6},{5,7},{6,4},{7,5},{8,10},{9,11},{10,... | collective-permute-start | bytes 196616 | tf_op jit(solution)/shard_map/ppermute | solution.py:326
  135.0 0.9 collective-permute-start.14
  135.9 1.9 %collective-permute-done.12.one = f32[32,4,128]{2,1,0:T(4,128)S(1)} collective-permute-done((f32[32,4,128]{2,1,0:T(4,128)S(1)}, f32[32,4,128]{2,1,0:T(4,128)S(1)}, u32[]{:S(2)}, u32[]{:S(2)}) %collective-permute-start.12) | collective-permute-done | bytes 65568 | tf_op jit(solution)/shard_map/ppermute | solution.py:326
  137.8 0.7 collective-permute-done.13.two
  138.5 0.8 collective-permute-done.14.three
  139.3 1.6 shard_map.106
  140.8 10.9 %all_to_all.40.picked = bf16[32,8,128]{2,1,0:T(8,128)(2,1)S(1)} all-to-all(bf16[32,8,128]{2,1,0:T(8,128)(2,1)S(1)} %get-tuple-element.94), channel_id=1, replica_groups=mesh['blk_0'=4,'blk_1'=4,'blk_2'=2,'col'=4] {'blk_0','blk_1','blk_2'}, dimensions={0} | all-to-all | bytes 131072 | tf_op jit(solution)/shard_map/all_to_all | solution.py:295
  151.7 3.1 %shard_map.107 = (f32[33,4,128]{2,1,0:T(4,128)S(1)}, f32[33,4,128]{2,1,0:T(4,128)S(1)}, f32[33,4,128]{2,1,0:T(4,128)S(1)}, f32[33,4,128]{2,1,0:T(4,128)S(1)}) custom-call(s32[128]{0:T(128)S(1)} %get-tuple-element.53.table, bf16[32,8,128]{2,1,0:T(8,128)(2,1)S(1)} %all_to_all.40.picked, bf16[32,512,512]{2,1,0:T(8,128)(2,1)S(1)} %get-tuple-element.66.turned), custom_call_target="tpu_custom_call" | custom-call | tf_op jit(solution)/shard_map/pallas_call | solution.py:317
  154.8 0.9 collective-permute-start.15
  155.7 3.0 %collective-permute-start.16 = (f32[33,4,128]{2,1,0:T(4,128)S(1)}, f32[33,4,128]{2,1,0:T(4,128)S(1)}, u32[]{:S(2)}, u32[]{:S(2)}) collective-permute-start(f32[33,4,128]{2,1,0:T(4,128)S(1)} %get-tuple-element.97), channel_id=1, source_target_pairs={{0,2},{1,3},{2,0},{3,1},{4,6},{5,7},{6,4},{7,5},{8,10},{9,11},{10,... | collective-permute-start | bytes 202760 | tf_op jit(solution)/shard_map/ppermute | solution.py:326
  158.7 0.3 collective-permute-start.17
  159.0 1.7 %collective-permute-done.15.one = f32[33,4,128]{2,1,0:T(4,128)S(1)} collective-permute-done((f32[33,4,128]{2,1,0:T(4,128)S(1)}, f32[33,4,128]{2,1,0:T(4,128)S(1)}, u32[]{:S(2)}, u32[]{:S(2)}) %collective-permute-start.15) | collective-permute-done | bytes 67616 | tf_op jit(solution)/shard_map/ppermute | solution.py:326
  160.7 1.6 collective-permute-done.16.two
  162.2 0.7 collective-permute-done.17.three
  163.0 0.8 shard_map.108
  163.8 0.5 slice_bitcast_fusion
Async XLA Ops:
  2.0 15.7 %all-to-all-start = ((s32[32,1,1]{2,1,0:T(1,128)}), s32[32,1,1]{2,1,0:T(1,128)S(1)}, u32[]{:S(2)}, u32[]{:S(2)}) async-start(s32[32,1,1]{2,1,0:T(1,128)} %copy.11), calls=%async_computation | async-start | bytes 32768 | tf_op jit(solution)/shard_map/all_to_all | solution.py:261
  39.4 7.7 %collective-permute-start = (f32[32,4,128]{2,1,0:T(4,128)S(1)}, f32[32,4,128]{2,1,0:T(4,128)S(1)}, u32[]{:S(2)}, u32[]{:S(2)}) collective-permute-start(f32[32,4,128]{2,1,0:T(4,128)S(1)} %get-tuple-element.56), channel_id=1, source_target_pairs={{0,1},{1,2},{2,3},{3,0},{4,5},{5,6},{6,7},{7,4},{8,9},{9,10},{10,1... | collective-permute-start | bytes 196616 | tf_op jit(solution)/shard_map/ppermute | solution.py:326
  40.9 6.2 %collective-permute-start.1 = (f32[32,4,128]{2,1,0:T(4,128)S(1)}, f32[32,4,128]{2,1,0:T(4,128)S(1)}, u32[]{:S(2)}, u32[]{:S(2)}) collective-permute-start(f32[32,4,128]{2,1,0:T(4,128)S(1)} %get-tuple-element.57), channel_id=1, source_target_pairs={{0,2},{1,3},{2,0},{3,1},{4,6},{5,7},{6,4},{7,5},{8,10},{9,11},{10,... | collective-permute-start | bytes 196616 | tf_op jit(solution)/shard_map/ppermute | solution.py:326
  43.7 4.3 %collective-permute-start.2 = (f32[32,4,128]{2,1,0:T(4,128)S(1)}, f32[32,4,128]{2,1,0:T(4,128)S(1)}, u32[]{:S(2)}, u32[]{:S(2)}) collective-permute-start(f32[32,4,128]{2,1,0:T(4,128)S(1)} %get-tuple-element.58), channel_id=1, source_target_pairs={{0,3},{1,0},{2,1},{3,2},{4,7},{5,4},{6,5},{7,6},{8,11},{9,8},{10,9... | collective-permute-start | bytes 196616 | tf_op jit(solution)/shard_map/ppermute | solution.py:326
  62.8 5.5 %collective-permute-start.3 = (f32[32,4,128]{2,1,0:T(4,128)S(1)}, f32[32,4,128]{2,1,0:T(4,128)S(1)}, u32[]{:S(2)}, u32[]{:S(2)}) collective-permute-start(f32[32,4,128]{2,1,0:T(4,128)S(1)} %get-tuple-element.68), channel_id=1, source_target_pairs={{0,1},{1,2},{2,3},{3,0},{4,5},{5,6},{6,7},{7,4},{8,9},{9,10},{10,1... | collective-permute-start | bytes 196616 | tf_op jit(solution)/shard_map/ppermute | solution.py:326
  63.4 7.0 %collective-permute-start.4 = (f32[32,4,128]{2,1,0:T(4,128)S(1)}, f32[32,4,128]{2,1,0:T(4,128)S(1)}, u32[]{:S(2)}, u32[]{:S(2)}) collective-permute-start(f32[32,4,128]{2,1,0:T(4,128)S(1)} %get-tuple-element.69), channel_id=1, source_target_pairs={{0,2},{1,3},{2,0},{3,1},{4,6},{5,7},{6,4},{7,5},{8,10},{9,11},{10,... | collective-permute-start | bytes 196616 | tf_op jit(solution)/shard_map/ppermute | solution.py:326
  66.9 4.3 %collective-permute-start.5 = (f32[32,4,128]{2,1,0:T(4,128)S(1)}, f32[32,4,128]{2,1,0:T(4,128)S(1)}, u32[]{:S(2)}, u32[]{:S(2)}) collective-permute-start(f32[32,4,128]{2,1,0:T(4,128)S(1)} %get-tuple-element.70), channel_id=1, source_target_pairs={{0,3},{1,0},{2,1},{3,2},{4,7},{5,4},{6,5},{7,6},{8,11},{9,8},{10,9... | collective-permute-start | bytes 196616 | tf_op jit(solution)/shard_map/ppermute | solution.py:326
  86.0 6.8 %collective-permute-start.6 = (f32[32,4,128]{2,1,0:T(4,128)S(1)}, f32[32,4,128]{2,1,0:T(4,128)S(1)}, u32[]{:S(2)}, u32[]{:S(2)}) collective-permute-start(f32[32,4,128]{2,1,0:T(4,128)S(1)} %get-tuple-element.75), channel_id=1, source_target_pairs={{0,1},{1,2},{2,3},{3,0},{4,5},{5,6},{6,7},{7,4},{8,9},{9,10},{10,1... | collective-permute-start | bytes 196616 | tf_op jit(solution)/shard_map/ppermute | solution.py:326
  86.1 6.7 %collective-permute-start.7 = (f32[32,4,128]{2,1,0:T(4,128)S(1)}, f32[32,4,128]{2,1,0:T(4,128)S(1)}, u32[]{:S(2)}, u32[]{:S(2)}) collective-permute-start(f32[32,4,128]{2,1,0:T(4,128)S(1)} %get-tuple-element.76), channel_id=1, source_target_pairs={{0,2},{1,3},{2,0},{3,1},{4,6},{5,7},{6,4},{7,5},{8,10},{9,11},{10,... | collective-permute-start | bytes 196616 | tf_op jit(solution)/shard_map/ppermute | solution.py:326
  89.3 4.3 %collective-permute-start.8 = (f32[32,4,128]{2,1,0:T(4,128)S(1)}, f32[32,4,128]{2,1,0:T(4,128)S(1)}, u32[]{:S(2)}, u32[]{:S(2)}) collective-permute-start(f32[32,4,128]{2,1,0:T(4,128)S(1)} %get-tuple-element.77), channel_id=1, source_target_pairs={{0,3},{1,0},{2,1},{3,2},{4,7},{5,4},{6,5},{7,6},{8,11},{9,8},{10,9... | collective-permute-start | bytes 196616 | tf_op jit(solution)/shard_map/ppermute | solution.py:326
  108.4 5.8 %collective-permute-start.9 = (f32[32,4,128]{2,1,0:T(4,128)S(1)}, f32[32,4,128]{2,1,0:T(4,128)S(1)}, u32[]{:S(2)}, u32[]{:S(2)}) collective-permute-start(f32[32,4,128]{2,1,0:T(4,128)S(1)} %get-tuple-element.82), channel_id=1, source_target_pairs={{0,1},{1,2},{2,3},{3,0},{4,5},{5,6},{6,7},{7,4},{8,9},{9,10},{10,1... | collective-permute-start | bytes 196616 | tf_op jit(solution)/shard_map/ppermute | solution.py:326
  109.4 6.5 %collective-permute-start.10 = (f32[32,4,128]{2,1,0:T(4,128)S(1)}, f32[32,4,128]{2,1,0:T(4,128)S(1)}, u32[]{:S(2)}, u32[]{:S(2)}) collective-permute-start(f32[32,4,128]{2,1,0:T(4,128)S(1)} %get-tuple-element.83), channel_id=1, source_target_pairs={{0,2},{1,3},{2,0},{3,1},{4,6},{5,7},{6,4},{7,5},{8,10},{9,11},{10,... | collective-permute-start | bytes 196616 | tf_op jit(solution)/shard_map/ppermute | solution.py:326
  112.4 4.3 %collective-permute-start.11 = (f32[32,4,128]{2,1,0:T(4,128)S(1)}, f32[32,4,128]{2,1,0:T(4,128)S(1)}, u32[]{:S(2)}, u32[]{:S(2)}) collective-permute-start(f32[32,4,128]{2,1,0:T(4,128)S(1)} %get-tuple-element.84), channel_id=1, source_target_pairs={{0,3},{1,0},{2,1},{3,2},{4,7},{5,4},{6,5},{7,6},{8,11},{9,8},{10,9... | collective-permute-start | bytes 196616 | tf_op jit(solution)/shard_map/ppermute | solution.py:326
  131.7 6.1 %collective-permute-start.12 = (f32[32,4,128]{2,1,0:T(4,128)S(1)}, f32[32,4,128]{2,1,0:T(4,128)S(1)}, u32[]{:S(2)}, u32[]{:S(2)}) collective-permute-start(f32[32,4,128]{2,1,0:T(4,128)S(1)} %get-tuple-element.89), channel_id=1, source_target_pairs={{0,1},{1,2},{2,3},{3,0},{4,5},{5,6},{6,7},{7,4},{8,9},{9,10},{10,1... | collective-permute-start | bytes 196616 | tf_op jit(solution)/shard_map/ppermute | solution.py:326
  131.9 6.6 %collective-permute-start.13 = (f32[32,4,128]{2,1,0:T(4,128)S(1)}, f32[32,4,128]{2,1,0:T(4,128)S(1)}, u32[]{:S(2)}, u32[]{:S(2)}) collective-permute-start(f32[32,4,128]{2,1,0:T(4,128)S(1)} %get-tuple-element.90), channel_id=1, source_target_pairs={{0,2},{1,3},{2,0},{3,1},{4,6},{5,7},{6,4},{7,5},{8,10},{9,11},{10,... | collective-permute-start | bytes 196616 | tf_op jit(solution)/shard_map/ppermute | solution.py:326
  135.0 4.3 %collective-permute-start.14 = (f32[32,4,128]{2,1,0:T(4,128)S(1)}, f32[32,4,128]{2,1,0:T(4,128)S(1)}, u32[]{:S(2)}, u32[]{:S(2)}) collective-permute-start(f32[32,4,128]{2,1,0:T(4,128)S(1)} %get-tuple-element.91), channel_id=1, source_target_pairs={{0,3},{1,0},{2,1},{3,2},{4,7},{5,4},{6,5},{7,6},{8,11},{9,8},{10,9... | collective-permute-start | bytes 196616 | tf_op jit(solution)/shard_map/ppermute | solution.py:326
  154.8 5.9 %collective-permute-start.15 = (f32[33,4,128]{2,1,0:T(4,128)S(1)}, f32[33,4,128]{2,1,0:T(4,128)S(1)}, u32[]{:S(2)}, u32[]{:S(2)}) collective-permute-start(f32[33,4,128]{2,1,0:T(4,128)S(1)} %get-tuple-element.96), channel_id=1, source_target_pairs={{0,1},{1,2},{2,3},{3,0},{4,5},{5,6},{6,7},{7,4},{8,9},{9,10},{10,1... | collective-permute-start | bytes 202760 | tf_op jit(solution)/shard_map/ppermute | solution.py:326
  155.7 6.6 %collective-permute-start.16 = (f32[33,4,128]{2,1,0:T(4,128)S(1)}, f32[33,4,128]{2,1,0:T(4,128)S(1)}, u32[]{:S(2)}, u32[]{:S(2)}) collective-permute-start(f32[33,4,128]{2,1,0:T(4,128)S(1)} %get-tuple-element.97), channel_id=1, source_target_pairs={{0,2},{1,3},{2,0},{3,1},{4,6},{5,7},{6,4},{7,5},{8,10},{9,11},{10,... | collective-permute-start | bytes 202760 | tf_op jit(solution)/shard_map/ppermute | solution.py:326
  158.7 4.3 %collective-permute-start.17 = (f32[33,4,128]{2,1,0:T(4,128)S(1)}, f32[33,4,128]{2,1,0:T(4,128)S(1)}, u32[]{:S(2)}, u32[]{:S(2)}) collective-permute-start(f32[33,4,128]{2,1,0:T(4,128)S(1)} %get-tuple-element.98), channel_id=1, source_target_pairs={{0,3},{1,0},{2,1},{3,2},{4,7},{5,4},{6,5},{7,6},{8,11},{9,8},{10,9... | collective-permute-start | bytes 202760 | tf_op jit(solution)/shard_map/ppermute | solution.py:326

commit v3 on v1

v3 whole, which is shorter than its diff:
```python
import functools

import jax
import jax.numpy as jnp
from jax import lax
from jax.experimental import pallas as pl
from jax.experimental.pallas import tpu as pltpu
from jax.sharding import Mesh
from jax.sharding import PartitionSpec as P

ITERS = 6
BLK = ("blk_0", "blk_1", "blk_2")
BLK_COL = ("blk_0", "blk_1", "blk_2", "col")
LANES = 128
GROUP = 16
FIRST_GROUP = 4

damping = 0.85

VMEM = pl.BlockSpec(memory_space=pltpu.VMEM)
SMEM = pl.BlockSpec(memory_space=pltpu.SMEM)
HBM = pl.BlockSpec(memory_space=pltpu.HBM)


def lane_row(column):
    rows = lax.broadcasted_iota(jnp.int32, column.shape, 0)
    lanes = lax.broadcasted_iota(jnp.int32, column.shape, 1)
    return jnp.sum(jnp.where(rows == lanes, column, 0.0), axis=0, keepdims=True)


def pieces(value):
    high = value.astype(jnp.bfloat16).astype(jnp.float32)
    rest = value - high
    middle = rest.astype(jnp.bfloat16).astype(jnp.float32)
    low = (rest - middle).astype(jnp.bfloat16).astype(jnp.float32)
    return high, middle, low


def targets(cols, c, row, valid, table):
    tiles = row.shape[0]
    owned = tiles

    def target(i, carry):
        block = lax.rem(row[i] // owned + cols - c, cols) * owned + lax.rem(row[i], owned)
        table[i] = jnp.where(valid[i] != 0, block, cols * owned)
        return carry

    lax.fori_loop(0, tiles, target, 0)


def started(pairs, sems):
    copies = [pltpu.make_async_copy(*pair, sems.at[i]) for i, pair in enumerate(pairs)]
    for copy in copies:
        copy.start()
    return copies


def send(asked, contrib, message, extra):
    for b in range(message.shape[0]):
        block = contrib[asked[0, b]]
        if extra is None:
            message[b, 0:4, :] = block.astype(jnp.bfloat16)
        else:
            message[b] = jnp.concatenate([block, extra], axis=0).astype(jnp.bfloat16)


def first_kernel(source_hbm, delta_hbm, degree_hbm, message, source, delta, degree, contrib, sems):
    owned = delta.shape[0]
    for copy in started(((source_hbm, source), (delta_hbm, delta), (degree_hbm, degree)), sems):
        copy.wait()
    for r in range(4):
        part = slice(LANES * r, LANES * (r + 1))
        contrib[:, r, :] = delta[:, part] * (damping / degree[:, part].astype(jnp.float32))
    blocks = contrib[...].astype(jnp.bfloat16)
    for b in range(message.shape[0]):
        message[b, 0:owned] = blocks
        request = lax.rem(source[b], owned).astype(jnp.float32)
        message[b, owned] = jnp.full((4, LANES), request, jnp.float32).astype(jnp.bfloat16)


def window_kernel(cols, *refs):
    _, delta_hbm, rank_hbm, degree_hbm, row_hbm, valid_hbm = refs[:6]
    table, scale, total, masses = refs[6:10]
    delta_in, rank_in, degree, row, valid, sems = refs[10:]
    copies = started(
        (
            (row_hbm, row),
            (valid_hbm, valid),
            (delta_hbm, delta_in),
            (rank_hbm, rank_in),
            (degree_hbm, degree),
        ),
        sems,
    )

    for copy in copies:
        copy.wait()
    targets(cols, lax.axis_index("col"), row, valid, table)
    mass = jnp.zeros((1, LANES), jnp.float32)
    for r in range(4):
        part = slice(LANES * r, LANES * (r + 1))
        delta = delta_in[:, part]
        scale[:, r, :] = damping / degree[:, part].astype(jnp.float32)
        total[:, r, :] = rank_in[:, part] + delta
        mass = mass + jnp.sum(jnp.abs(delta), axis=0, keepdims=True)
    masses[...] = jnp.concatenate([mass, jnp.zeros((7, LANES), jnp.float32)], axis=0)


def join_kernel(step, cells, asked, own, one, two, three, scale, total, masses, *rest):
    message, total_out, masses_out, contrib = rest
    delta = own[...] + one[...] + two[...] + three[...]
    total_out[...] = total[...] + delta
    contrib[...] = delta * scale[...]
    mass = jnp.sum(jnp.sum(jnp.abs(delta), axis=0), axis=0, keepdims=True)
    rows = lax.broadcasted_iota(jnp.int32, (8, LANES), 0)
    merged = jnp.where(rows == step, mass, masses[...])
    masses_out[...] = merged
    extra = None
    if step == ITERS - 1:
        sums = jnp.broadcast_to(jnp.sum(merged, axis=1, keepdims=True) / cells, (8, LANES))
        extra = jnp.concatenate([*pieces(lane_row(sums)), jnp.zeros((1, LANES), jnp.float32)], axis=0)
    send(asked, contrib, message, extra)


def product(vectors, rows, j, first, weight, contracted):
    wide = jnp.concatenate(
        [jnp.broadcast_to(vectors[j, first + r][None], (8, LANES)) for r in range(4)], axis=1
    )
    found = lax.dot_general(
        wide.astype(jnp.bfloat16),
        weight,
        (((1,), (contracted,)), ((), ())),
        preferred_element_type=jnp.float32,
    )
    block = found[:, 3 * LANES :]
    for r in (2, 1, 0):
        block = jnp.where(rows == r, found[:, LANES * r : LANES * (r + 1)], block)
    return block[:4]


def start_tile_kernel(cols, *refs):
    source_hbm, row_hbm, valid_hbm, received, weight = refs[:5]
    own, one, two, three, turned, asked = refs[5:11]
    source, row, valid, table, vectors, sums, small_sems = refs[11:]
    tiles = weight.shape[0]
    owned = tiles

    copies = started(((source_hbm, source), (row_hbm, row), (valid_hbm, valid)), small_sems)
    sums[...] = jnp.zeros_like(sums)
    asking = lax.broadcasted_iota(jnp.int32, (tiles, LANES), 0)
    lanes = lax.broadcasted_iota(jnp.int32, (tiles, LANES), 1)
    requests = received[:, owned, :, :].astype(jnp.float32)[:, 0, :]
    asked[...] = jnp.sum(
        jnp.where(asking == lanes, requests, 0.0), axis=0, keepdims=True
    ).astype(jnp.int32)
    for copy in copies:
        copy.wait()
    targets(cols, lax.axis_index("col"), row, valid, table)
    for j in range(tiles):
        vectors[j, 0:4] = received[j, lax.rem(source[j], owned)].astype(jnp.float32)
    rows = lax.broadcasted_iota(jnp.int32, (8, LANES), 0)

    def group(g, carry):
        found = []
        for u in range(FIRST_GROUP):
            j = g * FIRST_GROUP + u
            tile = weight[j]
            turned[j] = tile.T
            found.append((j, product(vectors, rows, j, 0, tile, 1)))
        for j, block in found:
            q = table[j]
            sums[q] = sums[q] + block
        return carry

    lax.fori_loop(0, tiles // FIRST_GROUP, group, 0)
    for s, out in enumerate((own, one, two, three)):
        out[...] = sums[s * owned : (s + 1) * owned]


def tile_kernel(last, table, picked, turned, own, one, two, three, vectors, sums):
    owned = tiles = picked.shape[0]
    sums[...] = jnp.zeros_like(sums)
    vectors[...] = picked[...].astype(jnp.float32)
    rows = lax.broadcasted_iota(jnp.int32, (8, LANES), 0)

    def group(g, carry):
        found = []
        for u in range(GROUP):
            j = g * GROUP + u
            found.append((j, product(vectors, rows, j, 0, turned[j], 0)))
        for j, block in found:
            q = table[j]
            sums[q] = sums[q] + block
        return carry

    lax.fori_loop(0, tiles // GROUP, group, 0)
    for s, out in enumerate((own, one, two, three)):
        out[0:owned] = sums[s * owned : (s + 1) * owned]
    if last:
        mass = jnp.zeros((1, LANES), jnp.float32)
        for r in (4, 5, 6):
            mass = mass + jnp.sum(vectors[:, r, :], axis=0, keepdims=True)
        for out in (own, one, two, three):
            out[owned] = jnp.broadcast_to(mass, (4, LANES))


def last_kernel(own, one, two, three, total, rank_out, delta_out, masses, ordered):
    owned = total.shape[0]
    for r in range(4):
        part = slice(LANES * r, LANES * (r + 1))
        rank_out[:, part] = total[:, r, :]
        delta_out[:, part] = (
            own[0:owned, r, :] + one[0:owned, r, :] + two[0:owned, r, :] + three[0:owned, r, :]
        )
    for s, part in enumerate((own, one, two, three)):
        ordered[lax.rem(lax.axis_index("col") + 4 - s, 4)] = part[owned]
    mass = ordered[0] + ordered[1] + ordered[2] + ordered[3]
    masses[...] = mass[0:1, 0 : masses.shape[1]]


def f32(*shape):
    return jax.ShapeDtypeStruct(shape, jnp.float32)


def s32(*shape):
    return jax.ShapeDtypeStruct(shape, jnp.int32)


def call(kernel, outs, specs_in, specs_out, scratch, vmem=4, cost=None):
    return pl.pallas_call(
        kernel,
        out_shape=outs,
        in_specs=specs_in,
        out_specs=specs_out,
        scratch_shapes=scratch,
        cost_estimate=cost,
        compiler_params=pltpu.CompilerParams(vmem_limit_bytes=vmem << 20),
    )


def on_device(rank_in, delta_in, out_degree, tile_weight, tile_source, tile_row, tile_valid):
    owned, width = delta_in.shape
    tiles = tile_row.shape[0]
    n_group = lax.axis_size(BLK)
    n_column = lax.axis_size("col")
    cells = owned * n_group * n_column * width
    held = f32(owned, 4, LANES)
    message = jax.ShapeDtypeStruct((n_group, 8, LANES), jnp.bfloat16)
    block_scratch = pltpu.VMEM((owned, 4, LANES), jnp.float32)
    keep = functools.partial(pltpu.with_memory_space_constraint, memory_space=pltpu.VMEM)
    leave = functools.partial(pltpu.with_memory_space_constraint, memory_space=pltpu.HBM)
    resident = pltpu.VMEM(tile_weight.shape, tile_weight.dtype)
    indices = pltpu.SMEM((tiles,), jnp.int32)
    floats = pltpu.VMEM((owned, width), jnp.float32)
    integers = pltpu.VMEM((owned, width), jnp.int32)
    tile_scratch = [
        pltpu.VMEM((tiles, 8, LANES), jnp.float32),
        pltpu.VMEM((n_column * owned + 1, 4, LANES), jnp.float32),
    ]
    out = call(
        first_kernel,
        jax.ShapeDtypeStruct((n_group, owned + 1, 4, LANES), jnp.bfloat16),
        [HBM] * 3,
        VMEM,
        [indices, floats, integers, block_scratch, pltpu.SemaphoreType.DMA((3,))],
        cost=pl.CostEstimate(flops=40 << 30, transcendentals=0, bytes_accessed=128 << 20),
    )(leave(tile_source), leave(delta_in), leave(out_degree))
    for step in range(ITERS):
        picked = lax.all_to_all(out, BLK, split_axis=0, concat_axis=0, tiled=True)
        last = step == ITERS - 1
        if step == 0:
            *parts, turned, asked = call(
                functools.partial(start_tile_kernel, n_column),
                (held,) * 4 + (resident, s32(1, LANES)),
                [HBM] * 3 + [VMEM, VMEM],
                (VMEM,) * 6,
                [indices] * 4
                + tile_scratch
                + [pltpu.SemaphoreType.DMA((3,))],
            )(
                leave(tile_source),
                leave(tile_row),
                leave(tile_valid),
                picked,
                tile_weight,
            )
            table, scale, total, masses = call(
                functools.partial(window_kernel, n_column),
                (s32(tiles), held, held, f32(8, LANES)),
                [VMEM] + [HBM] * 5,
                (SMEM,) + (VMEM,) * 3,
                [floats, floats, integers, indices, indices, pltpu.SemaphoreType.DMA((5,))],
                cost=pl.CostEstimate(flops=0, transcendentals=0, bytes_accessed=8 << 20),
            )(
                parts[0],
                leave(delta_in),
                leave(rank_in),
                leave(out_degree),
                leave(tile_row),
                leave(tile_valid),
            )
        else:
            parts = call(
                functools.partial(tile_kernel, last),
                (f32(owned + last, 4, LANES),) * 4,
                [SMEM, VMEM, VMEM],
                (VMEM,) * 4,
                tile_scratch,
            )(table, picked, keep(turned))
        own, others = parts[0], parts[1:]
        others = [
            lax.ppermute(part, "col", [(i, (i + s + 1) % n_column) for i in range(n_column)])
            for s, part in enumerate(others)
        ]
        if not last:
            out, total, masses = call(
                functools.partial(join_kernel, step + 1, cells),
                (message, held, f32(8, LANES)),
                [SMEM] + [VMEM] * 7,
                (VMEM,) * 3,
                [block_scratch],
            )(asked, own, *others, scale, total, masses)
    rank_out, delta_out, stacked = call(
        last_kernel,
        (f32(owned, width), f32(owned, width), f32(1, ITERS)),
        [VMEM] * 5,
        (VMEM,) * 3,
        [pltpu.VMEM((4, 4, LANES), jnp.float32)],
    )(own, *others, total)
    return rank_out, delta_out, stacked.reshape(ITERS)


def solution(mesh):
    finer = Mesh(
        mesh.devices.reshape(4, 4, 2, mesh.shape["col"]), ("blk_0", "blk_1", "blk_2", "col")
    )
    placed = (
        P(BLK_COL, None),
        P(BLK_COL, None),
        P(BLK_COL, None),
        P(BLK_COL, None, None),
        P(BLK_COL),
        P(BLK_COL),
        P(BLK_COL),
    )
    return jax.shard_map(
        on_device,
        mesh=finer,
        in_specs=placed,
        out_specs=(P(BLK_COL, None), P(BLK_COL, None), P()),
        check_vma=False,
    )
```

time: 183 us -> 158 us (0.86)
  blocking collectives: 68.1 us -> 81 us
  local copies, waits for them, and re-layouts: 10.8 us -> 0.01 us
  waiting for transfers between devices: 29.6 us -> 19.7 us
  Pallas kernels: 37.5 us -> 29.4 us
  starting transfers between devices: 34.9 us -> 27 us
    all_to_all x5 -> x6, blocking collectives: 52.6 us -> 81 us  [on_device(): picked = lax.all_to_all(out, BLK, split_axis=0, concat_axis=0, tiled=True)]
    all_to_all x1 -> x0, blocking collectives: 15.6 us -> none  [on_device(): lax.all_to_all(tile_source.reshape(n_group, 1), BLK, split_axis=0, concat...]
    unnamed x14 -> x2, local copies, waits for them, and re-layouts: 9.6 us -> 0.01 us
    pallas_call x9, Pallas kernels: 33.5 us -> 25.7 us  [the longest x5 15.1 us: on_device(): call(functools.partial(tile_kernel, last), (f32(owned + last, 4, LANES),)...]
    ppermute x18, waiting for transfers between devices: 25.4 us -> 19.7 us  [on_device(): lax.ppermute(part, 'col', [(i, (i + s + 1) % n_column) for i in range(n_c...]
    all_to_all x1 -> x0, waiting for transfers between devices: 4.2 us -> none  [on_device(): picked = lax.all_to_all(out, BLK, split_axis=0, concat_axis=0, tiled=True)]
    ppermute x18, starting transfers between devices: 31.1 us -> 27 us  [on_device(): lax.ppermute(part, 'col', [(i, (i + s + 1) % n_column) for i in range(n_c...]
    all_to_all x1 -> x0, starting transfers between devices: 3.86 us -> none  [on_device(): picked = lax.all_to_all(out, BLK, split_axis=0, concat_axis=0, tiled=True)]
  transfers between devices with their start and end apart: 19 -> 18, of which waited for: 19 -> 17; matrix products, arithmetic and copies ran while one was open for 0% -> 0% of each run, Pallas kernels for 1% -> 1%
where the time goes in v3:
time: 158 us
  blocking collectives  81 us (51%)
  Pallas kernels  29.4 us (19%)
  starting transfers between devices  27 us (17%)
  waiting for transfers between devices  19.7 us (12%)
    all_to_all x6, blocking collectives, on_device(): picked = lax.all_to_all(out, BLK, split_axis=0, concat_axis=0, tiled=True)  81 us
    ppermute x18, starting transfers between devices, on_device(): lax.ppermute(part, 'col', [(i, (i + s + 1) % n_column) for i in range(n_c...  27 us
    ppermute x18, waiting for transfers between devices, on_device(): lax.ppermute(part, 'col', [(i, (i + s + 1) % n_column) for i in range(n_c...  19.7 us
    pallas_call x5, Pallas kernels, on_device(): call(functools.partial(tile_kernel, last), (f32(owned + last, 4, LANES),)...  15.1 us
    pallas_call x1, Pallas kernels, on_device(): call(functools.partial(start_tile_kernel, n_column), (held,) * 4 + (resid...  6.59 us
    pallas_call x5, Pallas kernels, on_device(): call(functools.partial(join_kernel, step + 1, cells), (message, held, f32...  3.74 us
  transfers between devices with their start and end apart: 18, of which 17 were waited for; matrix products, arithmetic and copies ran while one was open for 0% of the time, Pallas kernels for 1%

profile of v3, /device:TPU:0, one launch (start us, length us, event | category | flops | bytes accessed | tf_op | source)
XLA Modules:
  0.0 157.9 jit_solution(12114640899397832864)
XLA Ops:
  0.6 0.0 copy-start
  0.6 1.4 shard_map.94
  2.0 26.8 %all_to_all.30.refs_3_ = bf16[32,33,4,128]{3,2,1,0:T(4,128)(2,1)S(1)} all-to-all(bf16[32,33,4,128]{3,2,1,0:T(4,128)(2,1)S(1)} %shard_map.94), channel_id=1, replica_groups=mesh['blk_0'=4,'blk_1'=4,'blk_2'=2,'col'=4] {'blk_0','blk_1','blk_2'}, dimensions={0} | all-to-all | bytes 2162688 | tf_op jit(solution)/shard_map/all_to_all | solution.py:269
  28.9 0.0 copy-done
  28.9 6.6 %shard_map.95 = (f32[32,4,128]{2,1,0:T(4,128)S(1)}, f32[32,4,128]{2,1,0:T(4,128)S(1)}, f32[32,4,128]{2,1,0:T(4,128)S(1)}, f32[32,4,128]{2,1,0:T(4,128)S(1)}, bf1...) custom-call(s32[32]{0:T(128)} %refs_0_.1, s32[32]{0:T(128)} %refs_4_.3, s32[32]{0:T(128)} %refs_5_.1, ...), custom_call_target="tpu_custom_call" | custom-call | tf_op jit(solution)/shard_map/pallas_call | solution.py:272
  35.4 1.6 collective-permute-start
  37.0 2.7 %collective-permute-start.1 = (f32[32,4,128]{2,1,0:T(4,128)S(1)}, f32[32,4,128]{2,1,0:T(4,128)S(1)}, u32[]{:S(2)}, u32[]{:S(2)}) collective-permute-start(f32[32,4,128]{2,1,0:T(4,128)S(1)} %get-tuple-element.54), channel_id=1, source_target_pairs={{0,2},{1,3},{2,0},{3,1},{4,6},{5,7},{6,4},{7,5},{8,10},{9,11},{10,... | collective-permute-start | bytes 196616 | tf_op jit(solution)/shard_map/ppermute | solution.py:312
  39.7 1.4 collective-permute-start.2
  41.2 1.8 %shard_map.96 = (s32[32]{0:T(128)S(1)}, f32[32,4,128]{2,1,0:T(4,128)S(1)}, f32[32,4,128]{2,1,0:T(4,128)S(1)}, f32[8,128]{1,0:T(8,128)S(1)}) custom-call(f32[32,4,128]{2,1,0:T(4,128)S(1)} %get-tuple-element.50.refs_0_.own, f32[32,512]{1,0:T(8,128)} %refs_1_.3, f32[32,512]{1,0:T(8,128)} %refs_2_.3, s32[32,512]{1,0:T(8,128)} %refs_3_.1, s32[32]{0:T(128)} %refs_4_.3, ...), custom_call_target="tpu_custom_call" | custom-call | bytes 8388608 | tf_op jit(solution)/shard_map/pallas_call | solution.py:287
  43.0 0.0 collective-permute-done.one
  43.0 0.2 collective-permute-done.1.two
  43.2 0.8 collective-permute-done.2.three
  44.0 0.6 shard_map.97
  44.6 10.8 %all_to_all.31.picked = bf16[32,8,128]{2,1,0:T(8,128)(2,1)S(1)} all-to-all(bf16[32,8,128]{2,1,0:T(8,128)(2,1)S(1)} %get-tuple-element.59), channel_id=1, replica_groups=mesh['blk_0'=4,'blk_1'=4,'blk_2'=2,'col'=4] {'blk_0','blk_1','blk_2'}, dimensions={0} | all-to-all | bytes 131072 | tf_op jit(solution)/shard_map/all_to_all | solution.py:269
  55.4 3.0 %shard_map.98 = (f32[32,4,128]{2,1,0:T(4,128)S(1)}, f32[32,4,128]{2,1,0:T(4,128)S(1)}, f32[32,4,128]{2,1,0:T(4,128)S(1)}, f32[32,4,128]{2,1,0:T(4,128)S(1)}) custom-call(s32[32]{0:T(128)S(1)} %get-tuple-element.51.table, bf16[32,8,128]{2,1,0:T(8,128)(2,1)S(1)} %all_to_all.31.picked, bf16[32,512,512]{2,1,0:T(8,128)(2,1)S(1)} %get-tuple-element.60.turned), custom_call_target="tpu_custom_call" | custom-call | tf_op jit(solution)/shard_map/pallas_call | solution.py:303
  58.4 0.6 collective-permute-start.3
  59.1 3.5 %collective-permute-start.4 = (f32[32,4,128]{2,1,0:T(4,128)S(1)}, f32[32,4,128]{2,1,0:T(4,128)S(1)}, u32[]{:S(2)}, u32[]{:S(2)}) collective-permute-start(f32[32,4,128]{2,1,0:T(4,128)S(1)} %get-tuple-element.63), channel_id=1, source_target_pairs={{0,2},{1,3},{2,0},{3,1},{4,6},{5,7},{6,4},{7,5},{8,10},{9,11},{10,... | collective-permute-start | bytes 196616 | tf_op jit(solution)/shard_map/ppermute | solution.py:312
  62.6 0.3 collective-permute-start.5
  62.9 1.1 collective-permute-done.3.one
  64.0 2.1 %collective-permute-done.4.two = f32[32,4,128]{2,1,0:T(4,128)S(1)} collective-permute-done((f32[32,4,128]{2,1,0:T(4,128)S(1)}, f32[32,4,128]{2,1,0:T(4,128)S(1)}, u32[]{:S(2)}, u32[]{:S(2)}) %collective-permute-start.4) | collective-permute-done | bytes 65568 | tf_op jit(solution)/shard_map/ppermute | solution.py:312
  66.1 0.8 collective-permute-done.5.three
  66.9 0.6 shard_map.99
  67.5 10.9 %all_to_all.32.picked = bf16[32,8,128]{2,1,0:T(8,128)(2,1)S(1)} all-to-all(bf16[32,8,128]{2,1,0:T(8,128)(2,1)S(1)} %get-tuple-element.67), channel_id=1, replica_groups=mesh['blk_0'=4,'blk_1'=4,'blk_2'=2,'col'=4] {'blk_0','blk_1','blk_2'}, dimensions={0} | all-to-all | bytes 131072 | tf_op jit(solution)/shard_map/all_to_all | solution.py:269
  78.4 3.0 %shard_map.100 = (f32[32,4,128]{2,1,0:T(4,128)S(1)}, f32[32,4,128]{2,1,0:T(4,128)S(1)}, f32[32,4,128]{2,1,0:T(4,128)S(1)}, f32[32,4,128]{2,1,0:T(4,128)S(1)}) custom-call(s32[32]{0:T(128)S(1)} %get-tuple-element.51.table, bf16[32,8,128]{2,1,0:T(8,128)(2,1)S(1)} %all_to_all.32.picked, bf16[32,512,512]{2,1,0:T(8,128)(2,1)S(1)} %get-tuple-element.60.turned), custom_call_target="tpu_custom_call" | custom-call | tf_op jit(solution)/shard_map/pallas_call | solution.py:303
  81.4 0.1 collective-permute-start.6
  81.5 3.2 %collective-permute-start.7 = (f32[32,4,128]{2,1,0:T(4,128)S(1)}, f32[32,4,128]{2,1,0:T(4,128)S(1)}, u32[]{:S(2)}, u32[]{:S(2)}) collective-permute-start(f32[32,4,128]{2,1,0:T(4,128)S(1)} %get-tuple-element.70), channel_id=1, source_target_pairs={{0,2},{1,3},{2,0},{3,1},{4,6},{5,7},{6,4},{7,5},{8,10},{9,11},{10,... | collective-permute-start | bytes 196616 | tf_op jit(solution)/shard_map/ppermute | solution.py:312
  84.6 0.9 collective-permute-start.8
  85.6 2.3 %collective-permute-done.6.one = f32[32,4,128]{2,1,0:T(4,128)S(1)} collective-permute-done((f32[32,4,128]{2,1,0:T(4,128)S(1)}, f32[32,4,128]{2,1,0:T(4,128)S(1)}, u32[]{:S(2)}, u32[]{:S(2)}) %collective-permute-start.6) | collective-permute-done | bytes 65568 | tf_op jit(solution)/shard_map/ppermute | solution.py:312
  87.9 0.3 collective-permute-done.7.two
  88.2 0.7 collective-permute-done.8.three
  88.9 0.6 shard_map.101
  89.5 10.9 %all_to_all.33.picked = bf16[32,8,128]{2,1,0:T(8,128)(2,1)S(1)} all-to-all(bf16[32,8,128]{2,1,0:T(8,128)(2,1)S(1)} %get-tuple-element.74), channel_id=1, replica_groups=mesh['blk_0'=4,'blk_1'=4,'blk_2'=2,'col'=4] {'blk_0','blk_1','blk_2'}, dimensions={0} | all-to-all | bytes 131072 | tf_op jit(solution)/shard_map/all_to_all | solution.py:269
  100.4 3.0 %shard_map.102 = (f32[32,4,128]{2,1,0:T(4,128)S(1)}, f32[32,4,128]{2,1,0:T(4,128)S(1)}, f32[32,4,128]{2,1,0:T(4,128)S(1)}, f32[32,4,128]{2,1,0:T(4,128)S(1)}) custom-call(s32[32]{0:T(128)S(1)} %get-tuple-element.51.table, bf16[32,8,128]{2,1,0:T(8,128)(2,1)S(1)} %all_to_all.33.picked, bf16[32,512,512]{2,1,0:T(8,128)(2,1)S(1)} %get-tuple-element.60.turned), custom_call_target="tpu_custom_call" | custom-call | tf_op jit(solution)/shard_map/pallas_call | solution.py:303
  103.4 1.0 collective-permute-start.9
  104.4 3.0 %collective-permute-start.10 = (f32[32,4,128]{2,1,0:T(4,128)S(1)}, f32[32,4,128]{2,1,0:T(4,128)S(1)}, u32[]{:S(2)}, u32[]{:S(2)}) collective-permute-start(f32[32,4,128]{2,1,0:T(4,128)S(1)} %get-tuple-element.77), channel_id=1, source_target_pairs={{0,2},{1,3},{2,0},{3,1},{4,6},{5,7},{6,4},{7,5},{8,10},{9,11},{10,... | collective-permute-start | bytes 196616 | tf_op jit(solution)/shard_map/ppermute | solution.py:312
  107.4 0.2 collective-permute-start.11
  107.6 1.6 %collective-permute-done.9.one = f32[32,4,128]{2,1,0:T(4,128)S(1)} collective-permute-done((f32[32,4,128]{2,1,0:T(4,128)S(1)}, f32[32,4,128]{2,1,0:T(4,128)S(1)}, u32[]{:S(2)}, u32[]{:S(2)}) %collective-permute-start.9) | collective-permute-done | bytes 65568 | tf_op jit(solution)/shard_map/ppermute | solution.py:312
  109.3 1.6 %collective-permute-done.10.two = f32[32,4,128]{2,1,0:T(4,128)S(1)} collective-permute-done((f32[32,4,128]{2,1,0:T(4,128)S(1)}, f32[32,4,128]{2,1,0:T(4,128)S(1)}, u32[]{:S(2)}, u32[]{:S(2)}) %collective-permute-start.10) | collective-permute-done | bytes 65568 | tf_op jit(solution)/shard_map/ppermute | solution.py:312
  110.9 0.8 collective-permute-done.11.three
  111.7 0.6 shard_map.103
  112.3 10.9 %all_to_all.34.picked = bf16[32,8,128]{2,1,0:T(8,128)(2,1)S(1)} all-to-all(bf16[32,8,128]{2,1,0:T(8,128)(2,1)S(1)} %get-tuple-element.81), channel_id=1, replica_groups=mesh['blk_0'=4,'blk_1'=4,'blk_2'=2,'col'=4] {'blk_0','blk_1','blk_2'}, dimensions={0} | all-to-all | bytes 131072 | tf_op jit(solution)/shard_map/all_to_all | solution.py:269
  123.2 3.0 %shard_map.104 = (f32[32,4,128]{2,1,0:T(4,128)S(1)}, f32[32,4,128]{2,1,0:T(4,128)S(1)}, f32[32,4,128]{2,1,0:T(4,128)S(1)}, f32[32,4,128]{2,1,0:T(4,128)S(1)}) custom-call(s32[32]{0:T(128)S(1)} %get-tuple-element.51.table, bf16[32,8,128]{2,1,0:T(8,128)(2,1)S(1)} %all_to_all.34.picked, bf16[32,512,512]{2,1,0:T(8,128)(2,1)S(1)} %get-tuple-element.60.turned), custom_call_target="tpu_custom_call" | custom-call | tf_op jit(solution)/shard_map/pallas_call | solution.py:303
  126.2 0.2 collective-permute-start.12
  126.5 3.1 %collective-permute-start.13 = (f32[32,4,128]{2,1,0:T(4,128)S(1)}, f32[32,4,128]{2,1,0:T(4,128)S(1)}, u32[]{:S(2)}, u32[]{:S(2)}) collective-permute-start(f32[32,4,128]{2,1,0:T(4,128)S(1)} %get-tuple-element.84), channel_id=1, source_target_pairs={{0,2},{1,3},{2,0},{3,1},{4,6},{5,7},{6,4},{7,5},{8,10},{9,11},{10,... | collective-permute-start | bytes 196616 | tf_op jit(solution)/shard_map/ppermute | solution.py:312
  129.6 0.9 collective-permute-start.14
  130.4 1.9 %collective-permute-done.12.one = f32[32,4,128]{2,1,0:T(4,128)S(1)} collective-permute-done((f32[32,4,128]{2,1,0:T(4,128)S(1)}, f32[32,4,128]{2,1,0:T(4,128)S(1)}, u32[]{:S(2)}, u32[]{:S(2)}) %collective-permute-start.12) | collective-permute-done | bytes 65568 | tf_op jit(solution)/shard_map/ppermute | solution.py:312
  132.4 0.7 collective-permute-done.13.two
  133.1 0.8 collective-permute-done.14.three
  133.8 1.2 shard_map.105
  135.1 10.9 %all_to_all.35.picked = bf16[32,8,128]{2,1,0:T(8,128)(2,1)S(1)} all-to-all(bf16[32,8,128]{2,1,0:T(8,128)(2,1)S(1)} %get-tuple-element.88), channel_id=1, replica_groups=mesh['blk_0'=4,'blk_1'=4,'blk_2'=2,'col'=4] {'blk_0','blk_1','blk_2'}, dimensions={0} | all-to-all | bytes 131072 | tf_op jit(solution)/shard_map/all_to_all | solution.py:269
  145.9 3.0 %shard_map.106 = (f32[33,4,128]{2,1,0:T(4,128)S(1)}, f32[33,4,128]{2,1,0:T(4,128)S(1)}, f32[33,4,128]{2,1,0:T(4,128)S(1)}, f32[33,4,128]{2,1,0:T(4,128)S(1)}) custom-call(s32[32]{0:T(128)S(1)} %get-tuple-element.51.table, bf16[32,8,128]{2,1,0:T(8,128)(2,1)S(1)} %all_to_all.35.picked, bf16[32,512,512]{2,1,0:T(8,128)(2,1)S(1)} %get-tuple-element.60.turned), custom_call_target="tpu_custom_call" | custom-call | tf_op jit(solution)/shard_map/pallas_call | solution.py:303
  149.0 0.9 collective-permute-start.15
  149.8 3.0 %collective-permute-start.16 = (f32[33,4,128]{2,1,0:T(4,128)S(1)}, f32[33,4,128]{2,1,0:T(4,128)S(1)}, u32[]{:S(2)}, u32[]{:S(2)}) collective-permute-start(f32[33,4,128]{2,1,0:T(4,128)S(1)} %get-tuple-element.91), channel_id=1, source_target_pairs={{0,2},{1,3},{2,0},{3,1},{4,6},{5,7},{6,4},{7,5},{8,10},{9,11},{10,... | collective-permute-start | bytes 202760 | tf_op jit(solution)/shard_map/ppermute | solution.py:312
  152.9 0.3 collective-permute-start.17
  153.2 1.7 %collective-permute-done.15.one = f32[33,4,128]{2,1,0:T(4,128)S(1)} collective-permute-done((f32[33,4,128]{2,1,0:T(4,128)S(1)}, f32[33,4,128]{2,1,0:T(4,128)S(1)}, u32[]{:S(2)}, u32[]{:S(2)}) %collective-permute-start.15) | collective-permute-done | bytes 67616 | tf_op jit(solution)/shard_map/ppermute | solution.py:312
  154.9 1.5 collective-permute-done.16.two
  156.4 0.7 collective-permute-done.17.three
  157.2 0.8 shard_map.107
Async XLA Ops:
  0.6 28.2 %copy-start = (bf16[32,512,512]{2,1,0:T(8,128)(2,1)S(1)}, bf16[32,512,512]{2,1,0:T(8,128)(2,1)}, u32[]{:S(2)}) copy-start(bf16[32,512,512]{2,1,0:T(8,128)(2,1)} %refs_4_.2) | copy-start | bytes 50331652
  35.4 7.5 %collective-permute-start = (f32[32,4,128]{2,1,0:T(4,128)S(1)}, f32[32,4,128]{2,1,0:T(4,128)S(1)}, u32[]{:S(2)}, u32[]{:S(2)}) collective-permute-start(f32[32,4,128]{2,1,0:T(4,128)S(1)} %get-tuple-element.53), channel_id=1, source_target_pairs={{0,1},{1,2},{2,3},{3,0},{4,5},{5,6},{6,7},{7,4},{8,9},{9,10},{10,1... | collective-permute-start | bytes 196616 | tf_op jit(solution)/shard_map/ppermute | solution.py:312
  37.0 6.2 %collective-permute-start.1 = (f32[32,4,128]{2,1,0:T(4,128)S(1)}, f32[32,4,128]{2,1,0:T(4,128)S(1)}, u32[]{:S(2)}, u32[]{:S(2)}) collective-permute-start(f32[32,4,128]{2,1,0:T(4,128)S(1)} %get-tuple-element.54), channel_id=1, source_target_pairs={{0,2},{1,3},{2,0},{3,1},{4,6},{5,7},{6,4},{7,5},{8,10},{9,11},{10,... | collective-permute-start | bytes 196616 | tf_op jit(solution)/shard_map/ppermute | solution.py:312
  39.7 4.3 %collective-permute-start.2 = (f32[32,4,128]{2,1,0:T(4,128)S(1)}, f32[32,4,128]{2,1,0:T(4,128)S(1)}, u32[]{:S(2)}, u32[]{:S(2)}) collective-permute-start(f32[32,4,128]{2,1,0:T(4,128)S(1)} %get-tuple-element.55), channel_id=1, source_target_pairs={{0,3},{1,0},{2,1},{3,2},{4,7},{5,4},{6,5},{7,6},{8,11},{9,8},{10,9... | collective-permute-start | bytes 196616 | tf_op jit(solution)/shard_map/ppermute | solution.py:312
  58.4 5.5 %collective-permute-start.3 = (f32[32,4,128]{2,1,0:T(4,128)S(1)}, f32[32,4,128]{2,1,0:T(4,128)S(1)}, u32[]{:S(2)}, u32[]{:S(2)}) collective-permute-start(f32[32,4,128]{2,1,0:T(4,128)S(1)} %get-tuple-element.62), channel_id=1, source_target_pairs={{0,1},{1,2},{2,3},{3,0},{4,5},{5,6},{6,7},{7,4},{8,9},{9,10},{10,1... | collective-permute-start | bytes 196616 | tf_op jit(solution)/shard_map/ppermute | solution.py:312
  59.1 7.0 %collective-permute-start.4 = (f32[32,4,128]{2,1,0:T(4,128)S(1)}, f32[32,4,128]{2,1,0:T(4,128)S(1)}, u32[]{:S(2)}, u32[]{:S(2)}) collective-permute-start(f32[32,4,128]{2,1,0:T(4,128)S(1)} %get-tuple-element.63), channel_id=1, source_target_pairs={{0,2},{1,3},{2,0},{3,1},{4,6},{5,7},{6,4},{7,5},{8,10},{9,11},{10,... | collective-permute-start | bytes 196616 | tf_op jit(solution)/shard_map/ppermute | solution.py:312
  62.6 4.3 %collective-permute-start.5 = (f32[32,4,128]{2,1,0:T(4,128)S(1)}, f32[32,4,128]{2,1,0:T(4,128)S(1)}, u32[]{:S(2)}, u32[]{:S(2)}) collective-permute-start(f32[32,4,128]{2,1,0:T(4,128)S(1)} %get-tuple-element.64), channel_id=1, source_target_pairs={{0,3},{1,0},{2,1},{3,2},{4,7},{5,4},{6,5},{7,6},{8,11},{9,8},{10,9... | collective-permute-start | bytes 196616 | tf_op jit(solution)/shard_map/ppermute | solution.py:312
  81.4 6.5 %collective-permute-start.6 = (f32[32,4,128]{2,1,0:T(4,128)S(1)}, f32[32,4,128]{2,1,0:T(4,128)S(1)}, u32[]{:S(2)}, u32[]{:S(2)}) collective-permute-start(f32[32,4,128]{2,1,0:T(4,128)S(1)} %get-tuple-element.69), channel_id=1, source_target_pairs={{0,1},{1,2},{2,3},{3,0},{4,5},{5,6},{6,7},{7,4},{8,9},{9,10},{10,1... | collective-permute-start | bytes 196616 | tf_op jit(solution)/shard_map/ppermute | solution.py:312
  81.5 6.7 %collective-permute-start.7 = (f32[32,4,128]{2,1,0:T(4,128)S(1)}, f32[32,4,128]{2,1,0:T(4,128)S(1)}, u32[]{:S(2)}, u32[]{:S(2)}) collective-permute-start(f32[32,4,128]{2,1,0:T(4,128)S(1)} %get-tuple-element.70), channel_id=1, source_target_pairs={{0,2},{1,3},{2,0},{3,1},{4,6},{5,7},{6,4},{7,5},{8,10},{9,11},{10,... | collective-permute-start | bytes 196616 | tf_op jit(solution)/shard_map/ppermute | solution.py:312
  84.6 4.3 %collective-permute-start.8 = (f32[32,4,128]{2,1,0:T(4,128)S(1)}, f32[32,4,128]{2,1,0:T(4,128)S(1)}, u32[]{:S(2)}, u32[]{:S(2)}) collective-permute-start(f32[32,4,128]{2,1,0:T(4,128)S(1)} %get-tuple-element.71), channel_id=1, source_target_pairs={{0,3},{1,0},{2,1},{3,2},{4,7},{5,4},{6,5},{7,6},{8,11},{9,8},{10,9... | collective-permute-start | bytes 196616 | tf_op jit(solution)/shard_map/ppermute | solution.py:312
  103.4 5.8 %collective-permute-start.9 = (f32[32,4,128]{2,1,0:T(4,128)S(1)}, f32[32,4,128]{2,1,0:T(4,128)S(1)}, u32[]{:S(2)}, u32[]{:S(2)}) collective-permute-start(f32[32,4,128]{2,1,0:T(4,128)S(1)} %get-tuple-element.76), channel_id=1, source_target_pairs={{0,1},{1,2},{2,3},{3,0},{4,5},{5,6},{6,7},{7,4},{8,9},{9,10},{10,1... | collective-permute-start | bytes 196616 | tf_op jit(solution)/shard_map/ppermute | solution.py:312
  104.4 6.5 %collective-permute-start.10 = (f32[32,4,128]{2,1,0:T(4,128)S(1)}, f32[32,4,128]{2,1,0:T(4,128)S(1)}, u32[]{:S(2)}, u32[]{:S(2)}) collective-permute-start(f32[32,4,128]{2,1,0:T(4,128)S(1)} %get-tuple-element.77), channel_id=1, source_target_pairs={{0,2},{1,3},{2,0},{3,1},{4,6},{5,7},{6,4},{7,5},{8,10},{9,11},{10,... | collective-permute-start | bytes 196616 | tf_op jit(solution)/shard_map/ppermute | solution.py:312
  107.4 4.3 %collective-permute-start.11 = (f32[32,4,128]{2,1,0:T(4,128)S(1)}, f32[32,4,128]{2,1,0:T(4,128)S(1)}, u32[]{:S(2)}, u32[]{:S(2)}) collective-permute-start(f32[32,4,128]{2,1,0:T(4,128)S(1)} %get-tuple-element.78), channel_id=1, source_target_pairs={{0,3},{1,0},{2,1},{3,2},{4,7},{5,4},{6,5},{7,6},{8,11},{9,8},{10,9... | collective-permute-start | bytes 196616 | tf_op jit(solution)/shard_map/ppermute | solution.py:312
  126.2 6.1 %collective-permute-start.12 = (f32[32,4,128]{2,1,0:T(4,128)S(1)}, f32[32,4,128]{2,1,0:T(4,128)S(1)}, u32[]{:S(2)}, u32[]{:S(2)}) collective-permute-start(f32[32,4,128]{2,1,0:T(4,128)S(1)} %get-tuple-element.83), channel_id=1, source_target_pairs={{0,1},{1,2},{2,3},{3,0},{4,5},{5,6},{6,7},{7,4},{8,9},{9,10},{10,1... | collective-permute-start | bytes 196616 | tf_op jit(solution)/shard_map/ppermute | solution.py:312
  126.5 6.6 %collective-permute-start.13 = (f32[32,4,128]{2,1,0:T(4,128)S(1)}, f32[32,4,128]{2,1,0:T(4,128)S(1)}, u32[]{:S(2)}, u32[]{:S(2)}) collective-permute-start(f32[32,4,128]{2,1,0:T(4,128)S(1)} %get-tuple-element.84), channel_id=1, source_target_pairs={{0,2},{1,3},{2,0},{3,1},{4,6},{5,7},{6,4},{7,5},{8,10},{9,11},{10,... | collective-permute-start | bytes 196616 | tf_op jit(solution)/shard_map/ppermute | solution.py:312
  129.6 4.3 %collective-permute-start.14 = (f32[32,4,128]{2,1,0:T(4,128)S(1)}, f32[32,4,128]{2,1,0:T(4,128)S(1)}, u32[]{:S(2)}, u32[]{:S(2)}) collective-permute-start(f32[32,4,128]{2,1,0:T(4,128)S(1)} %get-tuple-element.85), channel_id=1, source_target_pairs={{0,3},{1,0},{2,1},{3,2},{4,7},{5,4},{6,5},{7,6},{8,11},{9,8},{10,9... | collective-permute-start | bytes 196616 | tf_op jit(solution)/shard_map/ppermute | solution.py:312
  149.0 5.9 %collective-permute-start.15 = (f32[33,4,128]{2,1,0:T(4,128)S(1)}, f32[33,4,128]{2,1,0:T(4,128)S(1)}, u32[]{:S(2)}, u32[]{:S(2)}) collective-permute-start(f32[33,4,128]{2,1,0:T(4,128)S(1)} %get-tuple-element.90), channel_id=1, source_target_pairs={{0,1},{1,2},{2,3},{3,0},{4,5},{5,6},{6,7},{7,4},{8,9},{9,10},{10,1... | collective-permute-start | bytes 202760 | tf_op jit(solution)/shard_map/ppermute | solution.py:312
  149.8 6.6 %collective-permute-start.16 = (f32[33,4,128]{2,1,0:T(4,128)S(1)}, f32[33,4,128]{2,1,0:T(4,128)S(1)}, u32[]{:S(2)}, u32[]{:S(2)}) collective-permute-start(f32[33,4,128]{2,1,0:T(4,128)S(1)} %get-tuple-element.91), channel_id=1, source_target_pairs={{0,2},{1,3},{2,0},{3,1},{4,6},{5,7},{6,4},{7,5},{8,10},{9,11},{10,... | collective-permute-start | bytes 202760 | tf_op jit(solution)/shard_map/ppermute | solution.py:312
  152.9 4.3 %collective-permute-start.17 = (f32[33,4,128]{2,1,0:T(4,128)S(1)}, f32[33,4,128]{2,1,0:T(4,128)S(1)}, u32[]{:S(2)}, u32[]{:S(2)}) collective-permute-start(f32[33,4,128]{2,1,0:T(4,128)S(1)} %get-tuple-element.92), channel_id=1, source_target_pairs={{0,3},{1,0},{2,1},{3,2},{4,7},{5,4},{6,5},{7,6},{8,11},{9,8},{10,9... | collective-permute-start | bytes 202760 | tf_op jit(solution)/shard_map/ppermute | solution.py:312

commit v4 on v3

--- a/solution.py
+++ b/solution.py
@@ -12,7 +12,7 @@
 BLK = ("blk_0", "blk_1", "blk_2")
 BLK_COL = ("blk_0", "blk_1", "blk_2", "col")
 LANES = 128
-GROUP = 16
+GROUP = 32
 FIRST_GROUP = 4
 
 damping = 0.85
@@ -53,15 +53,6 @@
     for copy in copies:
         copy.start()
     return copies
-
-
-def send(asked, contrib, message, extra):
-    for b in range(message.shape[0]):
-        block = contrib[asked[0, b]]
-        if extra is None:
-            message[b, 0:4, :] = block.astype(jnp.bfloat16)
-        else:
-            message[b] = jnp.concatenate([block, extra], axis=0).astype(jnp.bfloat16)
 
 
 def first_kernel(source_hbm, delta_hbm, degree_hbm, message, source, delta, degree, contrib, sems):
@@ -80,7 +71,7 @@
 
 def window_kernel(cols, *refs):
     _, delta_hbm, rank_hbm, degree_hbm, row_hbm, valid_hbm = refs[:6]
-    table, scale, total, masses = refs[6:10]
+    table, degrees, total, masses = refs[6:10]
     delta_in, rank_in, degree, row, valid, sems = refs[10:]
     copies = started(
         (
@@ -100,26 +91,59 @@
     for r in range(4):
         part = slice(LANES * r, LANES * (r + 1))
         delta = delta_in[:, part]
-        scale[:, r, :] = damping / degree[:, part].astype(jnp.float32)
+        degrees[:, r, :] = degree[:, part].astype(jnp.float32)
         total[:, r, :] = rank_in[:, part] + delta
         mass = mass + jnp.sum(jnp.abs(delta), axis=0, keepdims=True)
     masses[...] = jnp.concatenate([mass, jnp.zeros((7, LANES), jnp.float32)], axis=0)
 
 
-def join_kernel(step, cells, asked, own, one, two, three, scale, total, masses, *rest):
-    message, total_out, masses_out, contrib = rest
-    delta = own[...] + one[...] + two[...] + three[...]
+def one_join_kernel(cols, own, one, two, three, degrees, total, masses, *refs):
+    message, total_out, masses_out, wants, contrib, asked, sem = refs
+    owned = total.shape[0]
+    parts = (own, one, two, three)
+    for s, part in enumerate(parts):
+        at = (cols - s) % cols
+        wants[at : at + 1, :] = part[owned, 0:1, :].astype(jnp.int32) + at * owned
+    copy = pltpu.make_async_copy(wants, asked, sem)
+    copy.start()
+    delta = own[0:owned] + one[0:owned] + two[0:owned] + three[0:owned]
     total_out[...] = total[...] + delta
-    contrib[...] = delta * scale[...]
+    contrib[:, 0:4, :] = delta * (damping / degrees[...])
+    contrib[:, 4:8, :] = degrees[...]
     mass = jnp.sum(jnp.sum(jnp.abs(delta), axis=0), axis=0, keepdims=True)
     rows = lax.broadcasted_iota(jnp.int32, (8, LANES), 0)
-    merged = jnp.where(rows == step, mass, masses[...])
-    masses_out[...] = merged
-    extra = None
-    if step == ITERS - 1:
-        sums = jnp.broadcast_to(jnp.sum(merged, axis=1, keepdims=True) / cells, (8, LANES))
-        extra = jnp.concatenate([*pieces(lane_row(sums)), jnp.zeros((1, LANES), jnp.float32)], axis=0)
-    send(asked, contrib, message, extra)
+    masses_out[...] = jnp.where(rows == 1, mass, masses[...])
+    copy.wait()
+    for b in range(message.shape[0]):
+        message[b] = contrib[asked[0, b]].astype(jnp.bfloat16)
+
+
+def tally(steps, own, one, two, three, total, masses):
+    owned = total.shape[0]
+    ranks = total[...]
+    merged = masses[...]
+    rows = lax.broadcasted_iota(jnp.int32, (8, LANES), 0)
+    for t, step in enumerate(steps):
+        part = slice(t * owned, (t + 1) * owned)
+        delta = own[part] + one[part] + two[part] + three[part]
+        ranks = ranks + delta
+        mass = jnp.sum(jnp.sum(jnp.abs(delta), axis=0), axis=0, keepdims=True)
+        merged = jnp.where(rows == step, mass, merged)
+    return ranks, merged, delta
+
+
+def early_join_kernel(steps, _, own, one, two, three, total, masses, total_out, masses_out):
+    total_out[...], masses_out[...], _ = tally(steps, own, one, two, three, total, masses)
+
+
+def late_join_kernel(cells, wants, own, one, two, three, degrees, total, masses, *refs):
+    message, total_out, contrib = refs
+    total_out[...], merged, delta = tally((ITERS - 1,), own, one, two, three, total, masses)
+    contrib[...] = delta * (damping / degrees[...])
+    sums = jnp.broadcast_to(jnp.sum(merged, axis=1, keepdims=True) / cells, (8, LANES))
+    extra = jnp.concatenate([*pieces(lane_row(sums)), jnp.zeros((1, LANES), jnp.float32)], axis=0)
+    for b in range(message.shape[0]):
+        message[b] = jnp.concatenate([contrib[wants[0, b]], extra], axis=0).astype(jnp.bfloat16)
 
 
 def product(vectors, rows, j, first, weight, contracted):
@@ -140,8 +164,8 @@
 
 def start_tile_kernel(cols, *refs):
     source_hbm, row_hbm, valid_hbm, received, weight = refs[:5]
-    own, one, two, three, turned, asked = refs[5:11]
-    source, row, valid, table, vectors, sums, small_sems = refs[11:]
+    own, one, two, three, turned = refs[5:10]
+    source, row, valid, table, vectors, sums, small_sems = refs[10:]
     tiles = weight.shape[0]
     owned = tiles
 
@@ -150,9 +174,9 @@
     asking = lax.broadcasted_iota(jnp.int32, (tiles, LANES), 0)
     lanes = lax.broadcasted_iota(jnp.int32, (tiles, LANES), 1)
     requests = received[:, owned, :, :].astype(jnp.float32)[:, 0, :]
-    asked[...] = jnp.sum(
-        jnp.where(asking == lanes, requests, 0.0), axis=0, keepdims=True
-    ).astype(jnp.int32)
+    asked = jnp.sum(jnp.where(asking == lanes, requests, 0.0), axis=0, keepdims=True)
+    for out in (own, one, two, three):
+        out[owned] = jnp.broadcast_to(asked, (4, LANES))
     for copy in copies:
         copy.wait()
     targets(cols, lax.axis_index("col"), row, valid, table)
@@ -174,13 +198,12 @@
 
     lax.fori_loop(0, tiles // FIRST_GROUP, group, 0)
     for s, out in enumerate((own, one, two, three)):
-        out[...] = sums[s * owned : (s + 1) * owned]
-
-
-def tile_kernel(last, table, picked, turned, own, one, two, three, vectors, sums):
-    owned = tiles = picked.shape[0]
+        out[0:owned] = sums[s * owned : (s + 1) * owned]
+
+
+def multiply(table, vectors, turned, sums):
+    tiles = turned.shape[0]
     sums[...] = jnp.zeros_like(sums)
-    vectors[...] = picked[...].astype(jnp.float32)
     rows = lax.broadcasted_iota(jnp.int32, (8, LANES), 0)
 
     def group(g, carry):
@@ -194,14 +217,60 @@
         return carry
 
     lax.fori_loop(0, tiles // GROUP, group, 0)
+
+
+def take_sums(arrived, scale, vectors):
+    tiles = vectors.shape[0]
+    columns = arrived.shape[0] // tiles
+    blocks = jnp.sum(arrived[...].reshape(tiles, columns, 4, LANES), axis=1)
+    vectors[:, 0:4, :] = blocks * scale[...]
+
+
+def give_parts(outs, earlier, sums, owned):
+    for s, out in enumerate(outs):
+        before = earlier[s :: len(outs)]
+        for t, part in enumerate(before):
+            out[t * owned : (t + 1) * owned] = part[...]
+        out[len(before) * owned :] = sums[s * owned : (s + 1) * owned]
+
+
+def relay_kernel(cols, first, *refs):
+    table, wants, arrived, *refs, vectors, sums = refs
+    owned = vectors.shape[0]
+    if first:
+        turned, message, *parts, scale = refs
+        vectors[...] = arrived[...].astype(jnp.float32)
+        scale[...] = damping / vectors[:, 4:8, :]
+        earlier = ()
+    else:
+        scale, turned, *earlier, message = refs[:-cols]
+        parts = refs[-cols:]
+        take_sums(arrived, scale, vectors)
+    multiply(table, vectors, turned, sums)
+    c = lax.axis_index("col")
+    for s in range(cols):
+        to = lax.rem(c + s, cols)
+        for b in range(message.shape[0] // cols):
+            message[b * cols + to] = sums[wants[s, b]]
+    give_parts(parts, earlier, sums, owned)
+
+
+def collect_kernel(table, arrived, scale, turned, own, one, two, three, vectors, sums):
+    take_sums(arrived, scale, vectors)
+    multiply(table, vectors, turned, sums)
+    give_parts((own, one, two, three), (), sums, vectors.shape[0])
+
+
+def end_tile_kernel(table, picked, turned, own, one, two, three, vectors, sums):
+    owned = picked.shape[0]
+    vectors[...] = picked[...].astype(jnp.float32)
+    multiply(table, vectors, turned, sums)
+    mass = jnp.zeros((1, LANES), jnp.float32)
+    for r in (4, 5, 6):
+        mass = mass + jnp.sum(vectors[:, r, :], axis=0, keepdims=True)
     for s, out in enumerate((own, one, two, three)):
         out[0:owned] = sums[s * owned : (s + 1) * owned]
-    if last:
-        mass = jnp.zeros((1, LANES), jnp.float32)
-        for r in (4, 5, 6):
-            mass = mass + jnp.sum(vectors[:, r, :], axis=0, keepdims=True)
-        for out in (own, one, two, three):
-            out[owned] = jnp.broadcast_to(mass, (4, LANES))
+        out[owned] = jnp.broadcast_to(mass, (4, LANES))
 
 
 def last_kernel(own, one, two, three, total, rank_out, delta_out, masses, ordered):
@@ -265,68 +334,110 @@
         [indices, floats, integers, block_scratch, pltpu.SemaphoreType.DMA((3,))],
         cost=pl.CostEstimate(flops=40 << 30, transcendentals=0, bytes_accessed=128 << 20),
     )(leave(tile_source), leave(delta_in), leave(out_degree))
-    for step in range(ITERS):
-        picked = lax.all_to_all(out, BLK, split_axis=0, concat_axis=0, tiled=True)
-        last = step == ITERS - 1
-        if step == 0:
-            *parts, turned, asked = call(
-                functools.partial(start_tile_kernel, n_column),
-                (held,) * 4 + (resident, s32(1, LANES)),
-                [HBM] * 3 + [VMEM, VMEM],
-                (VMEM,) * 6,
-                [indices] * 4
-                + tile_scratch
-                + [pltpu.SemaphoreType.DMA((3,))],
-            )(
-                leave(tile_source),
-                leave(tile_row),
-                leave(tile_valid),
-                picked,
-                tile_weight,
+    def over_columns(parts):
+        return [parts[0]] + [
+            lax.ppermute(
+                parts[s], "col", [(i, (i + s) % n_column) for i in range(n_column)]
             )
-            table, scale, total, masses = call(
-                functools.partial(window_kernel, n_column),
-                (s32(tiles), held, held, f32(8, LANES)),
-                [VMEM] + [HBM] * 5,
-                (SMEM,) + (VMEM,) * 3,
-                [floats, floats, integers, indices, indices, pltpu.SemaphoreType.DMA((5,))],
-                cost=pl.CostEstimate(flops=0, transcendentals=0, bytes_accessed=8 << 20),
-            )(
-                parts[0],
-                leave(delta_in),
-                leave(rank_in),
-                leave(out_degree),
-                leave(tile_row),
-                leave(tile_valid),
-            )
-        else:
-            parts = call(
-                functools.partial(tile_kernel, last),
-                (f32(owned + last, 4, LANES),) * 4,
-                [SMEM, VMEM, VMEM],
-                (VMEM,) * 4,
-                tile_scratch,
-            )(table, picked, keep(turned))
-        own, others = parts[0], parts[1:]
-        others = [
-            lax.ppermute(part, "col", [(i, (i + s + 1) % n_column) for i in range(n_column)])
-            for s, part in enumerate(others)
+            for s in range(1, n_column)
         ]
-        if not last:
-            out, total, masses = call(
-                functools.partial(join_kernel, step + 1, cells),
-                (message, held, f32(8, LANES)),
-                [SMEM] + [VMEM] * 7,
-                (VMEM,) * 3,
-                [block_scratch],
-            )(asked, own, *others, scale, total, masses)
+
+    def to_groups(message):
+        return lax.all_to_all(message, BLK, split_axis=0, concat_axis=0, tiled=True)
+
+    longer = f32(owned + 1, 4, LANES)
+    received = to_groups(out)
+    *parts, turned = call(
+        functools.partial(start_tile_kernel, n_column),
+        (longer,) * 4 + (resident,),
+        [HBM] * 3 + [VMEM, VMEM],
+        (VMEM,) * 5,
+        [indices] * 4 + tile_scratch + [pltpu.SemaphoreType.DMA((3,))],
+    )(leave(tile_source), leave(tile_row), leave(tile_valid), received, tile_weight)
+    turned = keep(turned)
+    table, degrees, total, masses = call(
+        functools.partial(window_kernel, n_column),
+        (s32(tiles), held, held, f32(8, LANES)),
+        [VMEM] + [HBM] * 5,
+        (SMEM,) + (VMEM,) * 3,
+        [floats, floats, integers, indices, indices, pltpu.SemaphoreType.DMA((5,))],
+        cost=pl.CostEstimate(flops=0, transcendentals=0, bytes_accessed=8 << 20),
+    )(
+        parts[0],
+        leave(delta_in),
+        leave(rank_in),
+        leave(out_degree),
+        leave(tile_row),
+        leave(tile_valid),
+    )
+    out, total, masses, wants = call(
+        functools.partial(one_join_kernel, n_column),
+        (message, held, f32(8, LANES), s32(8, LANES)),
+        [VMEM] * 7,
+        (VMEM,) * 4,
+        [
+            pltpu.VMEM((owned, 8, LANES), jnp.float32),
+            pltpu.SMEM((8, LANES), jnp.int32),
+            pltpu.SemaphoreType.DMA(()),
+        ],
+    )(*over_columns(parts), degrees, total, masses)
+    arrived = to_groups(out)
+    relayed = f32(n_group * n_column, 4, LANES)
+    relays = range(2, ITERS - 1)
+    earlier = []
+    for step in relays:
+        first, final = step == relays[0], step == relays[-1]
+        given = (table, wants, arrived) + (() if first else (scale,)) + (turned,)
+        given += tuple(earlier) if final else ()
+        rows = len(relays) * owned if final else owned
+        out, *parts = call(
+            functools.partial(relay_kernel, n_column, first),
+            (relayed,) + (f32(rows, 4, LANES),) * 4 + (held,) * first,
+            [SMEM, SMEM] + [VMEM] * (len(given) - 2),
+            (VMEM,) * (5 + first),
+            tile_scratch,
+        )(*given)
+        if first:
+            scale = parts.pop()
+        earlier += parts
+        arrived = lax.all_to_all(out, BLK_COL, split_axis=0, concat_axis=0, tiled=True)
+    middle = over_columns(parts)
+    parts = call(
+        collect_kernel,
+        (held,) * 4,
+        [SMEM] + [VMEM] * 3,
+        (VMEM,) * 4,
+        tile_scratch,
+    )(table, arrived, scale, turned)
+    total, masses = call(
+        functools.partial(early_join_kernel, tuple(relays)),
+        (held, f32(8, LANES)),
+        [VMEM] * 7,
+        (VMEM,) * 2,
+        [],
+        cost=pl.CostEstimate(flops=0, transcendentals=0, bytes_accessed=8 << 20),
+    )(parts[0], *middle, total, masses)
+    out, total = call(
+        functools.partial(late_join_kernel, cells),
+        (message, held),
+        [SMEM] + [VMEM] * 7,
+        (VMEM,) * 2,
+        [block_scratch],
+    )(wants, *over_columns(parts), degrees, total, masses)
+    parts = call(
+        end_tile_kernel,
+        (longer,) * 4,
+        [SMEM, VMEM, VMEM],
+        (VMEM,) * 4,
+        tile_scratch,
+    )(table, to_groups(out), turned)
     rank_out, delta_out, stacked = call(
         last_kernel,
         (f32(owned, width), f32(owned, width), f32(1, ITERS)),
         [VMEM] * 5,
         (VMEM,) * 3,
         [pltpu.VMEM((4, 4, LANES), jnp.float32)],
-    )(own, *others, total)
+    )(*over_columns(parts), total)
     return rank_out, delta_out, stacked.reshape(ITERS)
 
 

time: 158 us -> 152 us (0.962)
  local copies, waits for them, and re-layouts: 0.01 us -> 5.78 us
  waiting for transfers between devices: 19.7 us -> 14.5 us
  starting transfers between devices: 27 us -> 23.5 us
  Pallas kernels: 29.4 us -> 27.6 us
    ppermute x18 -> x12, waiting for transfers between devices: 19.7 us -> 8.8 us  [over_columns(): lax.ppermute(parts[s], 'col', [(i, (i + s) % n_column) for i in range(n_c...]
    ppermute x18 -> x12, starting transfers between devices: 27 us -> 18.8 us  [over_columns(): lax.ppermute(parts[s], 'col', [(i, (i + s) % n_column) for i in range(n_c...]
    unnamed x2 -> x8, local copies, waits for them, and re-layouts: 0.01 us -> 5.78 us
    all_to_all x0 -> x1, waiting for transfers between devices: none -> 5.74 us  [on_device(): lax.all_to_all(out, BLK_COL, split_axis=0, concat_axis=0, tiled=True)]
    all_to_all x0 -> x1, starting transfers between devices: none -> 4.62 us  [on_device(): lax.all_to_all(out, BLK_COL, split_axis=0, concat_axis=0, tiled=True)]
    pallas_call x11 -> x9, Pallas kernels: 25.4 us -> 23.6 us  [the longest x3 9.74 us: on_device(): call(functools.partial(relay_kernel, n_column, first), (relayed,) + (f32(...]
    all_to_all x6 -> x5, blocking collectives: 81 us -> 79.8 us  [the longest x3 48.3 us: to_groups(): return lax.all_to_all(message, BLK, split_axis=0, concat_axis=0, tiled=True)]
  transfers between devices with their start and end apart: 18 -> 13, of which waited for: 17 -> 8; matrix products, arithmetic and copies ran while one was open for 0% -> 0% of each run, Pallas kernels for 1% -> 3%
where the time goes in v4:
time: 152 us
  blocking collectives  79.8 us (52%)
  Pallas kernels  27.6 us (18%)
  starting transfers between devices  23.5 us (15%)
  waiting for transfers between devices  14.5 us (10%)
  local copies, waits for them, and re-layouts  5.78 us (4%)
    all_to_all x3, blocking collectives, to_groups(): return lax.all_to_all(message, BLK, split_axis=0, concat_axis=0, tiled=True)  48.3 us
    all_to_all x2, blocking collectives, on_device(): lax.all_to_all(out, BLK_COL, split_axis=0, concat_axis=0, tiled=True)  31.5 us
    ppermute x12, starting transfers between devices, over_columns(): lax.ppermute(parts[s], 'col', [(i, (i + s) % n_column) for i in range(n_c...  18.8 us
    pallas_call x3, Pallas kernels, on_device(): call(functools.partial(relay_kernel, n_column, first), (relayed,) + (f32(...  9.74 us
    ppermute x12, waiting for transfers between devices, over_columns(): lax.ppermute(parts[s], 'col', [(i, (i + s) % n_column) for i in range(n_c...  8.8 us
    pallas_call x1, Pallas kernels, on_device(): call(functools.partial(start_tile_kernel, n_column), (longer,) * 4 + (res...  6.59 us
    unnamed x8, local copies, waits for them, and re-layouts  5.78 us
    all_to_all x1, waiting for transfers between devices, on_device(): lax.all_to_all(out, BLK_COL, split_axis=0, concat_axis=0, tiled=True)  5.74 us
  transfers between devices with their start and end apart: 13, of which 8 were waited for; matrix products, arithmetic and copies ran while one was open for 0% of the time, Pallas kernels for 3%

profile of v4, /device:TPU:0, one launch (start us, length us, event | category | flops | bytes accessed | tf_op | source)
XLA Modules:
  0.0 151.9 jit_solution(10509893813660289904)
XLA Ops:
  0.6 0.0 copy-start.3
  0.6 1.4 shard_map.94
  2.0 26.8 %all_to_all.30.refs_3_ = bf16[32,33,4,128]{3,2,1,0:T(4,128)(2,1)S(1)} all-to-all(bf16[32,33,4,128]{3,2,1,0:T(4,128)(2,1)S(1)} %shard_map.94), channel_id=1, replica_groups=mesh['blk_0'=4,'blk_1'=4,'blk_2'=2,'col'=4] {'blk_0','blk_1','blk_2'}, dimensions={0} | all-to-all | bytes 2162688 | tf_op jit(solution)/shard_map/all_to_all | solution.py:346
  28.9 0.0 copy-done.3
  28.9 6.6 %shard_map.95 = (f32[33,4,128]{2,1,0:T(4,128)S(1)}, f32[33,4,128]{2,1,0:T(4,128)S(1)}, f32[33,4,128]{2,1,0:T(4,128)S(1)}, f32[33,4,128]{2,1,0:T(4,128)S(1)}, bf16[32,512,512]{2,1,0:T(8,128)(2,1)S(1)}) custom-call(s32[32]{0:T(128)} %refs_0_.1, s32[32]{0:T(128)} %refs_4_.3, s32[32]{0:T(128)} %refs_5_.1, bf16[32,33,4,128]{3,2,1,0:T(4,128)(2,1)S(1)} %all_to_all.30.refs_3_, ...), custom_call_target="tpu_custom_call" | custom-call | tf_op jit(solution)/shard_map/pallas_call | solution.py:350
  35.4 0.0 copy-start
  35.5 1.6 %collective-permute-start = (f32[33,4,128]{2,1,0:T(4,128)S(1)}, f32[33,4,128]{2,1,0:T(4,128)S(1)}, u32[]{:S(2)}, u32[]{:S(2)}) collective-permute-start(f32[33,4,128]{2,1,0:T(4,128)S(1)} %get-tuple-element.49), channel_id=1, source_target_pairs={{0,1},{1,2},{2,3},{3,0},{4,5},{5,6},{6,7},{7,4},{8,9},{9,10},{10,1... | collective-permute-start | bytes 202760 | tf_op jit(solution)/shard_map/ppermute | solution.py:339
  37.0 2.7 %collective-permute-start.1 = (f32[33,4,128]{2,1,0:T(4,128)S(1)}, f32[33,4,128]{2,1,0:T(4,128)S(1)}, u32[]{:S(2)}, u32[]{:S(2)}) collective-permute-start(f32[33,4,128]{2,1,0:T(4,128)S(1)} %get-tuple-element.50), channel_id=1, source_target_pairs={{0,2},{1,3},{2,0},{3,1},{4,6},{5,7},{6,4},{7,5},{8,10},{9,11},{10,... | collective-permute-start | bytes 202760 | tf_op jit(solution)/shard_map/ppermute | solution.py:339
  39.7 1.4 collective-permute-start.2
  41.2 1.8 %shard_map.96 = (s32[32]{0:T(128)S(1)}, f32[32,4,128]{2,1,0:T(4,128)S(1)}, f32[32,4,128]{2,1,0:T(4,128)S(1)}, f32[8,128]{1,0:T(8,128)S(1)}) custom-call(f32[33,4,128]{2,1,0:T(4,128)S(1)} %get-tuple-element.47.refs_0_.own, f32[32,512]{1,0:T(8,128)} %refs_1_.3, f32[32,512]{1,0:T(8,128)} %refs_2_.3, s32[32,512]{1,0:T(8,128)} %refs_3_.1, s32[32]{0:T(128)} %refs_4_.3, ...), custom_call_target="tpu_custom_call" | custom-call | bytes 8388608 | tf_op jit(solution)/shard_map/pallas_call | solution.py:358
  43.0 0.0 collective-permute-done.one
  43.0 0.3 collective-permute-done.1.two
  43.3 0.7 collective-permute-done.2.three
  44.0 0.6 shard_map.97
  44.7 10.8 %all_to_all.31.refs_2_ = bf16[32,8,128]{2,1,0:T(8,128)(2,1)S(1)} all-to-all(bf16[32,8,128]{2,1,0:T(8,128)(2,1)S(1)} %get-tuple-element.56), channel_id=1, replica_groups=mesh['blk_0'=4,'blk_1'=4,'blk_2'=2,'col'=4] {'blk_0','blk_1','blk_2'}, dimensions={0} | all-to-all | bytes 131072 | tf_op jit(solution)/shard_map/all_to_all | solution.py:346
  55.5 3.0 %shard_map.98 = (f32[128,4,128]{2,1,0:T(4,128)S(1)}, f32[32,4,128]{2,1,0:T(4,128)S(1)}, f32[32,4,128]{2,1,0:T(4,128)S(1)}, f32[32,4,128]{2,1,0:T(4,128)S(1)}, f3...) custom-call(s32[32]{0:T(128)S(1)} %get-tuple-element.48.refs_0_.table, s32[8,128]{1,0:T(8,128)S(1)} %get-tuple-element.55.refs_1_.wants, ...), custom_call_target="tpu_custom_call" | custom-call | tf_op jit(solution)/shard_map/pallas_call | solution.py:393
  58.5 16.4 %all_to_all.32.refs_2_ = f32[128,4,128]{2,1,0:T(4,128)S(1)} all-to-all(f32[128,4,128]{2,1,0:T(4,128)S(1)} %get-tuple-element.58), channel_id=1, replica_groups=mesh['blk_0'=4,'blk_1'=4,'blk_2'=2,'col'=4] {'blk_0','blk_1','blk_2','col'}, dimensions={0} | all-to-all | bytes 524288 | tf_op jit(solution)/shard_map/all_to_all | solution.py:403
  74.9 3.0 %shard_map.99 = (f32[128,4,128]{2,1,0:T(4,128)S(1)}, f32[32,4,128]{2,1,0:T(4,128)S(1)}, f32[32,4,128]{2,1,0:T(4,128)S(1)}, f32[32,4,128]{2,1,0:T(4,128)S(1)}, f32[32,4,128]{2,1,0:T(4,128)S(1)}) custom-call(s32[32]{0:T(128)S(1)} %get-tuple-element.48.refs_0_.table, s32[8,128]{1,0:T(8,128)S(1)} %get-tuple-element.55.refs_1_.wants, ...), custom_call_target="tpu_custom_call" | custom-call | tf_op jit(solution)/shard_map/pallas_call | solution.py:393
  77.9 15.1 %all_to_all.33.refs_2_ = f32[128,4,128]{2,1,0:T(4,128)S(1)} all-to-all(f32[128,4,128]{2,1,0:T(4,128)S(1)} %get-tuple-element.60), channel_id=1, replica_groups=mesh['blk_0'=4,'blk_1'=4,'blk_2'=2,'col'=4] {'blk_0','blk_1','blk_2','col'}, dimensions={0} | all-to-all | bytes 524288 | tf_op jit(solution)/shard_map/all_to_all | solution.py:403
  93.0 0.0 copy-done
  93.0 3.7 %shard_map.100 = (f32[128,4,128]{2,1,0:T(4,128)}, f32[96,4,128]{2,1,0:T(4,128)S(1)}, f32[96,4,128]{2,1,0:T(4,128)S(1)}, f32[96,4,128]{2,1,0:T(4,128)S(1)}, f32[96,4,128]{2,1,0:T(4,128)S(1)}) custom-call(s32[32]{0:T(128)S(1)} %get-tuple-element.48.refs_0_.table, s32[8,128]{1,0:T(8,128)S(1)} %get-tuple-element.55.refs_1_.wants, ...), custom_call_target="tpu_custom_call" | custom-call | tf_op jit(solution)/shard_map/pallas_call | solution.py:393
  96.7 4.6 %all-to-all-start.4 = ((f32[128,4,128]{2,1,0:T(4,128)}), f32[128,4,128]{2,1,0:T(4,128)S(1)}, u32[]{:S(2)}, u32[]{:S(2)}) async-start(f32[128,4,128]{2,1,0:T(4,128)} %get-tuple-element.69), calls=%async_computation.4 | async-start | bytes 524288 | tf_op jit(solution)/shard_map/all_to_all | solution.py:403
  101.4 1.0 collective-permute-start.6
  102.4 2.7 %collective-permute-start.7 = (f32[96,4,128]{2,1,0:T(4,128)S(1)}, f32[96,4,128]{2,1,0:T(4,128)S(1)}, u32[]{:S(2)}, u32[]{:S(2)}) collective-permute-start(f32[96,4,128]{2,1,0:T(4,128)S(1)} %get-tuple-element.76), channel_id=1, source_target_pairs={{0,2},{1,3},{2,0},{3,1},{4,6},{5,7},{6,4},{7,5},{8,10},{9,11},{10,... | collective-permute-start | bytes 589832 | tf_op jit(solution)/shard_map/ppermute | solution.py:339
  105.1 1.5 collective-permute-start.8
  106.5 5.7 %all-to-all-done.4.arrived = f32[128,4,128]{2,1,0:T(4,128)S(1)} async-done(((f32[128,4,128]{2,1,0:T(4,128)}), f32[128,4,128]{2,1,0:T(4,128)S(1)}, u32[]{:S(2)}, u32[]{:S(2)}) %all-to-all-start.4) | async-done | bytes 262176 | tf_op jit(solution)/shard_map/all_to_all | solution.py:403
  112.3 0.0 copy-start.1
  112.3 5.8 %copy-done.1 = bf16[32,512,512]{2,1,0:T(8,128)(2,1)S(1)} copy-done((bf16[32,512,512]{2,1,0:T(8,128)(2,1)S(1)}, bf16[32,512,512]{2,1,0:T(8,128)(2,1)}, u32[]{:S(2)}) %copy-start.1) | copy-done | bytes 16777240
  118.0 0.0 copy-start.2
  118.0 2.9 %shard_map.101 = (f32[32,4,128]{2,1,0:T(4,128)S(1)}, f32[32,4,128]{2,1,0:T(4,128)S(1)}, f32[32,4,128]{2,1,0:T(4,128)S(1)}, f32[32,4,128]{2,1,0:T(4,128)S(1)}) custom-call(s32[32]{0:T(128)S(1)} %get-tuple-element.48.refs_0_.table, f32[128,4,128]{2,1,0:T(4,128)S(1)} %all-to-all-done.4.arrived, f32[32,4,128]{2,1,0:T(4,128)S(1)} %get-tuple-element.59.refs_3_.scale, ...), custom_call_target="tpu_custom_call" | custom-call | tf_op jit(solution)/shard_map/pallas_call | solution.py:405
  120.9 0.4 collective-permute-start.3
  121.3 2.1 %collective-permute-start.4 = (f32[32,4,128]{2,1,0:T(4,128)S(1)}, f32[32,4,128]{2,1,0:T(4,128)S(1)}, u32[]{:S(2)}, u32[]{:S(2)}) collective-permute-start(f32[32,4,128]{2,1,0:T(4,128)S(1)} %get-tuple-element.72), channel_id=1, source_target_pairs={{0,2},{1,3},{2,0},{3,1},{4,6},{5,7},{6,4},{7,5},{8,10},{9,11},{10,... | collective-permute-start | bytes 196616 | tf_op jit(solution)/shard_map/ppermute | solution.py:339
  123.4 0.0 collective-permute-done.6.one
  123.4 1.3 collective-permute-start.5
  124.7 0.0 collective-permute-done.7.two
  124.7 0.0 collective-permute-done.8.three
  124.7 0.1 shard_map.102
  124.8 2.9 %collective-permute-done.3.one = f32[32,4,128]{2,1,0:T(4,128)S(1)} collective-permute-done((f32[32,4,128]{2,1,0:T(4,128)S(1)}, f32[32,4,128]{2,1,0:T(4,128)S(1)}, u32[]{:S(2)}, u32[]{:S(2)}) %collective-permute-start.3) | collective-permute-done | bytes 65568 | tf_op jit(solution)/shard_map/ppermute | solution.py:339
  127.7 0.0 collective-permute-done.4.two
  127.7 0.6 collective-permute-done.5.three
  128.3 0.8 shard_map.103
  129.1 10.7 %all_to_all.34.picked = bf16[32,8,128]{2,1,0:T(8,128)(2,1)S(1)} all-to-all(bf16[32,8,128]{2,1,0:T(8,128)(2,1)S(1)} %get-tuple-element.82), channel_id=1, replica_groups=mesh['blk_0'=4,'blk_1'=4,'blk_2'=2,'col'=4] {'blk_0','blk_1','blk_2'}, dimensions={0} | all-to-all | bytes 131072 | tf_op jit(solution)/shard_map/all_to_all | solution.py:346
  139.8 0.0 copy-done.2
  139.8 2.9 %shard_map.104 = (f32[33,4,128]{2,1,0:T(4,128)S(1)}, f32[33,4,128]{2,1,0:T(4,128)S(1)}, f32[33,4,128]{2,1,0:T(4,128)S(1)}, f32[33,4,128]{2,1,0:T(4,128)S(1)}) custom-call(s32[32]{0:T(128)S(1)} %get-tuple-element.48.refs_0_.table, bf16[32,8,128]{2,1,0:T(8,128)(2,1)S(1)} %all_to_all.34.picked, bf16[32,512,512]{2,1,0:T(8,128)(2,1)S(1)} %copy-done.2), custom_call_target="tpu_custom_call" | custom-call | tf_op jit(solution)/shard_map/pallas_call | solution.py:427
  142.7 1.3 collective-permute-start.9
  144.0 2.9 %collective-permute-start.10 = (f32[33,4,128]{2,1,0:T(4,128)S(1)}, f32[33,4,128]{2,1,0:T(4,128)S(1)}, u32[]{:S(2)}, u32[]{:S(2)}) collective-permute-start(f32[33,4,128]{2,1,0:T(4,128)S(1)} %get-tuple-element.85), channel_id=1, source_target_pairs={{0,2},{1,3},{2,0},{3,1},{4,6},{5,7},{6,4},{7,5},{8,10},{9,11},{10,... | collective-permute-start | bytes 202760 | tf_op jit(solution)/shard_map/ppermute | solution.py:339
  146.8 0.0 collective-permute-start.11
  146.8 1.4 collective-permute-done.9.one
  148.2 2.2 %collective-permute-done.10.two = f32[33,4,128]{2,1,0:T(4,128)S(1)} collective-permute-done((f32[33,4,128]{2,1,0:T(4,128)S(1)}, f32[33,4,128]{2,1,0:T(4,128)S(1)}, u32[]{:S(2)}, u32[]{:S(2)}) %collective-permute-start.10) | collective-permute-done | bytes 67616 | tf_op jit(solution)/shard_map/ppermute | solution.py:339
  150.4 0.7 collective-permute-done.11.three
  151.1 0.8 shard_map.105
Async XLA Ops:
  0.6 28.2 %copy-start.3 = (bf16[32,512,512]{2,1,0:T(8,128)(2,1)S(1)}, bf16[32,512,512]{2,1,0:T(8,128)(2,1)}, u32[]{:S(2)}) copy-start(bf16[32,512,512]{2,1,0:T(8,128)(2,1)} %refs_4_.2) | copy-start | bytes 50331652
  35.4 57.6 %copy-start = (bf16[32,512,512]{2,1,0:T(8,128)(2,1)}, bf16[32,512,512]{2,1,0:T(8,128)(2,1)S(1)}, u32[]{:S(2)}) copy-start(bf16[32,512,512]{2,1,0:T(8,128)(2,1)S(1)} %get-tuple-element.57.refs_3_.refs_4_.turned) | copy-start | bytes 50331652
  35.5 7.5 %collective-permute-start = (f32[33,4,128]{2,1,0:T(4,128)S(1)}, f32[33,4,128]{2,1,0:T(4,128)S(1)}, u32[]{:S(2)}, u32[]{:S(2)}) collective-permute-start(f32[33,4,128]{2,1,0:T(4,128)S(1)} %get-tuple-element.49), channel_id=1, source_target_pairs={{0,1},{1,2},{2,3},{3,0},{4,5},{5,6},{6,7},{7,4},{8,9},{9,10},{10,1... | collective-permute-start | bytes 202760 | tf_op jit(solution)/shard_map/ppermute | solution.py:339
  37.0 6.3 %collective-permute-start.1 = (f32[33,4,128]{2,1,0:T(4,128)S(1)}, f32[33,4,128]{2,1,0:T(4,128)S(1)}, u32[]{:S(2)}, u32[]{:S(2)}) collective-permute-start(f32[33,4,128]{2,1,0:T(4,128)S(1)} %get-tuple-element.50), channel_id=1, source_target_pairs={{0,2},{1,3},{2,0},{3,1},{4,6},{5,7},{6,4},{7,5},{8,10},{9,11},{10,... | collective-permute-start | bytes 202760 | tf_op jit(solution)/shard_map/ppermute | solution.py:339
  39.7 4.3 %collective-permute-start.2 = (f32[33,4,128]{2,1,0:T(4,128)S(1)}, f32[33,4,128]{2,1,0:T(4,128)S(1)}, u32[]{:S(2)}, u32[]{:S(2)}) collective-permute-start(f32[33,4,128]{2,1,0:T(4,128)S(1)} %get-tuple-element.51), channel_id=1, source_target_pairs={{0,3},{1,0},{2,1},{3,2},{4,7},{5,4},{6,5},{7,6},{8,11},{9,8},{10,9... | collective-permute-start | bytes 202760 | tf_op jit(solution)/shard_map/ppermute | solution.py:339
  96.7 15.5 %all-to-all-start.4 = ((f32[128,4,128]{2,1,0:T(4,128)}), f32[128,4,128]{2,1,0:T(4,128)S(1)}, u32[]{:S(2)}, u32[]{:S(2)}) async-start(f32[128,4,128]{2,1,0:T(4,128)} %get-tuple-element.69), calls=%async_computation.4 | async-start | bytes 524288 | tf_op jit(solution)/shard_map/all_to_all | solution.py:403
  101.4 22.1 %collective-permute-start.6 = (f32[96,4,128]{2,1,0:T(4,128)S(1)}, f32[96,4,128]{2,1,0:T(4,128)S(1)}, u32[]{:S(2)}, u32[]{:S(2)}) collective-permute-start(f32[96,4,128]{2,1,0:T(4,128)S(1)} %get-tuple-element.75), channel_id=1, source_target_pairs={{0,1},{1,2},{2,3},{3,0},{4,5},{5,6},{6,7},{7,4},{8,9},{9,10},{10,1... | collective-permute-start | bytes 589832 | tf_op jit(solution)/shard_map/ppermute | solution.py:339
  102.4 22.3 %collective-permute-start.7 = (f32[96,4,128]{2,1,0:T(4,128)S(1)}, f32[96,4,128]{2,1,0:T(4,128)S(1)}, u32[]{:S(2)}, u32[]{:S(2)}) collective-permute-start(f32[96,4,128]{2,1,0:T(4,128)S(1)} %get-tuple-element.76), channel_id=1, source_target_pairs={{0,2},{1,3},{2,0},{3,1},{4,6},{5,7},{6,4},{7,5},{8,10},{9,11},{10,... | collective-permute-start | bytes 589832 | tf_op jit(solution)/shard_map/ppermute | solution.py:339
  105.1 19.6 %collective-permute-start.8 = (f32[96,4,128]{2,1,0:T(4,128)S(1)}, f32[96,4,128]{2,1,0:T(4,128)S(1)}, u32[]{:S(2)}, u32[]{:S(2)}) collective-permute-start(f32[96,4,128]{2,1,0:T(4,128)S(1)} %get-tuple-element.77), channel_id=1, source_target_pairs={{0,3},{1,0},{2,1},{3,2},{4,7},{5,4},{6,5},{7,6},{8,11},{9,8},{10,9... | collective-permute-start | bytes 589832 | tf_op jit(solution)/shard_map/ppermute | solution.py:339
  112.3 5.8 %copy-start.1 = (bf16[32,512,512]{2,1,0:T(8,128)(2,1)S(1)}, bf16[32,512,512]{2,1,0:T(8,128)(2,1)}, u32[]{:S(2)}) copy-start(bf16[32,512,512]{2,1,0:T(8,128)(2,1)} %copy-done) | copy-start | bytes 50331652
  118.0 21.8 %copy-start.2 = (bf16[32,512,512]{2,1,0:T(8,128)(2,1)S(1)}, bf16[32,512,512]{2,1,0:T(8,128)(2,1)}, u32[]{:S(2)}) copy-start(bf16[32,512,512]{2,1,0:T(8,128)(2,1)} %copy-done) | copy-start | bytes 50331652
  120.9 6.8 %collective-permute-start.3 = (f32[32,4,128]{2,1,0:T(4,128)S(1)}, f32[32,4,128]{2,1,0:T(4,128)S(1)}, u32[]{:S(2)}, u32[]{:S(2)}) collective-permute-start(f32[32,4,128]{2,1,0:T(4,128)S(1)} %get-tuple-element.71), channel_id=1, source_target_pairs={{0,1},{1,2},{2,3},{3,0},{4,5},{5,6},{6,7},{7,4},{8,9},{9,10},{10,1... | collective-permute-start | bytes 196616 | tf_op jit(solution)/shard_map/ppermute | solution.py:339
  121.3 6.4 %collective-permute-start.4 = (f32[32,4,128]{2,1,0:T(4,128)S(1)}, f32[32,4,128]{2,1,0:T(4,128)S(1)}, u32[]{:S(2)}, u32[]{:S(2)}) collective-permute-start(f32[32,4,128]{2,1,0:T(4,128)S(1)} %get-tuple-element.72), channel_id=1, source_target_pairs={{0,2},{1,3},{2,0},{3,1},{4,6},{5,7},{6,4},{7,5},{8,10},{9,11},{10,... | collective-permute-start | bytes 196616 | tf_op jit(solution)/shard_map/ppermute | solution.py:339
  123.4 4.9 %collective-permute-start.5 = (f32[32,4,128]{2,1,0:T(4,128)S(1)}, f32[32,4,128]{2,1,0:T(4,128)S(1)}, u32[]{:S(2)}, u32[]{:S(2)}) collective-permute-start(f32[32,4,128]{2,1,0:T(4,128)S(1)} %get-tuple-element.73), channel_id=1, source_target_pairs={{0,3},{1,0},{2,1},{3,2},{4,7},{5,4},{6,5},{7,6},{8,11},{9,8},{10,9... | collective-permute-start | bytes 196616 | tf_op jit(solution)/shard_map/ppermute | solution.py:339
  142.7 5.6 %collective-permute-start.9 = (f32[33,4,128]{2,1,0:T(4,128)S(1)}, f32[33,4,128]{2,1,0:T(4,128)S(1)}, u32[]{:S(2)}, u32[]{:S(2)}) collective-permute-start(f32[33,4,128]{2,1,0:T(4,128)S(1)} %get-tuple-element.84), channel_id=1, source_target_pairs={{0,1},{1,2},{2,3},{3,0},{4,5},{5,6},{6,7},{7,4},{8,9},{9,10},{10,1... | collective-permute-start | bytes 202760 | tf_op jit(solution)/shard_map/ppermute | solution.py:339
  144.0 6.5 %collective-permute-start.10 = (f32[33,4,128]{2,1,0:T(4,128)S(1)}, f32[33,4,128]{2,1,0:T(4,128)S(1)}, u32[]{:S(2)}, u32[]{:S(2)}) collective-permute-start(f32[33,4,128]{2,1,0:T(4,128)S(1)} %get-tuple-element.85), channel_id=1, source_target_pairs={{0,2},{1,3},{2,0},{3,1},{4,6},{5,7},{6,4},{7,5},{8,10},{9,11},{10,... | collective-permute-start | bytes 202760 | tf_op jit(solution)/shard_map/ppermute | solution.py:339
  146.8 4.3 %collective-permute-start.11 = (f32[33,4,128]{2,1,0:T(4,128)S(1)}, f32[33,4,128]{2,1,0:T(4,128)S(1)}, u32[]{:S(2)}, u32[]{:S(2)}) collective-permute-start(f32[33,4,128]{2,1,0:T(4,128)S(1)} %get-tuple-element.86), channel_id=1, source_target_pairs={{0,3},{1,0},{2,1},{3,2},{4,7},{5,4},{6,5},{7,6},{8,11},{9,8},{10,9... | collective-permute-start | bytes 202760 | tf_op jit(solution)/shard_map/ppermute | solution.py:339

commit v5 on v4

--- a/solution.py
+++ b/solution.py
@@ -12,8 +12,9 @@
 BLK = ("blk_0", "blk_1", "blk_2")
 BLK_COL = ("blk_0", "blk_1", "blk_2", "col")
 LANES = 128
+CORES = 2
 GROUP = 32
-FIRST_GROUP = 4
+FIRST_GROUP = 16
 
 damping = 0.85
 
@@ -62,11 +63,13 @@
     for r in range(4):
         part = slice(LANES * r, LANES * (r + 1))
         contrib[:, r, :] = delta[:, part] * (damping / degree[:, part].astype(jnp.float32))
+    half = owned // CORES
     blocks = contrib[...].astype(jnp.bfloat16)
     for b in range(message.shape[0]):
-        message[b, 0:owned] = blocks
+        core = b % CORES
+        message[b, 0:half] = blocks[core * half : (core + 1) * half]
         request = lax.rem(source[b], owned).astype(jnp.float32)
-        message[b, owned] = jnp.full((4, LANES), request, jnp.float32).astype(jnp.bfloat16)
+        message[b, half] = jnp.full((4, LANES), request, jnp.float32).astype(jnp.bfloat16)
 
 
 def window_kernel(cols, *refs):
@@ -163,9 +166,9 @@
 
 
 def start_tile_kernel(cols, *refs):
-    source_hbm, row_hbm, valid_hbm, received, weight = refs[:5]
-    own, one, two, three, turned = refs[5:10]
-    source, row, valid, table, vectors, sums, small_sems = refs[10:]
+    source_hbm, row_hbm, valid_hbm, received, swapped, weight = refs[:6]
+    own, one, two, three, turned = refs[6:11]
+    source, row, valid, table, vectors, sums, small_sems = refs[11:]
     tiles = weight.shape[0]
     owned = tiles
 
@@ -173,7 +176,8 @@
     sums[...] = jnp.zeros_like(sums)
     asking = lax.broadcasted_iota(jnp.int32, (tiles, LANES), 0)
     lanes = lax.broadcasted_iota(jnp.int32, (tiles, LANES), 1)
-    requests = received[:, owned, :, :].astype(jnp.float32)[:, 0, :]
+    half = owned // CORES
+    requests = received[:, half, :, :].astype(jnp.float32)[:, 0, :]
     asked = jnp.sum(jnp.where(asking == lanes, requests, 0.0), axis=0, keepdims=True)
     for out in (own, one, two, three):
         out[owned] = jnp.broadcast_to(asked, (4, LANES))
@@ -181,7 +185,13 @@
         copy.wait()
     targets(cols, lax.axis_index("col"), row, valid, table)
     for j in range(tiles):
-        vectors[j, 0:4] = received[j, lax.rem(source[j], owned)].astype(jnp.float32)
+        block = lax.rem(source[j], owned)
+        at = lax.rem(block, half)
+        vectors[j, 0:4] = jnp.where(
+            block // half == lax.axis_index(BLK[-1]),
+            received[j, at].astype(jnp.float32),
+            swapped[j, at].astype(jnp.float32),
+        )
     rows = lax.broadcasted_iota(jnp.int32, (8, LANES), 0)
 
     def group(g, carry):
@@ -328,7 +338,7 @@
     ]
     out = call(
         first_kernel,
-        jax.ShapeDtypeStruct((n_group, owned + 1, 4, LANES), jnp.bfloat16),
+        jax.ShapeDtypeStruct((n_group, owned // CORES + 1, 4, LANES), jnp.bfloat16),
         [HBM] * 3,
         VMEM,
         [indices, floats, integers, block_scratch, pltpu.SemaphoreType.DMA((3,))],
@@ -347,13 +357,14 @@
 
     longer = f32(owned + 1, 4, LANES)
     received = to_groups(out)
+    swapped = lax.ppermute(received, BLK[-1], [(i, CORES - 1 - i) for i in range(CORES)])
     *parts, turned = call(
         functools.partial(start_tile_kernel, n_column),
         (longer,) * 4 + (resident,),
-        [HBM] * 3 + [VMEM, VMEM],
+        [HBM] * 3 + [VMEM] * 3,
         (VMEM,) * 5,
         [indices] * 4 + tile_scratch + [pltpu.SemaphoreType.DMA((3,))],
-    )(leave(tile_source), leave(tile_row), leave(tile_valid), received, tile_weight)
+    )(leave(tile_source), leave(tile_row), leave(tile_valid), received, swapped, tile_weight)
     turned = keep(turned)
     table, degrees, total, masses = call(
         functools.partial(window_kernel, n_column),

time: 152 us -> 148 us (0.974)
  blocking collectives: 79.8 us -> 73.7 us
  waiting for transfers between devices: 14.5 us -> 16.6 us
    all_to_all x3, blocking collectives: 48.3 us -> 42.2 us  [to_groups(): return lax.all_to_all(message, BLK, split_axis=0, concat_axis=0, tiled=True)]
    ppermute x0 -> x1, waiting for transfers between devices: none -> 1.93 us  [on_device(): lax.ppermute(received, BLK[-1], [(i, CORES - 1 - i) for i in range(CORES)])]
  transfers between devices with their start and end apart: 13 -> 14, of which waited for: 8 -> 9; matrix products, arithmetic and copies ran while one was open for 0% -> 0% of each run, Pallas kernels for 3% -> 3%
where the time goes in v5:
time: 148 us; the launch traced here: 147 us
  blocking collectives  73.7 us (50%)
  Pallas kernels  26.9 us (18%)
  starting transfers between devices  23.5 us (16%)
  waiting for transfers between devices  16.6 us (11%)
  local copies, waits for them, and re-layouts  5.78 us (4%)
    all_to_all x3, blocking collectives, to_groups(): return lax.all_to_all(message, BLK, split_axis=0, concat_axis=0, tiled=True)  42.2 us
    all_to_all x2, blocking collectives, on_device(): lax.all_to_all(out, BLK_COL, split_axis=0, concat_axis=0, tiled=True)  31.5 us
    ppermute x12, starting transfers between devices, over_columns(): lax.ppermute(parts[s], 'col', [(i, (i + s) % n_column) for i in range(n_c...  18.7 us
    pallas_call x3, Pallas kernels, on_device(): call(functools.partial(relay_kernel, n_column, first), (relayed,) + (f32(...  9.74 us
    ppermute x12, waiting for transfers between devices, over_columns(): lax.ppermute(parts[s], 'col', [(i, (i + s) % n_column) for i in range(n_c...  8.8 us
    pallas_call x1, Pallas kernels, on_device(): call(functools.partial(start_tile_kernel, n_column), (longer,) * 4 + (res...  6.06 us
    all_to_all x1, waiting for transfers between devices, on_device(): lax.all_to_all(out, BLK_COL, split_axis=0, concat_axis=0, tiled=True)  5.85 us
    unnamed x8, local copies, waits for them, and re-layouts  5.78 us
  transfers between devices with their start and end apart: 14, of which 9 were waited for; matrix products, arithmetic and copies ran while one was open for 0% of the time, Pallas kernels for 3%

profile of v5, /device:TPU:0, one launch (start us, length us, event | category | flops | bytes accessed | tf_op | source)
XLA Modules:
  0.0 147.3 jit_solution(17565121594833712708)
XLA Ops:
  0.6 0.0 copy-start.3
  0.6 1.3 shard_map.94
  1.9 20.6 %all_to_all.30.refs_3_ = bf16[32,17,4,128]{3,2,1,0:T(4,128)(2,1)S(1)} all-to-all(bf16[32,17,4,128]{3,2,1,0:T(4,128)(2,1)S(1)} %shard_map.94), channel_id=1, replica_groups=mesh['blk_0'=4,'blk_1'=4,'blk_2'=2,'col'=4] {'blk_0','blk_1','blk_2'}, dimensions={0} | all-to-all | bytes 1114112 | tf_op jit(solution)/shard_map/all_to_all | solution.py:356
  22.5 0.0 collective-permute-start
  22.6 1.9 %collective-permute-done.refs_4_ = bf16[32,17,4,128]{3,2,1,0:T(4,128)(2,1)S(1)} collective-permute-done((bf16[32,17,4,128]{3,2,1,0:T(4,128)(2,1)S(1)}, bf16[32,17,4,128]{3,2,1,0:T(4,128)(2,1)S(1)}, u32[]{:S(2)}, u32[]{:S(2)}) %collective-permute-start) | collective-permute-done | bytes 557088 | tf_op jit(solution)/shard_map/ppermute | solution.py:360
  24.5 0.0 copy-done.3
  24.5 6.1 %shard_map.95 = (f32[33,4,128]{2,1,0:T(4,128)S(1)}, f32[33,4,128]{2,1,0:T(4,128)S(1)}, f32[33,4,128]{2,1,0:T(4,128)S(1)}, f32[33,4,128]{2,1,0:T(4,128)S(1)}, bf16[32,512,512]{2,1,0:T(8,128)(2,1)S(1)}) custom-call(s32[32]{0:T(128)} %refs_0_.1, s32[32]{0:T(128)} %refs_4_.1, s32[32]{0:T(128)} %refs_5_.3, bf16[32,17,4,128]{3,2,1,0:T(4,128)(2,1)S(1)} %all_to_all.30.refs_3_, ...), custom_call_target="tpu_custom_call" | custom-call | tf_op jit(solution)/shard_map/pallas_call | solution.py:361
  30.6 0.0 copy-start
  30.6 1.6 %collective-permute-start.1 = (f32[33,4,128]{2,1,0:T(4,128)S(1)}, f32[33,4,128]{2,1,0:T(4,128)S(1)}, u32[]{:S(2)}, u32[]{:S(2)}) collective-permute-start(f32[33,4,128]{2,1,0:T(4,128)S(1)} %get-tuple-element.49), channel_id=1, source_target_pairs={{0,1},{1,2},{2,3},{3,0},{4,5},{5,6},{6,7},{7,4},{8,9},{9,10},{10,1... | collective-permute-start | bytes 202760 | tf_op jit(solution)/shard_map/ppermute | solution.py:349
  32.1 2.7 %collective-permute-start.2 = (f32[33,4,128]{2,1,0:T(4,128)S(1)}, f32[33,4,128]{2,1,0:T(4,128)S(1)}, u32[]{:S(2)}, u32[]{:S(2)}) collective-permute-start(f32[33,4,128]{2,1,0:T(4,128)S(1)} %get-tuple-element.50), channel_id=1, source_target_pairs={{0,2},{1,3},{2,0},{3,1},{4,6},{5,7},{6,4},{7,5},{8,10},{9,11},{10,... | collective-permute-start | bytes 202760 | tf_op jit(solution)/shard_map/ppermute | solution.py:349
  34.9 1.4 collective-permute-start.3
  36.3 1.8 %shard_map.96 = (s32[32]{0:T(128)S(1)}, f32[32,4,128]{2,1,0:T(4,128)S(1)}, f32[32,4,128]{2,1,0:T(4,128)S(1)}, f32[8,128]{1,0:T(8,128)S(1)}) custom-call(f32[33,4,128]{2,1,0:T(4,128)S(1)} %get-tuple-element.47.refs_0_.own, f32[32,512]{1,0:T(8,128)} %refs_1_.3, f32[32,512]{1,0:T(8,128)} %refs_2_.3, s32[32,512]{1,0:T(8,128)} %refs_3_.1, s32[32]{0:T(128)} %refs_4_.1, ...), custom_call_target="tpu_custom_call" | custom-call | bytes 8388608 | tf_op jit(solution)/shard_map/pallas_call | solution.py:369
  38.1 0.0 collective-permute-done.1.one
  38.1 0.3 collective-permute-done.2.two
  38.5 0.7 collective-permute-done.3.three
  39.1 0.6 shard_map.97
  39.8 10.9 %all_to_all.31.refs_2_ = bf16[32,8,128]{2,1,0:T(8,128)(2,1)S(1)} all-to-all(bf16[32,8,128]{2,1,0:T(8,128)(2,1)S(1)} %get-tuple-element.56), channel_id=1, replica_groups=mesh['blk_0'=4,'blk_1'=4,'blk_2'=2,'col'=4] {'blk_0','blk_1','blk_2'}, dimensions={0} | all-to-all | bytes 131072 | tf_op jit(solution)/shard_map/all_to_all | solution.py:356
  50.7 3.0 %shard_map.98 = (f32[128,4,128]{2,1,0:T(4,128)S(1)}, f32[32,4,128]{2,1,0:T(4,128)S(1)}, f32[32,4,128]{2,1,0:T(4,128)S(1)}, f32[32,4,128]{2,1,0:T(4,128)S(1)}, f3...) custom-call(s32[32]{0:T(128)S(1)} %get-tuple-element.48.refs_0_.table, s32[8,128]{1,0:T(8,128)S(1)} %get-tuple-element.55.refs_1_.wants, ...), custom_call_target="tpu_custom_call" | custom-call | tf_op jit(solution)/shard_map/pallas_call | solution.py:404
  53.7 16.4 %all_to_all.32.refs_2_ = f32[128,4,128]{2,1,0:T(4,128)S(1)} all-to-all(f32[128,4,128]{2,1,0:T(4,128)S(1)} %get-tuple-element.58), channel_id=1, replica_groups=mesh['blk_0'=4,'blk_1'=4,'blk_2'=2,'col'=4] {'blk_0','blk_1','blk_2','col'}, dimensions={0} | all-to-all | bytes 524288 | tf_op jit(solution)/shard_map/all_to_all | solution.py:414
  70.1 3.0 %shard_map.99 = (f32[128,4,128]{2,1,0:T(4,128)S(1)}, f32[32,4,128]{2,1,0:T(4,128)S(1)}, f32[32,4,128]{2,1,0:T(4,128)S(1)}, f32[32,4,128]{2,1,0:T(4,128)S(1)}, f32[32,4,128]{2,1,0:T(4,128)S(1)}) custom-call(s32[32]{0:T(128)S(1)} %get-tuple-element.48.refs_0_.table, s32[8,128]{1,0:T(8,128)S(1)} %get-tuple-element.55.refs_1_.wants, ...), custom_call_target="tpu_custom_call" | custom-call | tf_op jit(solution)/shard_map/pallas_call | solution.py:404
  73.1 15.1 %all_to_all.33.refs_2_ = f32[128,4,128]{2,1,0:T(4,128)S(1)} all-to-all(f32[128,4,128]{2,1,0:T(4,128)S(1)} %get-tuple-element.60), channel_id=1, replica_groups=mesh['blk_0'=4,'blk_1'=4,'blk_2'=2,'col'=4] {'blk_0','blk_1','blk_2','col'}, dimensions={0} | all-to-all | bytes 524288 | tf_op jit(solution)/shard_map/all_to_all | solution.py:414
  88.3 0.0 copy-done
  88.3 3.7 %shard_map.100 = (f32[128,4,128]{2,1,0:T(4,128)}, f32[96,4,128]{2,1,0:T(4,128)S(1)}, f32[96,4,128]{2,1,0:T(4,128)S(1)}, f32[96,4,128]{2,1,0:T(4,128)S(1)}, f32[96,4,128]{2,1,0:T(4,128)S(1)}) custom-call(s32[32]{0:T(128)S(1)} %get-tuple-element.48.refs_0_.table, s32[8,128]{1,0:T(8,128)S(1)} %get-tuple-element.55.refs_1_.wants, ...), custom_call_target="tpu_custom_call" | custom-call | tf_op jit(solution)/shard_map/pallas_call | solution.py:404
  92.0 4.8 %all-to-all-start.4 = ((f32[128,4,128]{2,1,0:T(4,128)}), f32[128,4,128]{2,1,0:T(4,128)S(1)}, u32[]{:S(2)}, u32[]{:S(2)}) async-start(f32[128,4,128]{2,1,0:T(4,128)} %get-tuple-element.69), calls=%async_computation.4 | async-start | bytes 524288 | tf_op jit(solution)/shard_map/all_to_all | solution.py:414
  96.8 0.9 collective-permute-start.7
  97.7 2.7 %collective-permute-start.8 = (f32[96,4,128]{2,1,0:T(4,128)S(1)}, f32[96,4,128]{2,1,0:T(4,128)S(1)}, u32[]{:S(2)}, u32[]{:S(2)}) collective-permute-start(f32[96,4,128]{2,1,0:T(4,128)S(1)} %get-tuple-element.76), channel_id=1, source_target_pairs={{0,2},{1,3},{2,0},{3,1},{4,6},{5,7},{6,4},{7,5},{8,10},{9,11},{10,... | collective-permute-start | bytes 589832 | tf_op jit(solution)/shard_map/ppermute | solution.py:349
  100.4 1.4 collective-permute-start.9
  101.8 5.8 %all-to-all-done.4.arrived = f32[128,4,128]{2,1,0:T(4,128)S(1)} async-done(((f32[128,4,128]{2,1,0:T(4,128)}), f32[128,4,128]{2,1,0:T(4,128)S(1)}, u32[]{:S(2)}, u32[]{:S(2)}) %all-to-all-start.4) | async-done | bytes 262176 | tf_op jit(solution)/shard_map/all_to_all | solution.py:414
  107.7 0.0 copy-start.1
  107.7 5.8 %copy-done.1 = bf16[32,512,512]{2,1,0:T(8,128)(2,1)S(1)} copy-done((bf16[32,512,512]{2,1,0:T(8,128)(2,1)S(1)}, bf16[32,512,512]{2,1,0:T(8,128)(2,1)}, u32[]{:S(2)}) %copy-start.1) | copy-done | bytes 16777240
  113.4 0.0 copy-start.2
  113.4 2.9 %shard_map.101 = (f32[32,4,128]{2,1,0:T(4,128)S(1)}, f32[32,4,128]{2,1,0:T(4,128)S(1)}, f32[32,4,128]{2,1,0:T(4,128)S(1)}, f32[32,4,128]{2,1,0:T(4,128)S(1)}) custom-call(s32[32]{0:T(128)S(1)} %get-tuple-element.48.refs_0_.table, f32[128,4,128]{2,1,0:T(4,128)S(1)} %all-to-all-done.4.arrived, f32[32,4,128]{2,1,0:T(4,128)S(1)} %get-tuple-element.59.refs_3_.scale, ...), custom_call_target="tpu_custom_call" | custom-call | tf_op jit(solution)/shard_map/pallas_call | solution.py:416
  116.3 0.4 collective-permute-start.4
  116.7 2.1 %collective-permute-start.5 = (f32[32,4,128]{2,1,0:T(4,128)S(1)}, f32[32,4,128]{2,1,0:T(4,128)S(1)}, u32[]{:S(2)}, u32[]{:S(2)}) collective-permute-start(f32[32,4,128]{2,1,0:T(4,128)S(1)} %get-tuple-element.72), channel_id=1, source_target_pairs={{0,2},{1,3},{2,0},{3,1},{4,6},{5,7},{6,4},{7,5},{8,10},{9,11},{10,... | collective-permute-start | bytes 196616 | tf_op jit(solution)/shard_map/ppermute | solution.py:349
  118.8 0.0 collective-permute-done.7.one
  118.8 1.3 collective-permute-start.6
  120.1 0.0 collective-permute-done.8.two
  120.1 0.0 collective-permute-done.9.three
  120.1 0.1 shard_map.102
  120.2 2.9 %collective-permute-done.4.one = f32[32,4,128]{2,1,0:T(4,128)S(1)} collective-permute-done((f32[32,4,128]{2,1,0:T(4,128)S(1)}, f32[32,4,128]{2,1,0:T(4,128)S(1)}, u32[]{:S(2)}, u32[]{:S(2)}) %collective-permute-start.4) | collective-permute-done | bytes 65568 | tf_op jit(solution)/shard_map/ppermute | solution.py:349
  123.1 0.0 collective-permute-done.5.two
  123.1 0.6 collective-permute-done.6.three
  123.7 0.8 shard_map.103
  124.5 10.7 %all_to_all.34.picked = bf16[32,8,128]{2,1,0:T(8,128)(2,1)S(1)} all-to-all(bf16[32,8,128]{2,1,0:T(8,128)(2,1)S(1)} %get-tuple-element.82), channel_id=1, replica_groups=mesh['blk_0'=4,'blk_1'=4,'blk_2'=2,'col'=4] {'blk_0','blk_1','blk_2'}, dimensions={0} | all-to-all | bytes 131072 | tf_op jit(solution)/shard_map/all_to_all | solution.py:356
  135.2 0.0 copy-done.2
  135.2 2.9 %shard_map.104 = (f32[33,4,128]{2,1,0:T(4,128)S(1)}, f32[33,4,128]{2,1,0:T(4,128)S(1)}, f32[33,4,128]{2,1,0:T(4,128)S(1)}, f32[33,4,128]{2,1,0:T(4,128)S(1)}) custom-call(s32[32]{0:T(128)S(1)} %get-tuple-element.48.refs_0_.table, bf16[32,8,128]{2,1,0:T(8,128)(2,1)S(1)} %all_to_all.34.picked, bf16[32,512,512]{2,1,0:T(8,128)(2,1)S(1)} %copy-done.2), custom_call_target="tpu_custom_call" | custom-call | tf_op jit(solution)/shard_map/pallas_call | solution.py:438
  138.1 1.3 collective-permute-start.10
  139.3 2.9 %collective-permute-start.11 = (f32[33,4,128]{2,1,0:T(4,128)S(1)}, f32[33,4,128]{2,1,0:T(4,128)S(1)}, u32[]{:S(2)}, u32[]{:S(2)}) collective-permute-start(f32[33,4,128]{2,1,0:T(4,128)S(1)} %get-tuple-element.85), channel_id=1, source_target_pairs={{0,2},{1,3},{2,0},{3,1},{4,6},{5,7},{6,4},{7,5},{8,10},{9,11},{10,... | collective-permute-start | bytes 202760 | tf_op jit(solution)/shard_map/ppermute | solution.py:349
  142.2 0.0 collective-permute-start.12
  142.2 1.4 collective-permute-done.10.one
  143.6 2.2 %collective-permute-done.11.two = f32[33,4,128]{2,1,0:T(4,128)S(1)} collective-permute-done((f32[33,4,128]{2,1,0:T(4,128)S(1)}, f32[33,4,128]{2,1,0:T(4,128)S(1)}, u32[]{:S(2)}, u32[]{:S(2)}) %collective-permute-start.11) | collective-permute-done | bytes 67616 | tf_op jit(solution)/shard_map/ppermute | solution.py:349
  145.8 0.7 collective-permute-done.12.three
  146.5 0.8 shard_map.105
Async XLA Ops:
  0.6 23.9 %copy-start.3 = (bf16[32,512,512]{2,1,0:T(8,128)(2,1)S(1)}, bf16[32,512,512]{2,1,0:T(8,128)(2,1)}, u32[]{:S(2)}) copy-start(bf16[32,512,512]{2,1,0:T(8,128)(2,1)} %refs_5_.2) | copy-start | bytes 50331652
  22.5 2.0 %collective-permute-start = (bf16[32,17,4,128]{3,2,1,0:T(4,128)(2,1)S(1)}, bf16[32,17,4,128]{3,2,1,0:T(4,128)(2,1)S(1)}, u32[]{:S(2)}, u32[]{:S(2)}) collective-permute-start(bf16[32,17,4,128]{3,2,1,0:T(4,128)(2,1)S(1)} %all_to_all.30.refs_3_), channel_id=1, source_target_pairs={{0,4},{4,0},{1,5},{5,1},{2,6},{6,2},{3,7},{7,3},{8,12},{12,8},{9,1... | collective-permute-start | bytes 1671176 | tf_op jit(solution)/shard_map/ppermute | solution.py:360
  30.6 57.7 %copy-start = (bf16[32,512,512]{2,1,0:T(8,128)(2,1)}, bf16[32,512,512]{2,1,0:T(8,128)(2,1)S(1)}, u32[]{:S(2)}) copy-start(bf16[32,512,512]{2,1,0:T(8,128)(2,1)S(1)} %get-tuple-element.57.refs_3_.refs_4_.turned) | copy-start | bytes 50331652
  30.6 7.5 %collective-permute-start.1 = (f32[33,4,128]{2,1,0:T(4,128)S(1)}, f32[33,4,128]{2,1,0:T(4,128)S(1)}, u32[]{:S(2)}, u32[]{:S(2)}) collective-permute-start(f32[33,4,128]{2,1,0:T(4,128)S(1)} %get-tuple-element.49), channel_id=1, source_target_pairs={{0,1},{1,2},{2,3},{3,0},{4,5},{5,6},{6,7},{7,4},{8,9},{9,10},{10,1... | collective-permute-start | bytes 202760 | tf_op jit(solution)/shard_map/ppermute | solution.py:349
  32.1 6.3 %collective-permute-start.2 = (f32[33,4,128]{2,1,0:T(4,128)S(1)}, f32[33,4,128]{2,1,0:T(4,128)S(1)}, u32[]{:S(2)}, u32[]{:S(2)}) collective-permute-start(f32[33,4,128]{2,1,0:T(4,128)S(1)} %get-tuple-element.50), channel_id=1, source_target_pairs={{0,2},{1,3},{2,0},{3,1},{4,6},{5,7},{6,4},{7,5},{8,10},{9,11},{10,... | collective-permute-start | bytes 202760 | tf_op jit(solution)/shard_map/ppermute | solution.py:349
  34.9 4.3 %collective-permute-start.3 = (f32[33,4,128]{2,1,0:T(4,128)S(1)}, f32[33,4,128]{2,1,0:T(4,128)S(1)}, u32[]{:S(2)}, u32[]{:S(2)}) collective-permute-start(f32[33,4,128]{2,1,0:T(4,128)S(1)} %get-tuple-element.51), channel_id=1, source_target_pairs={{0,3},{1,0},{2,1},{3,2},{4,7},{5,4},{6,5},{7,6},{8,11},{9,8},{10,9... | collective-permute-start | bytes 202760 | tf_op jit(solution)/shard_map/ppermute | solution.py:349
  92.0 15.7 %all-to-all-start.4 = ((f32[128,4,128]{2,1,0:T(4,128)}), f32[128,4,128]{2,1,0:T(4,128)S(1)}, u32[]{:S(2)}, u32[]{:S(2)}) async-start(f32[128,4,128]{2,1,0:T(4,128)} %get-tuple-element.69), calls=%async_computation.4 | async-start | bytes 524288 | tf_op jit(solution)/shard_map/all_to_all | solution.py:414
  96.8 22.1 %collective-permute-start.7 = (f32[96,4,128]{2,1,0:T(4,128)S(1)}, f32[96,4,128]{2,1,0:T(4,128)S(1)}, u32[]{:S(2)}, u32[]{:S(2)}) collective-permute-start(f32[96,4,128]{2,1,0:T(4,128)S(1)} %get-tuple-element.75), channel_id=1, source_target_pairs={{0,1},{1,2},{2,3},{3,0},{4,5},{5,6},{6,7},{7,4},{8,9},{9,10},{10,1... | collective-permute-start | bytes 589832 | tf_op jit(solution)/shard_map/ppermute | solution.py:349
  97.7 22.4 %collective-permute-start.8 = (f32[96,4,128]{2,1,0:T(4,128)S(1)}, f32[96,4,128]{2,1,0:T(4,128)S(1)}, u32[]{:S(2)}, u32[]{:S(2)}) collective-permute-start(f32[96,4,128]{2,1,0:T(4,128)S(1)} %get-tuple-element.76), channel_id=1, source_target_pairs={{0,2},{1,3},{2,0},{3,1},{4,6},{5,7},{6,4},{7,5},{8,10},{9,11},{10,... | collective-permute-start | bytes 589832 | tf_op jit(solution)/shard_map/ppermute | solution.py:349
  100.4 19.7 %collective-permute-start.9 = (f32[96,4,128]{2,1,0:T(4,128)S(1)}, f32[96,4,128]{2,1,0:T(4,128)S(1)}, u32[]{:S(2)}, u32[]{:S(2)}) collective-permute-start(f32[96,4,128]{2,1,0:T(4,128)S(1)} %get-tuple-element.77), channel_id=1, source_target_pairs={{0,3},{1,0},{2,1},{3,2},{4,7},{5,4},{6,5},{7,6},{8,11},{9,8},{10,9... | collective-permute-start | bytes 589832 | tf_op jit(solution)/shard_map/ppermute | solution.py:349
  107.7 5.8 %copy-start.1 = (bf16[32,512,512]{2,1,0:T(8,128)(2,1)S(1)}, bf16[32,512,512]{2,1,0:T(8,128)(2,1)}, u32[]{:S(2)}) copy-start(bf16[32,512,512]{2,1,0:T(8,128)(2,1)} %copy-done) | copy-start | bytes 50331652
  113.4 21.8 %copy-start.2 = (bf16[32,512,512]{2,1,0:T(8,128)(2,1)S(1)}, bf16[32,512,512]{2,1,0:T(8,128)(2,1)}, u32[]{:S(2)}) copy-start(bf16[32,512,512]{2,1,0:T(8,128)(2,1)} %copy-done) | copy-start | bytes 50331652
  116.3 6.8 %collective-permute-start.4 = (f32[32,4,128]{2,1,0:T(4,128)S(1)}, f32[32,4,128]{2,1,0:T(4,128)S(1)}, u32[]{:S(2)}, u32[]{:S(2)}) collective-permute-start(f32[32,4,128]{2,1,0:T(4,128)S(1)} %get-tuple-element.71), channel_id=1, source_target_pairs={{0,1},{1,2},{2,3},{3,0},{4,5},{5,6},{6,7},{7,4},{8,9},{9,10},{10,1... | collective-permute-start | bytes 196616 | tf_op jit(solution)/shard_map/ppermute | solution.py:349
  116.7 6.4 %collective-permute-start.5 = (f32[32,4,128]{2,1,0:T(4,128)S(1)}, f32[32,4,128]{2,1,0:T(4,128)S(1)}, u32[]{:S(2)}, u32[]{:S(2)}) collective-permute-start(f32[32,4,128]{2,1,0:T(4,128)S(1)} %get-tuple-element.72), channel_id=1, source_target_pairs={{0,2},{1,3},{2,0},{3,1},{4,6},{5,7},{6,4},{7,5},{8,10},{9,11},{10,... | collective-permute-start | bytes 196616 | tf_op jit(solution)/shard_map/ppermute | solution.py:349
  118.8 4.9 %collective-permute-start.6 = (f32[32,4,128]{2,1,0:T(4,128)S(1)}, f32[32,4,128]{2,1,0:T(4,128)S(1)}, u32[]{:S(2)}, u32[]{:S(2)}) collective-permute-start(f32[32,4,128]{2,1,0:T(4,128)S(1)} %get-tuple-element.73), channel_id=1, source_target_pairs={{0,3},{1,0},{2,1},{3,2},{4,7},{5,4},{6,5},{7,6},{8,11},{9,8},{10,9... | collective-permute-start | bytes 196616 | tf_op jit(solution)/shard_map/ppermute | solution.py:349
  138.1 5.6 %collective-permute-start.10 = (f32[33,4,128]{2,1,0:T(4,128)S(1)}, f32[33,4,128]{2,1,0:T(4,128)S(1)}, u32[]{:S(2)}, u32[]{:S(2)}) collective-permute-start(f32[33,4,128]{2,1,0:T(4,128)S(1)} %get-tuple-element.84), channel_id=1, source_target_pairs={{0,1},{1,2},{2,3},{3,0},{4,5},{5,6},{6,7},{7,4},{8,9},{9,10},{10,1... | collective-permute-start | bytes 202760 | tf_op jit(solution)/shard_map/ppermute | solution.py:349
  139.3 6.5 %collective-permute-start.11 = (f32[33,4,128]{2,1,0:T(4,128)S(1)}, f32[33,4,128]{2,1,0:T(4,128)S(1)}, u32[]{:S(2)}, u32[]{:S(2)}) collective-permute-start(f32[33,4,128]{2,1,0:T(4,128)S(1)} %get-tuple-element.85), channel_id=1, source_target_pairs={{0,2},{1,3},{2,0},{3,1},{4,6},{5,7},{6,4},{7,5},{8,10},{9,11},{10,... | collective-permute-start | bytes 202760 | tf_op jit(solution)/shard_map/ppermute | solution.py:349
  142.2 4.3 %collective-permute-start.12 = (f32[33,4,128]{2,1,0:T(4,128)S(1)}, f32[33,4,128]{2,1,0:T(4,128)S(1)}, u32[]{:S(2)}, u32[]{:S(2)}) collective-permute-start(f32[33,4,128]{2,1,0:T(4,128)S(1)} %get-tuple-element.86), channel_id=1, source_target_pairs={{0,3},{1,0},{2,1},{3,2},{4,7},{5,4},{6,5},{7,6},{8,11},{9,8},{10,9... | collective-permute-start | bytes 202760 | tf_op jit(solution)/shard_map/ppermute | solution.py:349

commit v6 on v5

--- a/solution.py
+++ b/solution.py
@@ -13,8 +13,9 @@
 BLK_COL = ("blk_0", "blk_1", "blk_2", "col")
 LANES = 128
 CORES = 2
+LAST_GROUP = 8
 GROUP = 32
-FIRST_GROUP = 16
+FIRST_GROUP = 32
 
 damping = 0.85
 
@@ -265,9 +266,26 @@
     give_parts(parts, earlier, sums, owned)
 
 
-def collect_kernel(table, arrived, scale, turned, own, one, two, three, vectors, sums):
+def collect_kernel(table, arrived, scale, turned_hbm, own, one, two, three, turned, vectors, sums, sems):
+    tiles = turned.shape[0]
+
+    def fetch(j):
+        return pltpu.make_async_copy(turned_hbm.at[j], turned.at[j], sems.at[j])
+
+    for j in range(tiles):
+        fetch(j).start(priority=j % 2)
     take_sums(arrived, scale, vectors)
-    multiply(table, vectors, turned, sums)
+    sums[...] = jnp.zeros_like(sums)
+    rows = lax.broadcasted_iota(jnp.int32, (8, LANES), 0)
+    for g in range(0, tiles, LAST_GROUP):
+        found = []
+        for j in range(g, g + LAST_GROUP):
+            fetch(j).wait()
+        for j in range(g, g + LAST_GROUP):
+            found.append((j, product(vectors, rows, j, 0, turned[j], 0)))
+        for j, block in found:
+            q = table[j]
+            sums[q] = sums[q] + block
     give_parts((own, one, two, three), (), sums, vectors.shape[0])
 
 
@@ -365,6 +383,7 @@
         (VMEM,) * 5,
         [indices] * 4 + tile_scratch + [pltpu.SemaphoreType.DMA((3,))],
     )(leave(tile_source), leave(tile_row), leave(tile_valid), received, swapped, tile_weight)
+    unplaced = turned
     turned = keep(turned)
     table, degrees, total, masses = call(
         functools.partial(window_kernel, n_column),
@@ -413,13 +432,13 @@
         earlier += parts
         arrived = lax.all_to_all(out, BLK_COL, split_axis=0, concat_axis=0, tiled=True)
     middle = over_columns(parts)
-    parts = call(
+    *parts, turned = call(
         collect_kernel,
-        (held,) * 4,
-        [SMEM] + [VMEM] * 3,
-        (VMEM,) * 4,
-        tile_scratch,
-    )(table, arrived, scale, turned)
+        (held,) * 4 + (resident,),
+        [SMEM] + [VMEM] * 2 + [HBM],
+        (VMEM,) * 5,
+        tile_scratch + [pltpu.SemaphoreType.DMA((tiles,))],
+    )(table, arrived, scale, leave(unplaced))
     total, masses = call(
         functools.partial(early_join_kernel, tuple(relays)),
         (held, f32(8, LANES)),
@@ -441,7 +460,7 @@
         [SMEM, VMEM, VMEM],
         (VMEM,) * 4,
         tile_scratch,
-    )(table, to_groups(out), turned)
+    )(table, to_groups(out), keep(turned))
     rank_out, delta_out, stacked = call(
         last_kernel,
         (f32(owned, width), f32(owned, width), f32(1, ITERS)),

time: 148 us -> 146 us (0.986)
  local copies, waits for them, and re-layouts: 5.78 us -> 0.01 us
  Pallas kernels: 26.9 us -> 31.2 us
    unnamed x8 -> x4, local copies, waits for them, and re-layouts: 5.78 us -> 0.01 us
    pallas_call x1, Pallas kernels: 2.86 us -> 7.51 us  [on_device(): call(collect_kernel, (held,) * 4 + (resident,), [SMEM] + [VMEM] * 2 + [HB...]
  transfers between devices with their start and end apart: 14 -> 14, of which waited for: 9 -> 9; matrix products, arithmetic and copies ran while one was open for 0% -> 0% of each run, Pallas kernels for 3% -> 6%
where the time goes in v6:
time: 146 us
  blocking collectives  73.7 us (50%)
  Pallas kernels  31.2 us (21%)
  starting transfers between devices  23.5 us (16%)
  waiting for transfers between devices  16.5 us (11%)
    all_to_all x3, blocking collectives, to_groups(): return lax.all_to_all(message, BLK, split_axis=0, concat_axis=0, tiled=True)  42.2 us
    all_to_all x2, blocking collectives, on_device(): lax.all_to_all(out, BLK_COL, split_axis=0, concat_axis=0, tiled=True)  31.5 us
    ppermute x12, starting transfers between devices, over_columns(): lax.ppermute(parts[s], 'col', [(i, (i + s) % n_column) for i in range(n_c...  18.8 us
    pallas_call x3, Pallas kernels, on_device(): call(functools.partial(relay_kernel, n_column, first), (relayed,) + (f32(...  9.74 us
    ppermute x12, waiting for transfers between devices, over_columns(): lax.ppermute(parts[s], 'col', [(i, (i + s) % n_column) for i in range(n_c...  8.81 us
    pallas_call x1, Pallas kernels, on_device(): call(collect_kernel, (held,) * 4 + (resident,), [SMEM] + [VMEM] * 2 + [HB...  7.51 us
    all_to_all x1, waiting for transfers between devices, on_device(): lax.all_to_all(out, BLK_COL, split_axis=0, concat_axis=0, tiled=True)  5.74 us
    pallas_call x1, Pallas kernels, on_device(): call(functools.partial(start_tile_kernel, n_column), (longer,) * 4 + (res...  5.71 us
  transfers between devices with their start and end apart: 14, of which 9 were waited for; matrix products, arithmetic and copies ran while one was open for 0% of the time, Pallas kernels for 6%

profile of v6, /device:TPU:0, one launch (start us, length us, event | category | flops | bytes accessed | tf_op | source)
XLA Modules:
  0.0 145.7 jit_solution(9051350210959778028)
XLA Ops:
  0.6 0.0 copy-start.1
  0.6 1.3 shard_map.94
  1.9 20.6 %all_to_all.30.refs_3_ = bf16[32,17,4,128]{3,2,1,0:T(4,128)(2,1)S(1)} all-to-all(bf16[32,17,4,128]{3,2,1,0:T(4,128)(2,1)S(1)} %shard_map.94), channel_id=1, replica_groups=mesh['blk_0'=4,'blk_1'=4,'blk_2'=2,'col'=4] {'blk_0','blk_1','blk_2'}, dimensions={0} | all-to-all | bytes 1114112 | tf_op jit(solution)/shard_map/all_to_all | solution.py:374
  22.5 0.0 collective-permute-start
  22.6 1.9 %collective-permute-done.refs_4_ = bf16[32,17,4,128]{3,2,1,0:T(4,128)(2,1)S(1)} collective-permute-done((bf16[32,17,4,128]{3,2,1,0:T(4,128)(2,1)S(1)}, bf16[32,17,4,128]{3,2,1,0:T(4,128)(2,1)S(1)}, u32[]{:S(2)}, u32[]{:S(2)}) %collective-permute-start) | collective-permute-done | bytes 557088 | tf_op jit(solution)/shard_map/ppermute | solution.py:378
  24.5 0.0 copy-done.1
  24.5 5.7 %shard_map.95 = (f32[33,4,128]{2,1,0:T(4,128)S(1)}, f32[33,4,128]{2,1,0:T(4,128)S(1)}, f32[33,4,128]{2,1,0:T(4,128)S(1)}, f32[33,4,128]{2,1,0:T(4,128)S(1)}, bf16[32,512,512]{2,1,0:T(8,128)(2,1)S(1)}) custom-call(s32[32]{0:T(128)} %refs_0_.1, s32[32]{0:T(128)} %refs_4_.1, s32[32]{0:T(128)} %refs_5_.3, bf16[32,17,4,128]{3,2,1,0:T(4,128)(2,1)S(1)} %all_to_all.30.refs_3_, ...), custom_call_target="tpu_custom_call" | custom-call | tf_op jit(solution)/shard_map/pallas_call | solution.py:379
  30.2 0.0 copy-start
  30.2 1.6 %collective-permute-start.1 = (f32[33,4,128]{2,1,0:T(4,128)S(1)}, f32[33,4,128]{2,1,0:T(4,128)S(1)}, u32[]{:S(2)}, u32[]{:S(2)}) collective-permute-start(f32[33,4,128]{2,1,0:T(4,128)S(1)} %get-tuple-element.50), channel_id=1, source_target_pairs={{0,1},{1,2},{2,3},{3,0},{4,5},{5,6},{6,7},{7,4},{8,9},{9,10},{10,1... | collective-permute-start | bytes 202760 | tf_op jit(solution)/shard_map/ppermute | solution.py:367
  31.8 2.7 %collective-permute-start.2 = (f32[33,4,128]{2,1,0:T(4,128)S(1)}, f32[33,4,128]{2,1,0:T(4,128)S(1)}, u32[]{:S(2)}, u32[]{:S(2)}) collective-permute-start(f32[33,4,128]{2,1,0:T(4,128)S(1)} %get-tuple-element.51), channel_id=1, source_target_pairs={{0,2},{1,3},{2,0},{3,1},{4,6},{5,7},{6,4},{7,5},{8,10},{9,11},{10,... | collective-permute-start | bytes 202760 | tf_op jit(solution)/shard_map/ppermute | solution.py:367
  34.5 1.4 collective-permute-start.3
  35.9 1.8 %shard_map.96 = (s32[32]{0:T(128)S(1)}, f32[32,4,128]{2,1,0:T(4,128)S(1)}, f32[32,4,128]{2,1,0:T(4,128)S(1)}, f32[8,128]{1,0:T(8,128)S(1)}) custom-call(f32[33,4,128]{2,1,0:T(4,128)S(1)} %get-tuple-element.48.refs_0_.own, f32[32,512]{1,0:T(8,128)} %refs_1_.3, f32[32,512]{1,0:T(8,128)} %refs_2_.3, s32[32,512]{1,0:T(8,128)} %refs_3_.1, s32[32]{0:T(128)} %refs_4_.1, ...), custom_call_target="tpu_custom_call" | custom-call | bytes 8388608 | tf_op jit(solution)/shard_map/pallas_call | solution.py:388
  37.8 0.0 collective-permute-done.1.one
  37.8 0.3 collective-permute-done.2.two
  38.1 0.7 collective-permute-done.3.three
  38.8 0.6 shard_map.97
  39.5 10.9 %all_to_all.31.refs_2_ = bf16[32,8,128]{2,1,0:T(8,128)(2,1)S(1)} all-to-all(bf16[32,8,128]{2,1,0:T(8,128)(2,1)S(1)} %get-tuple-element.57), channel_id=1, replica_groups=mesh['blk_0'=4,'blk_1'=4,'blk_2'=2,'col'=4] {'blk_0','blk_1','blk_2'}, dimensions={0} | all-to-all | bytes 131072 | tf_op jit(solution)/shard_map/all_to_all | solution.py:374
  50.3 3.0 %shard_map.98 = (f32[128,4,128]{2,1,0:T(4,128)S(1)}, f32[32,4,128]{2,1,0:T(4,128)S(1)}, f32[32,4,128]{2,1,0:T(4,128)S(1)}, f32[32,4,128]{2,1,0:T(4,128)S(1)}, f3...) custom-call(s32[32]{0:T(128)S(1)} %get-tuple-element.49.refs_0_.table, s32[8,128]{1,0:T(8,128)S(1)} %get-tuple-element.56.refs_1_.wants, ...), custom_call_target="tpu_custom_call" | custom-call | tf_op jit(solution)/shard_map/pallas_call | solution.py:423
  53.4 16.4 %all_to_all.32.refs_2_ = f32[128,4,128]{2,1,0:T(4,128)S(1)} all-to-all(f32[128,4,128]{2,1,0:T(4,128)S(1)} %get-tuple-element.59), channel_id=1, replica_groups=mesh['blk_0'=4,'blk_1'=4,'blk_2'=2,'col'=4] {'blk_0','blk_1','blk_2','col'}, dimensions={0} | all-to-all | bytes 524288 | tf_op jit(solution)/shard_map/all_to_all | solution.py:433
  69.8 3.0 %shard_map.99 = (f32[128,4,128]{2,1,0:T(4,128)S(1)}, f32[32,4,128]{2,1,0:T(4,128)S(1)}, f32[32,4,128]{2,1,0:T(4,128)S(1)}, f32[32,4,128]{2,1,0:T(4,128)S(1)}, f32[32,4,128]{2,1,0:T(4,128)S(1)}) custom-call(s32[32]{0:T(128)S(1)} %get-tuple-element.49.refs_0_.table, s32[8,128]{1,0:T(8,128)S(1)} %get-tuple-element.56.refs_1_.wants, ...), custom_call_target="tpu_custom_call" | custom-call | tf_op jit(solution)/shard_map/pallas_call | solution.py:423
  72.8 15.1 %all_to_all.33.refs_2_ = f32[128,4,128]{2,1,0:T(4,128)S(1)} all-to-all(f32[128,4,128]{2,1,0:T(4,128)S(1)} %get-tuple-element.61), channel_id=1, replica_groups=mesh['blk_0'=4,'blk_1'=4,'blk_2'=2,'col'=4] {'blk_0','blk_1','blk_2','col'}, dimensions={0} | all-to-all | bytes 524288 | tf_op jit(solution)/shard_map/all_to_all | solution.py:433
  87.9 0.0 copy-done
  87.9 3.7 %shard_map.100 = (f32[128,4,128]{2,1,0:T(4,128)}, f32[96,4,128]{2,1,0:T(4,128)S(1)}, f32[96,4,128]{2,1,0:T(4,128)S(1)}, f32[96,4,128]{2,1,0:T(4,128)S(1)}, f32[96,4,128]{2,1,0:T(4,128)S(1)}) custom-call(s32[32]{0:T(128)S(1)} %get-tuple-element.49.refs_0_.table, s32[8,128]{1,0:T(8,128)S(1)} %get-tuple-element.56.refs_1_.wants, ...), custom_call_target="tpu_custom_call" | custom-call | tf_op jit(solution)/shard_map/pallas_call | solution.py:423
  91.6 4.6 %all-to-all-start.4 = ((f32[128,4,128]{2,1,0:T(4,128)}), f32[128,4,128]{2,1,0:T(4,128)S(1)}, u32[]{:S(2)}, u32[]{:S(2)}) async-start(f32[128,4,128]{2,1,0:T(4,128)} %get-tuple-element.70), calls=%async_computation.4 | async-start | bytes 524288 | tf_op jit(solution)/shard_map/all_to_all | solution.py:433
  96.2 1.0 collective-permute-start.7
  97.3 2.7 %collective-permute-start.8 = (f32[96,4,128]{2,1,0:T(4,128)S(1)}, f32[96,4,128]{2,1,0:T(4,128)S(1)}, u32[]{:S(2)}, u32[]{:S(2)}) collective-permute-start(f32[96,4,128]{2,1,0:T(4,128)S(1)} %get-tuple-element.77), channel_id=1, source_target_pairs={{0,2},{1,3},{2,0},{3,1},{4,6},{5,7},{6,4},{7,5},{8,10},{9,11},{10,... | collective-permute-start | bytes 589832 | tf_op jit(solution)/shard_map/ppermute | solution.py:367
  99.9 1.5 %collective-permute-start.9 = (f32[96,4,128]{2,1,0:T(4,128)S(1)}, f32[96,4,128]{2,1,0:T(4,128)S(1)}, u32[]{:S(2)}, u32[]{:S(2)}) collective-permute-start(f32[96,4,128]{2,1,0:T(4,128)S(1)} %get-tuple-element.78), channel_id=1, source_target_pairs={{0,3},{1,0},{2,1},{3,2},{4,7},{5,4},{6,5},{7,6},{8,11},{9,8},{10,9... | collective-permute-start | bytes 589832 | tf_op jit(solution)/shard_map/ppermute | solution.py:367
  101.4 5.7 %all-to-all-done.4.arrived = f32[128,4,128]{2,1,0:T(4,128)S(1)} async-done(((f32[128,4,128]{2,1,0:T(4,128)}), f32[128,4,128]{2,1,0:T(4,128)S(1)}, u32[]{:S(2)}, u32[]{:S(2)}) %all-to-all-start.4) | async-done | bytes 262176 | tf_op jit(solution)/shard_map/all_to_all | solution.py:433
  107.1 7.5 %shard_map.101 = (f32[32,4,128]{2,1,0:T(4,128)S(1)}, f32[32,4,128]{2,1,0:T(4,128)S(1)}, f32[32,4,128]{2,1,0:T(4,128)S(1)}, f32[32,4,128]{2,1,0:T(4,128)S(1)}, bf16[32,512,512]{2,1,0:T(8,128)(2,1)S(1)}) custom-call(s32[32]{0:T(128)S(1)} %get-tuple-element.49.refs_0_.table, f32[128,4,128]{2,1,0:T(4,128)S(1)} %all-to-all-done.4.arrived, ...), custom_call_target="tpu_custom_call" | custom-call | tf_op jit(solution)/shard_map/pallas_call | solution.py:435
  114.7 0.4 collective-permute-start.4
  115.1 2.1 %collective-permute-start.5 = (f32[32,4,128]{2,1,0:T(4,128)S(1)}, f32[32,4,128]{2,1,0:T(4,128)S(1)}, u32[]{:S(2)}, u32[]{:S(2)}) collective-permute-start(f32[32,4,128]{2,1,0:T(4,128)S(1)} %get-tuple-element.73), channel_id=1, source_target_pairs={{0,2},{1,3},{2,0},{3,1},{4,6},{5,7},{6,4},{7,5},{8,10},{9,11},{10,... | collective-permute-start | bytes 196616 | tf_op jit(solution)/shard_map/ppermute | solution.py:367
  117.2 0.0 collective-permute-done.7.one
  117.2 1.2 collective-permute-start.6
  118.5 0.0 collective-permute-done.8.two
  118.5 0.0 collective-permute-done.9.three
  118.5 0.1 shard_map.102
  118.6 2.9 %collective-permute-done.4.one = f32[32,4,128]{2,1,0:T(4,128)S(1)} collective-permute-done((f32[32,4,128]{2,1,0:T(4,128)S(1)}, f32[32,4,128]{2,1,0:T(4,128)S(1)}, u32[]{:S(2)}, u32[]{:S(2)}) %collective-permute-start.4) | collective-permute-done | bytes 65568 | tf_op jit(solution)/shard_map/ppermute | solution.py:367
  121.5 0.0 collective-permute-done.5.two
  121.5 0.6 collective-permute-done.6.three
  122.1 0.8 shard_map.103
  122.9 10.7 %all_to_all.34.picked = bf16[32,8,128]{2,1,0:T(8,128)(2,1)S(1)} all-to-all(bf16[32,8,128]{2,1,0:T(8,128)(2,1)S(1)} %get-tuple-element.83), channel_id=1, replica_groups=mesh['blk_0'=4,'blk_1'=4,'blk_2'=2,'col'=4] {'blk_0','blk_1','blk_2'}, dimensions={0} | all-to-all | bytes 131072 | tf_op jit(solution)/shard_map/all_to_all | solution.py:374
  133.6 2.9 %shard_map.104 = (f32[33,4,128]{2,1,0:T(4,128)S(1)}, f32[33,4,128]{2,1,0:T(4,128)S(1)}, f32[33,4,128]{2,1,0:T(4,128)S(1)}, f32[33,4,128]{2,1,0:T(4,128)S(1)}) custom-call(s32[32]{0:T(128)S(1)} %get-tuple-element.49.refs_0_.table, bf16[32,8,128]{2,1,0:T(8,128)(2,1)S(1)} %all_to_all.34.picked, bf16[32,512,512]{2,1,0:T(8,128)(2,1)S(1)} %get-tuple-element.84.turned), custom_call_target="tpu_custom_call" | custom-call | tf_op jit(solution)/shard_map/pallas_call | solution.py:457
  136.4 1.3 collective-permute-start.10
  137.7 2.9 %collective-permute-start.11 = (f32[33,4,128]{2,1,0:T(4,128)S(1)}, f32[33,4,128]{2,1,0:T(4,128)S(1)}, u32[]{:S(2)}, u32[]{:S(2)}) collective-permute-start(f32[33,4,128]{2,1,0:T(4,128)S(1)} %get-tuple-element.87), channel_id=1, source_target_pairs={{0,2},{1,3},{2,0},{3,1},{4,6},{5,7},{6,4},{7,5},{8,10},{9,11},{10,... | collective-permute-start | bytes 202760 | tf_op jit(solution)/shard_map/ppermute | solution.py:367
  140.6 0.0 collective-permute-start.12
  140.6 1.4 collective-permute-done.10.one
  142.0 2.2 %collective-permute-done.11.two = f32[33,4,128]{2,1,0:T(4,128)S(1)} collective-permute-done((f32[33,4,128]{2,1,0:T(4,128)S(1)}, f32[33,4,128]{2,1,0:T(4,128)S(1)}, u32[]{:S(2)}, u32[]{:S(2)}) %collective-permute-start.11) | collective-permute-done | bytes 67616 | tf_op jit(solution)/shard_map/ppermute | solution.py:367
  144.2 0.7 collective-permute-done.12.three
  144.9 0.8 shard_map.105
Async XLA Ops:
  0.6 23.9 %copy-start.1 = (bf16[32,512,512]{2,1,0:T(8,128)(2,1)S(1)}, bf16[32,512,512]{2,1,0:T(8,128)(2,1)}, u32[]{:S(2)}) copy-start(bf16[32,512,512]{2,1,0:T(8,128)(2,1)} %refs_5_.2) | copy-start | bytes 50331652
  22.5 2.0 %collective-permute-start = (bf16[32,17,4,128]{3,2,1,0:T(4,128)(2,1)S(1)}, bf16[32,17,4,128]{3,2,1,0:T(4,128)(2,1)S(1)}, u32[]{:S(2)}, u32[]{:S(2)}) collective-permute-start(bf16[32,17,4,128]{3,2,1,0:T(4,128)(2,1)S(1)} %all_to_all.30.refs_3_), channel_id=1, source_target_pairs={{0,4},{4,0},{1,5},{5,1},{2,6},{6,2},{3,7},{7,3},{8,12},{12,8},{9,1... | collective-permute-start | bytes 1671176 | tf_op jit(solution)/shard_map/ppermute | solution.py:378
  30.2 57.7 %copy-start = (bf16[32,512,512]{2,1,0:T(8,128)(2,1)}, bf16[32,512,512]{2,1,0:T(8,128)(2,1)S(1)}, u32[]{:S(2)}) copy-start(bf16[32,512,512]{2,1,0:T(8,128)(2,1)S(1)} %get-tuple-element.58.refs_3_.refs_4_.turned_hbm) | copy-start | bytes 50331652
  30.2 7.5 %collective-permute-start.1 = (f32[33,4,128]{2,1,0:T(4,128)S(1)}, f32[33,4,128]{2,1,0:T(4,128)S(1)}, u32[]{:S(2)}, u32[]{:S(2)}) collective-permute-start(f32[33,4,128]{2,1,0:T(4,128)S(1)} %get-tuple-element.50), channel_id=1, source_target_pairs={{0,1},{1,2},{2,3},{3,0},{4,5},{5,6},{6,7},{7,4},{8,9},{9,10},{10,1... | collective-permute-start | bytes 202760 | tf_op jit(solution)/shard_map/ppermute | solution.py:367
  31.8 6.3 %collective-permute-start.2 = (f32[33,4,128]{2,1,0:T(4,128)S(1)}, f32[33,4,128]{2,1,0:T(4,128)S(1)}, u32[]{:S(2)}, u32[]{:S(2)}) collective-permute-start(f32[33,4,128]{2,1,0:T(4,128)S(1)} %get-tuple-element.51), channel_id=1, source_target_pairs={{0,2},{1,3},{2,0},{3,1},{4,6},{5,7},{6,4},{7,5},{8,10},{9,11},{10,... | collective-permute-start | bytes 202760 | tf_op jit(solution)/shard_map/ppermute | solution.py:367
  34.5 4.3 %collective-permute-start.3 = (f32[33,4,128]{2,1,0:T(4,128)S(1)}, f32[33,4,128]{2,1,0:T(4,128)S(1)}, u32[]{:S(2)}, u32[]{:S(2)}) collective-permute-start(f32[33,4,128]{2,1,0:T(4,128)S(1)} %get-tuple-element.52), channel_id=1, source_target_pairs={{0,3},{1,0},{2,1},{3,2},{4,7},{5,4},{6,5},{7,6},{8,11},{9,8},{10,9... | collective-permute-start | bytes 202760 | tf_op jit(solution)/shard_map/ppermute | solution.py:367
  91.6 15.5 %all-to-all-start.4 = ((f32[128,4,128]{2,1,0:T(4,128)}), f32[128,4,128]{2,1,0:T(4,128)S(1)}, u32[]{:S(2)}, u32[]{:S(2)}) async-start(f32[128,4,128]{2,1,0:T(4,128)} %get-tuple-element.70), calls=%async_computation.4 | async-start | bytes 524288 | tf_op jit(solution)/shard_map/all_to_all | solution.py:433
  96.2 21.0 %collective-permute-start.7 = (f32[96,4,128]{2,1,0:T(4,128)S(1)}, f32[96,4,128]{2,1,0:T(4,128)S(1)}, u32[]{:S(2)}, u32[]{:S(2)}) collective-permute-start(f32[96,4,128]{2,1,0:T(4,128)S(1)} %get-tuple-element.76), channel_id=1, source_target_pairs={{0,1},{1,2},{2,3},{3,0},{4,5},{5,6},{6,7},{7,4},{8,9},{9,10},{10,1... | collective-permute-start | bytes 589832 | tf_op jit(solution)/shard_map/ppermute | solution.py:367
  97.3 21.2 %collective-permute-start.8 = (f32[96,4,128]{2,1,0:T(4,128)S(1)}, f32[96,4,128]{2,1,0:T(4,128)S(1)}, u32[]{:S(2)}, u32[]{:S(2)}) collective-permute-start(f32[96,4,128]{2,1,0:T(4,128)S(1)} %get-tuple-element.77), channel_id=1, source_target_pairs={{0,2},{1,3},{2,0},{3,1},{4,6},{5,7},{6,4},{7,5},{8,10},{9,11},{10,... | collective-permute-start | bytes 589832 | tf_op jit(solution)/shard_map/ppermute | solution.py:367
  99.9 18.5 %collective-permute-start.9 = (f32[96,4,128]{2,1,0:T(4,128)S(1)}, f32[96,4,128]{2,1,0:T(4,128)S(1)}, u32[]{:S(2)}, u32[]{:S(2)}) collective-permute-start(f32[96,4,128]{2,1,0:T(4,128)S(1)} %get-tuple-element.78), channel_id=1, source_target_pairs={{0,3},{1,0},{2,1},{3,2},{4,7},{5,4},{6,5},{7,6},{8,11},{9,8},{10,9... | collective-permute-start | bytes 589832 | tf_op jit(solution)/shard_map/ppermute | solution.py:367
  114.7 6.8 %collective-permute-start.4 = (f32[32,4,128]{2,1,0:T(4,128)S(1)}, f32[32,4,128]{2,1,0:T(4,128)S(1)}, u32[]{:S(2)}, u32[]{:S(2)}) collective-permute-start(f32[32,4,128]{2,1,0:T(4,128)S(1)} %get-tuple-element.72), channel_id=1, source_target_pairs={{0,1},{1,2},{2,3},{3,0},{4,5},{5,6},{6,7},{7,4},{8,9},{9,10},{10,1... | collective-permute-start | bytes 196616 | tf_op jit(solution)/shard_map/ppermute | solution.py:367
  115.1 6.4 %collective-permute-start.5 = (f32[32,4,128]{2,1,0:T(4,128)S(1)}, f32[32,4,128]{2,1,0:T(4,128)S(1)}, u32[]{:S(2)}, u32[]{:S(2)}) collective-permute-start(f32[32,4,128]{2,1,0:T(4,128)S(1)} %get-tuple-element.73), channel_id=1, source_target_pairs={{0,2},{1,3},{2,0},{3,1},{4,6},{5,7},{6,4},{7,5},{8,10},{9,11},{10,... | collective-permute-start | bytes 196616 | tf_op jit(solution)/shard_map/ppermute | solution.py:367
  117.2 4.9 %collective-permute-start.6 = (f32[32,4,128]{2,1,0:T(4,128)S(1)}, f32[32,4,128]{2,1,0:T(4,128)S(1)}, u32[]{:S(2)}, u32[]{:S(2)}) collective-permute-start(f32[32,4,128]{2,1,0:T(4,128)S(1)} %get-tuple-element.74), channel_id=1, source_target_pairs={{0,3},{1,0},{2,1},{3,2},{4,7},{5,4},{6,5},{7,6},{8,11},{9,8},{10,9... | collective-permute-start | bytes 196616 | tf_op jit(solution)/shard_map/ppermute | solution.py:367
  136.4 5.6 %collective-permute-start.10 = (f32[33,4,128]{2,1,0:T(4,128)S(1)}, f32[33,4,128]{2,1,0:T(4,128)S(1)}, u32[]{:S(2)}, u32[]{:S(2)}) collective-permute-start(f32[33,4,128]{2,1,0:T(4,128)S(1)} %get-tuple-element.86), channel_id=1, source_target_pairs={{0,1},{1,2},{2,3},{3,0},{4,5},{5,6},{6,7},{7,4},{8,9},{9,10},{10,1... | collective-permute-start | bytes 202760 | tf_op jit(solution)/shard_map/ppermute | solution.py:367
  137.7 6.5 %collective-permute-start.11 = (f32[33,4,128]{2,1,0:T(4,128)S(1)}, f32[33,4,128]{2,1,0:T(4,128)S(1)}, u32[]{:S(2)}, u32[]{:S(2)}) collective-permute-start(f32[33,4,128]{2,1,0:T(4,128)S(1)} %get-tuple-element.87), channel_id=1, source_target_pairs={{0,2},{1,3},{2,0},{3,1},{4,6},{5,7},{6,4},{7,5},{8,10},{9,11},{10,... | collective-permute-start | bytes 202760 | tf_op jit(solution)/shard_map/ppermute | solution.py:367
  140.6 4.3 %collective-permute-start.12 = (f32[33,4,128]{2,1,0:T(4,128)S(1)}, f32[33,4,128]{2,1,0:T(4,128)S(1)}, u32[]{:S(2)}, u32[]{:S(2)}) collective-permute-start(f32[33,4,128]{2,1,0:T(4,128)S(1)} %get-tuple-element.88), channel_id=1, source_target_pairs={{0,3},{1,0},{2,1},{3,2},{4,7},{5,4},{6,5},{7,6},{8,11},{9,8},{10,9... | collective-permute-start | bytes 202760 | tf_op jit(solution)/shard_map/ppermute | solution.py:367
